TPU v7x, 32 devices: a whole 2x2x4 slice. The times are simulated.
32 devices in a mesh: ens: 2 (over y), node: 16 (over z, x, core).
Axes of the slice: x: 2, y: 2, z: 4, core: 2. Of those that a mesh axis runs over, the one named last changes fastest.
Arguments:
- hidden_embedding: bfloat16 [2, 16384, 1024], P('ens', 'node'), may hold values from -6 to 6
- random_perturbation: bfloat16 [2, 1024], P('ens'), may hold values from -3 to 3
- norm_gain: float32 [1024], replicated, may hold values from 0.5 to 1.5
- w_qkv: bfloat16 [1024, 3072], replicated, may hold values from -40 to 40
- w_proj: bfloat16 [1024, 1024], replicated, may hold values from -0.1875 to 0.1875
- w_fields: bfloat16 [1024, 100], replicated, may hold values from -0.1875 to 0.1875
- observed_reality: float32 [100, 16384], P(None, 'node'), may hold values from -6 to 6
- counts: int32 [16], replicated, may hold values from 512 to 1024, as said below
Outputs:
- predicted_outputs: bfloat16 [2, 100, 16384], P('ens', None, 'node')
- probabilistic_score: float32 [100, 16384], P(None, 'node')
- scaled_derivative: float32 [2, 100, 16384], P('ens', None, 'node')
Inputs may be any that keep to these rules, and one draw needn't show every extreme that they name: `counts`: each shard has at least half of its 1024 slots live, its live nodes come first, one shard is full and one is exactly half full.
All inputs are finite; a program needn't handle non-finite values.
Results may differ from a plain program's by a relative error of at most 0.013.
The roundings to bfloat16 on the way count: a program that leaves them out, or rounds other values in their place, can miss the bound.
Values may be sent and summed in bfloat16 or wider, within the bound.
No kernel may reach another device: no remote copies, remote signals or barrier semaphores. Data moves between devices by JAX's collectives and lax.ppermute only.
A program may use at most 128 MiB of HBM per device.

v0:
```python
import jax
import jax.numpy as jnp
from jax import lax
from jax.sharding import PartitionSpec as P

HEADS = 16
HEAD_GROUP = 4
HALF_WINDOW = 256


smooth_sq = 0.01
alpha_fair = 0.95


def padded(block, sides, width):
    for axis, dim in sides:
        count = lax.axis_size(axis)
        forward = [(i, i + 1) for i in range(count - 1)]
        backward = [(target, source) for source, target in forward]
        low = lax.ppermute(
            lax.slice_in_dim(block, block.shape[dim] - width, None, axis=dim), axis, forward
        )
        high = lax.ppermute(lax.slice_in_dim(block, 0, width, axis=dim), axis, backward)
        block = jnp.concatenate([low, block, high], axis=dim)
    return block


def attend(query, keys, values, allowed, heads, group):
    mem, rows, window_width = query.shape
    keyn = keys.shape[1]
    head_dim = window_width // heads
    groups = heads // group

    def split(arr, count):
        return jnp.moveaxis(arr.reshape(mem, count, groups, group, head_dim), 2, 1).reshape(
            mem * groups, count, group, head_dim
        )

    def one_group(item):
        q_part, k_part, v_part = item
        scores = jnp.einsum(
            "qhd,khd->hqk", q_part, k_part, preferred_element_type=jnp.float32
        ) / jnp.sqrt(jnp.float32(head_dim))
        scores = jnp.where(allowed[None], scores, jnp.float32(-1e30))
        top = jnp.max(scores, axis=-1, keepdims=True)
        expd = jnp.exp(scores - top)
        probs = (expd / jnp.sum(expd, axis=-1, keepdims=True)).astype(jnp.bfloat16)
        return jnp.einsum("hqk,khd->qhd", probs, v_part, preferred_element_type=jnp.float32).astype(
            jnp.bfloat16
        )

    out = lax.map(one_group, (split(query, rows), split(keys, keyn), split(values, keyn)))
    out = jnp.moveaxis(out.reshape(mem, groups, rows, group, head_dim), 1, 2)
    return out.reshape(mem, rows, window_width)


def score_fragments(gridded_quantities, observed_reality, valid_flags):
    total = gridded_quantities.shape[0]

    def pair(row):
        diff = row[None] - gridded_quantities
        absd = jnp.sqrt(diff * diff + smooth_sq)
        return (jnp.sum(absd, axis=0), jnp.sum(diff / absd, axis=0))

    pair_sum, pair_grad = lax.map(pair, gridded_quantities)
    dtruth = gridded_quantities - observed_reality[None]
    atruth = jnp.sqrt(dtruth * dtruth + smooth_sq)
    eps_fair = (1.0 - alpha_fair) / total
    probabilistic_score = valid_flags[None] * (
        jnp.mean(atruth, axis=0)
        - (1.0 - eps_fair)
        / (2.0 * total * (total - 1))
        * (jnp.sum(pair_sum, axis=0) - total * jnp.sqrt(jnp.float32(smooth_sq)))
    )
    scaled_derivative = valid_flags[None, None] * (
        dtruth / atruth - (1.0 - eps_fair) / (total - 1) * pair_grad
    )
    return (probabilistic_score, scaled_derivative)


def on_device(
    hidden_embedding,
    random_perturbation,
    norm_gain,
    w_qkv,
    w_proj,
    w_fields,
    observed_reality,
    counts,
):
    mem, rows, window_width = hidden_embedding.shape
    shards = lax.axis_size("node")
    place = lax.axis_index("node")
    own_count = counts[place]
    low_count = jnp.where(place > 0, counts[jnp.maximum(place - 1, 0)], 0)
    high_count = jnp.where(place < shards - 1, counts[jnp.minimum(place + 1, shards - 1)], 0)
    slot = jnp.arange(rows, dtype=jnp.int32)
    local_valid_flags = (slot < own_count).astype(jnp.float32)
    rim = jnp.arange(HALF_WINDOW, dtype=jnp.int32)
    key_live = jnp.concatenate(
        [rim + rows - HALF_WINDOW < low_count, slot < own_count, rim < high_count]
    )
    rel = jnp.arange(rows + 2 * HALF_WINDOW, dtype=jnp.int32)[None, :] - HALF_WINDOW - slot[:, None]
    allowed = (rel >= -HALF_WINDOW) & (rel < HALF_WINDOW) & (key_live[None, :] | (rel == 0))
    x32 = hidden_embedding.astype(jnp.float32)
    mean = jnp.mean(x32, axis=-1, keepdims=True)
    var = jnp.mean((x32 - mean) ** 2, axis=-1, keepdims=True)
    scale_rows = (
        norm_gain[None, None, :] * (1.0 + random_perturbation.astype(jnp.float32))[:, None, :]
    )
    normed = ((x32 - mean) * lax.rsqrt(var + 1e-05) * scale_rows).astype(jnp.bfloat16)
    query = jnp.einsum(
        "mnc,cd->mnd", normed, w_qkv[:, :window_width], preferred_element_type=jnp.float32
    ).astype(jnp.bfloat16)
    window_normed = padded(normed, (("node", 1),), HALF_WINDOW)
    window_kv = jnp.einsum(
        "mnc,cd->mnd", window_normed, w_qkv[:, window_width:], preferred_element_type=jnp.float32
    ).astype(jnp.bfloat16)
    attended = attend(
        query,
        window_kv[..., :window_width],
        window_kv[..., window_width:],
        allowed,
        HEADS,
        HEAD_GROUP,
    )
    updated = (
        x32 + jnp.einsum("mnc,cd->mnd", attended, w_proj, preferred_element_type=jnp.float32)
    ).astype(jnp.bfloat16)
    gridded_quantities = jnp.einsum(
        "mnc,cv->mvn", updated, w_fields, preferred_element_type=jnp.float32
    )
    predicted_outputs = (gridded_quantities * local_valid_flags[None, None, :]).astype(jnp.bfloat16)
    whole_ensemble_outputs = lax.all_gather(predicted_outputs, "ens", axis=0, tiled=True).astype(
        jnp.float32
    )
    probabilistic_score, grad_all = score_fragments(
        whole_ensemble_outputs, observed_reality, local_valid_flags
    )
    scaled_derivative = lax.dynamic_slice_in_dim(grad_all, lax.axis_index("ens") * mem, mem, 0)
    return (predicted_outputs, probabilistic_score, scaled_derivative)


def solution(mesh):
    return jax.shard_map(
        on_device,
        mesh=mesh,
        in_specs=(P("ens", "node", None), P("ens", None), P(), P(), P(), P(), P(None, "node"), P()),
        out_specs=(P("ens", None, "node"), P(None, "node"), P("ens", None, "node")),
        check_vma=False,
    )
```

profile of v0, /device:TPU:25, one launch (start us, length us, event | category | flops | bytes accessed | tf_op | source)
XLA Modules:
  0.0 175.5 jit_solution(10528355080754188211)
XLA Ops:
  0.7 2.1 %convert_reduce_fusion = f32[1024]{0:T(1024)S(1)} fusion(bf16[1,1024,1024]{2,1,0:T(8,128)(2,1)} %param.12), kind=kLoop, calls=%fused_computation.54 | loop fusion | flops 2096128 | bytes 2101248 | tf_op jit(solution)/shard_map/reduce_sum | solution.py:106
  4.5 1.3 copy-done.2
  5.9 3.7 %collective-permute-start = (bf16[1,256,1024]{2,1,0:T(8,128)(2,1)S(1)}, bf16[1,256,1024]{2,1,0:T(8,128)(2,1)}, u32[]{:S(2)}, u32[]{:S(2)}) collective-permute-start(bf16[1,256,1024]{2,1,0:T(8,128)(2,1)S(1)} %get-tuple-element.116), channel_id=1, source_target_pairs={{0,1},{1,2},{2,3},{3,4},{4,5},{5,6},{6,7},{7,8},{8,9},{9,10},{10,1... | collective-permute-start | bytes 1572872 | tf_op jit(solution)/shard_map/ppermute | solution.py:20
  9.6 1.9 %collective-permute-start.1 = (bf16[1,256,1024]{2,1,0:T(8,128)(2,1)S(1)}, bf16[1,256,1024]{2,1,0:T(8,128)(2,1)}, u32[]{:S(2)}, u32[]{:S(2)}) collective-permute-start(bf16[1,256,1024]{2,1,0:T(8,128)(2,1)S(1)} %get-tuple-element.117), channel_id=1, source_target_pairs={{1,0},{2,1},{3,2},{4,3},{5,4},{6,5},{7,6},{8,7},{9,8},{10,9},{11,1... | collective-permute-start | bytes 1572872 | tf_op jit(solution)/shard_map/ppermute | solution.py:23
  12.2 1.3 iota_compare_fusion
  14.8 6.2 %fusion.79 = bf16[1024,1024]{0,1:T(8,128)(2,1)} fusion(bf16[1024,3072]{1,0:T(8,128)(2,1)} %param.15, bf16[1,1024,1024]{2,1,0:T(8,128)(2,1)} %copy-done.2), kind=kOutput, calls=%fused_computation.72 | convolution fusion | flops 2148532224 | bytes 6291456 | tf_op jit(solution)/shard_map/mnc,cd->mnd/dot_general | solution.py:112
  21.0 2.0 %collective-permute-done.1 = bf16[1,256,1024]{2,1,0:T(8,128)(2,1)} collective-permute-done((bf16[1,256,1024]{2,1,0:T(8,128)(2,1)S(1)}, bf16[1,256,1024]{2,1,0:T(8,128)(2,1)}, u32[]{:S(2)}, u32[]{:S(2)}) %collective-permute-start.1) | collective-permute-done | bytes 524320 | tf_op jit(solution)/shard_map/ppermute | solution.py:23
  23.0 8.8 %fusion.62 = bf16[1,1536,2048]{2,1,0:T(8,128)(2,1)S(1)} fusion(bf16[1024,3072]{1,0:T(8,128)(2,1)} %param.15, bf16[1,256,1024]{2,1,0:T(8,128)(2,1)} %collective-permute-done.1, bf16[1,1024,1024]{2,1,0:T(8,128)(2,1)S(1)} %copy-done.3, bf16[1,256,1024]{2,1,0:T(8,128)(2,1)} %collective-permute-done), kind=kOutput, calls=%fused_computation.51 | convolution fusion | flops 6455033856 | bytes 13631488 | tf_op jit(solution)/shard_map/mnc,cd->mnd/dot_general | solution.py:116
  31.8 3.6 %fusion.103 = (bf16[1,1536,1024]{2,1,0:T(8,128)(2,1)}, bf16[1,1536,1024]{2,1,0:T(8,128)(2,1)}) fusion(bf16[1,1536,2048]{2,1,0:T(8,128)(2,1)S(1)} %fusion.62), kind=kLoop, calls=%fused_computation.95 | loop fusion | bytes 12582912 | tf_op jit(solution)/shard_map/slice | solution.py:121
  35.4 4.6 %copy.18 = bf16[1,1536,1024]{1,2,0:T(8,128)(2,1)} copy(bf16[1,1536,1024]{2,1,0:T(8,128)(2,1)} %get-tuple-element.114) | data formatting | bytes 6291456 | tf_op jit(solution)/shard_map/slice | solution.py:121
  40.0 4.7 %copy.17 = bf16[1,1536,1024]{1,2,0:T(8,128)(2,1)} copy(bf16[1,1536,1024]{2,1,0:T(8,128)(2,1)} %get-tuple-element.115) | data formatting | bytes 6291456 | tf_op jit(solution)/shard_map/slice | solution.py:122
  44.7 108.8 %while.24 = (s32[]{:T(128)}, bf16[4,1024,4,64]{1,3,2,0:T(8,128)(2,1)}, bf16[4,1536,4,64]{1,3,2,0:T(8,128)(2,1)}, bf16[4,1024,4,64]{1,3,2,0:T(8,128)(2,1)}, bf16[...) while((s32[]{:T(128)}, ...), condition=%wide.region_5.6_spmd.clone, body=%wide.region_2.5_spmd.clone.sunk | while | flops 2483821568 | bytes 8694357 | solution.py:52
  44.7 3.7 %fusion.122 = pred[1024,1536]{1,0:T(8,128)(4,1)} fusion(s32[1536]{0:T(1024)S(1)} %get-tuple-element.225, pred[1536]{0:T(1024)(128)(4,1)S(1)} %get-tuple-element.226), kind=kLoop, calls=%fused_computation.21.clone.1 | loop fusion | flops 11010048 | bytes 1580544 | tf_op jit(solution)/shard_map/and | solution.py:104
  48.4 10.6 %fusion.123 = f32[4,1024]{1,0:T(4,128)S(1)} fusion(pred[1024,1536]{1,0:T(8,128)(4,1)} %fusion.122, bf16[4,1536,4,64]{1,3,2,0:T(8,128)(2,1)} %get-tuple-element.224, s32[]{:T(128)} %get-tuple-element.212, bf16[4,1024,4,64]{1,3,2,0:T(8,128)(2,1)} %get-tuple-element.223), kind=kOutput, calls=%fused_computation.94.clone.1 | convolution fusion | flops 830473728 | bytes 2900992 | tf_op jit(solution)/shard_map/while/body/eval_jaxpr/sub | solution.py:46
  59.0 12.9 %fusion.124 = bf16[4,1024,4,64]{1,3,2,0:T(8,128)(2,1)} fusion(bf16[4,1024,4,64]{1,3,2,0:T(8,128)(2,1)} %get-tuple-element.213, s32[]{:T(128)} %get-tuple-element.212, f32[4,1024]{1,0:T(4,128)S(1)} %fusion.123, pred[1024,1536]{1,0:T(8,128)(4,1)} %fusion.122, bf16[4,1536,4,64]{1,3,2,0:T(8,128)(2,1)} %get-tuple-element.222, ...), kind=kOutput, calls=%fused_computation.26.clone.1 | convolution fusion | flops 1642337792 | bytes 4212736 | tf_op jit(solution)/shard_map/while/body/eval_jaxpr/hqk,khd->qhd/dot_general | solution.py:48
  72.0 3.7 %fusion.122 = pred[1024,1536]{1,0:T(8,128)(4,1)} fusion(s32[1536]{0:T(1024)S(1)} %get-tuple-element.225, pred[1536]{0:T(1024)(128)(4,1)S(1)} %get-tuple-element.226), kind=kLoop, calls=%fused_computation.21.clone.1 | loop fusion | flops 11010048 | bytes 1580544 | tf_op jit(solution)/shard_map/and | solution.py:104
  75.6 10.6 %fusion.123 = f32[4,1024]{1,0:T(4,128)S(1)} fusion(pred[1024,1536]{1,0:T(8,128)(4,1)} %fusion.122, bf16[4,1536,4,64]{1,3,2,0:T(8,128)(2,1)} %get-tuple-element.224, s32[]{:T(128)} %get-tuple-element.212, bf16[4,1024,4,64]{1,3,2,0:T(8,128)(2,1)} %get-tuple-element.223), kind=kOutput, calls=%fused_computation.94.clone.1 | convolution fusion | flops 830473728 | bytes 2900992 | tf_op jit(solution)/shard_map/while/body/eval_jaxpr/sub | solution.py:46
  86.3 12.9 %fusion.124 = bf16[4,1024,4,64]{1,3,2,0:T(8,128)(2,1)} fusion(bf16[4,1024,4,64]{1,3,2,0:T(8,128)(2,1)} %get-tuple-element.213, s32[]{:T(128)} %get-tuple-element.212, f32[4,1024]{1,0:T(4,128)S(1)} %fusion.123, pred[1024,1536]{1,0:T(8,128)(4,1)} %fusion.122, bf16[4,1536,4,64]{1,3,2,0:T(8,128)(2,1)} %get-tuple-element.222, ...), kind=kOutput, calls=%fused_computation.26.clone.1 | convolution fusion | flops 1642337792 | bytes 4212736 | tf_op jit(solution)/shard_map/while/body/eval_jaxpr/hqk,khd->qhd/dot_general | solution.py:48
  99.2 3.7 %fusion.122 = pred[1024,1536]{1,0:T(8,128)(4,1)} fusion(s32[1536]{0:T(1024)S(1)} %get-tuple-element.225, pred[1536]{0:T(1024)(128)(4,1)S(1)} %get-tuple-element.226), kind=kLoop, calls=%fused_computation.21.clone.1 | loop fusion | flops 11010048 | bytes 1580544 | tf_op jit(solution)/shard_map/and | solution.py:104
  102.8 10.6 %fusion.123 = f32[4,1024]{1,0:T(4,128)S(1)} fusion(pred[1024,1536]{1,0:T(8,128)(4,1)} %fusion.122, bf16[4,1536,4,64]{1,3,2,0:T(8,128)(2,1)} %get-tuple-element.224, s32[]{:T(128)} %get-tuple-element.212, bf16[4,1024,4,64]{1,3,2,0:T(8,128)(2,1)} %get-tuple-element.223), kind=kOutput, calls=%fused_computation.94.clone.1 | convolution fusion | flops 830473728 | bytes 2900992 | tf_op jit(solution)/shard_map/while/body/eval_jaxpr/sub | solution.py:46
  113.5 12.9 %fusion.124 = bf16[4,1024,4,64]{1,3,2,0:T(8,128)(2,1)} fusion(bf16[4,1024,4,64]{1,3,2,0:T(8,128)(2,1)} %get-tuple-element.213, s32[]{:T(128)} %get-tuple-element.212, f32[4,1024]{1,0:T(4,128)S(1)} %fusion.123, pred[1024,1536]{1,0:T(8,128)(4,1)} %fusion.122, bf16[4,1536,4,64]{1,3,2,0:T(8,128)(2,1)} %get-tuple-element.222, ...), kind=kOutput, calls=%fused_computation.26.clone.1 | convolution fusion | flops 1642337792 | bytes 4212736 | tf_op jit(solution)/shard_map/while/body/eval_jaxpr/hqk,khd->qhd/dot_general | solution.py:48
  126.4 3.7 %fusion.122 = pred[1024,1536]{1,0:T(8,128)(4,1)} fusion(s32[1536]{0:T(1024)S(1)} %get-tuple-element.225, pred[1536]{0:T(1024)(128)(4,1)S(1)} %get-tuple-element.226), kind=kLoop, calls=%fused_computation.21.clone.1 | loop fusion | flops 11010048 | bytes 1580544 | tf_op jit(solution)/shard_map/and | solution.py:104
  130.0 10.6 %fusion.123 = f32[4,1024]{1,0:T(4,128)S(1)} fusion(pred[1024,1536]{1,0:T(8,128)(4,1)} %fusion.122, bf16[4,1536,4,64]{1,3,2,0:T(8,128)(2,1)} %get-tuple-element.224, s32[]{:T(128)} %get-tuple-element.212, bf16[4,1024,4,64]{1,3,2,0:T(8,128)(2,1)} %get-tuple-element.223), kind=kOutput, calls=%fused_computation.94.clone.1 | convolution fusion | flops 830473728 | bytes 2900992 | tf_op jit(solution)/shard_map/while/body/eval_jaxpr/sub | solution.py:46
  140.7 12.9 %fusion.124 = bf16[4,1024,4,64]{1,3,2,0:T(8,128)(2,1)} fusion(bf16[4,1024,4,64]{1,3,2,0:T(8,128)(2,1)} %get-tuple-element.213, s32[]{:T(128)} %get-tuple-element.212, f32[4,1024]{1,0:T(4,128)S(1)} %fusion.123, pred[1024,1536]{1,0:T(8,128)(4,1)} %fusion.122, bf16[4,1536,4,64]{1,3,2,0:T(8,128)(2,1)} %get-tuple-element.222, ...), kind=kOutput, calls=%fused_computation.26.clone.1 | convolution fusion | flops 1642337792 | bytes 4212736 | tf_op jit(solution)/shard_map/while/body/eval_jaxpr/hqk,khd->qhd/dot_general | solution.py:48
  153.6 5.2 %fusion.90 = bf16[1,100,1024]{2,1,0:T(8,128)(2,1)S(1)} fusion(bf16[1024,100]{0,1:T(8,128)(2,1)S(1)} %copy-done.10, bf16[1024,1024]{0,1:T(8,128)(2,1)} %bitcast.122, bf16[1024,1024]{1,0:T(8,128)(2,1)S(1)} %copy-done, bf16[1,1024,1024]{2,1,0:T(8,128)(2,1)} %param.12, f32[1024]{0:T(1024)S(1)} %copy-done.6), kind=kOutput, calls=%fused_computation.75 | convolution fusion | flops 2360549376 | bytes 6705152 | tf_op jit(solution)/shard_map/mnc,cv->mvn/dot_general | solution.py:130
  159.5 7.9 %all-gather.1 = bf16[2,100,1024]{2,1,0:T(8,128)(2,1)S(1)} all-gather(bf16[1,100,1024]{2,1,0:T(8,128)(2,1)S(1)} %fusion.90), channel_id=2, replica_groups=mesh['ens'=2,'node'=16] {'ens'}, dimensions={0}, use_global_device_ids=true | all-gather | bytes 614400 | tf_op jit(solution)/shard_map/all_gather | solution.py:134
  167.5 3.1 %while.23 = (s32[]{:T(128)}, f32[2,100,1024]{2,1,0:T(8,128)}, f32[2,100,1024]{2,1,0:T(8,128)}, f32[2,100,1024]{2,1,0:T(8,128)S(1)}, s32[]{:T(128)}) while((s32[]{:T(128)}, f32[2,100,1024]{2,1,0:T(8,128)}, f32[2,100,1024]{2,1,0:T(8,128)}, f32[2,100,1024]{2,1,0:T(8,128)S(1)}, s32[]{:T(128)}) %tuple.58), condition=%wide.region_10.11_spmd, body=%wide.region_7.10_spmd.sunk | while | flops 1024002 | bytes 4538945 | solution.py:65
  168.1 1.0 bitcast_dynamic-update-slice_fusion.3
  169.6 1.0 bitcast_dynamic-update-slice_fusion.3
  170.6 1.5 broadcast_subtract_fusion
  172.3 1.2 copy.19
  173.4 1.3 reduce_sum.66
  (43 shorter events, 5.3 us)
Async XLA Ops:
  0.6 152.9 %copy-start = (bf16[1024,1024]{1,0:T(8,128)(2,1)S(1)}, bf16[1024,1024]{1,0:T(8,128)(2,1)}, u32[]{:S(2)}) copy-start(bf16[1024,1024]{1,0:T(8,128)(2,1)} %param.16) | copy-start | bytes 6291460
  0.6 2.4 %copy-start.1 = (bf16[1,1024,1024]{2,1,0:T(8,128)(2,1)S(1)}, bf16[1,1024,1024]{2,1,0:T(8,128)(2,1)}, u32[]{:S(2)}) copy-start(bf16[1,1024,1024]{2,1,0:T(8,128)(2,1)} %param.12) | copy-start | bytes 6291460
  0.7 3.1 %copy-start.9 = (bf16[1,1024]{1,0:T(2,128)(2,1)S(1)}, bf16[1,1024]{1,0:T(2,128)(2,1)}, u32[]{:S(2)}) copy-start(bf16[1,1024]{1,0:T(2,128)(2,1)} %param.13) | copy-start | bytes 6148
  0.7 3.1 %copy-start.8 = (f32[1024]{0:T(1024)S(1)}, f32[1024]{0:T(1024)}, u32[]{:S(2)}) copy-start(f32[1024]{0:T(1024)} %param.14) | copy-start | bytes 12292
  3.8 7.8 %copy-start.7 = (s32[16]{0:T(128)S(1)}, s32[16]{0:T(128)}, u32[]{:S(2)}) copy-start(s32[16]{0:T(128)} %param.19) | copy-start | bytes 196
  4.5 1.4 copy-start.2
  5.9 15.1 %collective-permute-start = (bf16[1,256,1024]{2,1,0:T(8,128)(2,1)S(1)}, bf16[1,256,1024]{2,1,0:T(8,128)(2,1)}, u32[]{:S(2)}, u32[]{:S(2)}) collective-permute-start(bf16[1,256,1024]{2,1,0:T(8,128)(2,1)S(1)} %get-tuple-element.116), channel_id=1, source_target_pairs={{0,1},{1,2},{2,3},{3,4},{4,5},{5,6},{6,7},{7,8},{8,9},{9,10},{10,1... | collective-permute-start | bytes 1572872 | tf_op jit(solution)/shard_map/ppermute | solution.py:20
  9.6 13.4 %collective-permute-start.1 = (bf16[1,256,1024]{2,1,0:T(8,128)(2,1)S(1)}, bf16[1,256,1024]{2,1,0:T(8,128)(2,1)}, u32[]{:S(2)}, u32[]{:S(2)}) collective-permute-start(bf16[1,256,1024]{2,1,0:T(8,128)(2,1)S(1)} %get-tuple-element.117), channel_id=1, source_target_pairs={{1,0},{2,1},{3,2},{4,3},{5,4},{6,5},{7,6},{8,7},{9,8},{10,9},{11,1... | collective-permute-start | bytes 1572872 | tf_op jit(solution)/shard_map/ppermute | solution.py:23
  14.8 8.2 %copy-start.3 = (bf16[1,1024,1024]{2,1,0:T(8,128)(2,1)S(1)}, bf16[1,1024,1024]{2,1,0:T(8,128)(2,1)}, u32[]{:S(2)}) copy-start(bf16[1,1024,1024]{2,1,0:T(8,128)(2,1)} %copy-done.2) | copy-start | bytes 6291460
  44.7 108.8 %copy-start.6 = (f32[1024]{0:T(1024)S(1)}, f32[1024]{0:T(1024)}, u32[]{:S(2)}) copy-start(f32[1024]{0:T(1024)} %get-tuple-element.125) | copy-start | bytes 12292
  44.7 108.8 %copy-start.10 = (bf16[1024,100]{0,1:T(8,128)(2,1)S(1)}, bf16[1024,100]{0,1:T(8,128)(2,1)}, u32[]{:S(2)}) copy-start(bf16[1024,100]{0,1:T(8,128)(2,1)} %param.17) | copy-start | bytes 614404
  158.8 0.7 copy-start.4
  170.6 1.5 copy-start.5
where the time goes:
time: 176 us
  matrix products  114 us (65%)
  other arithmetic  24.3 us (14%)
  local copies, waits for them, and re-layouts  19.1 us (11%)
  blocking collectives  7.92 us (4%)
  starting transfers between devices  5.6 us (3%)
  between operations  2.15 us (1%)
  waiting for transfers between devices  2.02 us (1%)
    dot_general x4, matrix products, one_group(): jnp.einsum('hqk,khd->qhd', probs, v_part, preferred_element_type=jnp.floa...  51.6 us
    sub x4, matrix products, one_group(): expd = jnp.exp(scores - top)  42.5 us
    and x4, other arithmetic, on_device(): (rel >= -HALF_WINDOW) & (rel < HALF_WINDOW)  14.7 us
    dot_general x1, matrix products, on_device(): jnp.einsum('mnc,cd->mnd', window_normed, w_qkv[:, window_width:], preferr...  8.82 us
    slice x2, local copies, waits for them, and re-layouts, on_device(): window_kv[..., :window_width]  8.2 us
    all_gather x1, blocking collectives, on_device(): lax.all_gather(predicted_outputs, 'ens', axis=0, tiled=True)  7.92 us
    dot_general x1, matrix products, on_device(): jnp.einsum('mnc,cd->mnd', normed, w_qkv[:, :window_width], preferred_elem...  6.17 us
    dot_general x1, matrix products, on_device(): jnp.einsum('mnc,cv->mvn', updated, w_fields, preferred_element_type=jnp.f...  5.21 us
  transfers between devices with their start and end apart: 2, of which 1 were waited for; matrix products, arithmetic and copies ran while one was open for 5% of the time, Pallas kernels for 0%

commit v1 on v0

v1 whole, which is shorter than its diff:
```python
import functools

import jax
import jax.numpy as jnp
from jax import lax
from jax.experimental import pallas as pl
from jax.experimental.pallas import tpu as pltpu
from jax.sharding import PartitionSpec as P

HEADS = 16
HALF_WINDOW = 256
LANES = 128

smooth_sq = 0.01
alpha_fair = 0.95
NEG = -1e30
LOG2E = 1.4426950408889634

F32 = jnp.float32
BF16 = jnp.bfloat16
VMEM = pl.BlockSpec(memory_space=pltpu.VMEM)
SMEM = pl.BlockSpec(memory_space=pltpu.SMEM)
ANY = pl.BlockSpec(memory_space=pl.ANY)


def iota(shape, dim):
    return lax.broadcasted_iota(jnp.int32, shape, dim)


def normalize(x, scale):
    x32 = x.astype(F32)
    mean = jnp.mean(x32, axis=-1, keepdims=True)
    centred = x32 - mean
    var = jnp.mean(centred * centred, axis=-1, keepdims=True)
    return (centred * lax.rsqrt(var + 1e-05) * scale).astype(BF16)


def channel_scale(gain_ref, pert_ref):
    return gain_ref[...] * (1.0 + pert_ref[...].astype(F32))


def dead_flags(rows, live):
    return jnp.where((iota((rows, LANES), 0) >= live) & (iota((rows, LANES), 1) == 0), 1.0, 0.0).astype(BF16)


def attend_block(query, keys, values, flags, store, pairs):
    half = HALF_WINDOW
    row = iota((2 * half, half), 0) % half
    col = iota((2 * half, half), 1)
    near = jnp.where(col >= row, 0.0, NEG)
    far = jnp.where(col < row, 0.0, NEG)
    bias = jnp.where(iota((2 * half, LANES), 1) == 0, NEG, 0.0).astype(BF16)
    ones = jnp.ones((3 * half, LANES), BF16)
    lane = iota((half, LANES), 1)
    first = lane < LANES // 2
    for c in range(pairs):
        q = query(c)
        zero = jnp.zeros_like(q)
        both = jnp.concatenate([jnp.where(first, q, zero), jnp.where(first, zero, q)], axis=0)
        both = jnp.concatenate([both, bias], axis=1)
        k = jnp.concatenate([keys(c), flags], axis=1)
        s = lax.dot_general(both, k, (((1,), (1,)), ((), ())), preferred_element_type=F32)
        s = jnp.concatenate([s[:, :half] + near, s[:, half : 2 * half], s[:, 2 * half :] + far], axis=1)
        top = jnp.max(s, axis=1, keepdims=True)
        p = jnp.exp2((s - top) * LOG2E).astype(BF16)
        v = jnp.concatenate([values(c), ones], axis=1)
        o = jnp.dot(p, v, preferred_element_type=F32)
        num = jnp.where(first, o[:half, :LANES], o[half:, :LANES])
        den = jnp.where(first, o[:half, LANES:], o[half:, LANES:])
        store(c, (num / den).astype(BF16))


def decode(x, attended, w_proj, w_fields):
    updated = (x.astype(F32) + jnp.dot(attended, w_proj, preferred_element_type=F32)).astype(BF16)
    return lax.dot_general(w_fields, updated, (((0,), (1,)), ((), ())), preferred_element_type=F32)


def cols(c):
    return slice(c * LANES, (c + 1) * LANES)


def inner_kernel(counts, x_ref, pert, gain, w_qkv, w_proj, w_fields, out, q_edge, kv, normed, q_in, att):
    rows, width = x_ref.shape
    half = HALF_WINDOW
    own = counts[lax.axis_index("node")]
    scale = channel_scale(gain, pert)
    for b in range(rows // half):
        normed[b * half : (b + 1) * half, :] = normalize(x_ref[b * half : (b + 1) * half, :], scale)
    step = 256

    def project(j, _):
        at = pl.ds(pl.multiple_of(j * step, step), step)
        q = jnp.dot(normed[...], w_qkv[:, at], preferred_element_type=F32).astype(BF16)
        q = q * jnp.asarray((width // HEADS) ** -0.5, BF16)
        q_edge[:half, at] = q[:half]
        q_in[:, at] = q[half : rows - half]
        q_edge[half:, at] = q[rows - half :]
        return 0

    lax.fori_loop(0, width // step, project, 0)

    def project_kv(j, _):
        at = pl.ds(pl.multiple_of(j * step, step), step)
        src = pl.ds(pl.multiple_of(width + j * step, step), step)
        kv[:, at] = jnp.dot(normed[...], w_qkv[:, src], preferred_element_type=F32).astype(BF16)
        return 0

    lax.fori_loop(0, 2 * width // step, project_kv, 0)

    def block(b, _):
        start = pl.multiple_of(b * half, half)
        here = pl.ds(start, half)
        window = pl.ds(start, 3 * half)

        def store(c, value):
            att[:, cols(c)] = value

        attend_block(
            lambda c: q_in[here, cols(c)],
            lambda c: kv[window, cols(c)],
            lambda c: kv[window, slice(width + c * LANES, width + (c + 1) * LANES)],
            dead_flags(3 * half, own - start),
            store,
            width // LANES,
        )
        x = x_ref[pl.ds(pl.multiple_of(start + half, half), half), :]
        fields = decode(x, att[...], w_proj[...], w_fields[...])
        live = iota(fields.shape, 1) + start + half < own
        out[:, pl.ds(start, half)] = jnp.where(live, fields, 0.0).astype(BF16)
        return 0

    lax.fori_loop(0, rows // half - 2, block, 0)


def edge_kernel(counts, low, high, x_ref, pert, gain, w_qkv, w_proj, w_fields, q_edge, kv, out, normed, halo, att):
    rows, width = x_ref.shape
    half = HALF_WINDOW
    place = lax.axis_index("node")
    shards = counts.shape[0]
    own = counts[place]
    low_live = jnp.where(place > 0, counts[jnp.maximum(place - 1, 0)], 0)
    high_live = jnp.where(place < shards - 1, counts[jnp.minimum(place + 1, shards - 1)], 0)
    scale = channel_scale(gain, pert)
    normed[:half, :] = normalize(low[...], scale)
    normed[half:, :] = normalize(high[...], scale)
    step = 256

    def project_kv(j, _):
        at = pl.ds(pl.multiple_of(j * step, step), step)
        src = pl.ds(pl.multiple_of(width + j * step, step), step)
        halo[:, at] = jnp.dot(normed[...], w_qkv[:, src], preferred_element_type=F32).astype(BF16)
        return 0

    lax.fori_loop(0, 2 * width // step, project_kv, 0)

    def store(c, value):
        att[:, cols(c)] = value

    def vcols(c):
        return slice(width + c * LANES, width + (c + 1) * LANES)

    flags_low = jnp.concatenate([dead_flags(half, low_live - (rows - half)), dead_flags(2 * half, own)], axis=0)
    flags_high = jnp.concatenate(
        [dead_flags(2 * half, own - (rows - 2 * half)), dead_flags(half, high_live)], axis=0
    )
    tail = rows - 2 * half
    for side in range(2):
        if side == 0:
            q = lambda c: q_edge[:half, cols(c)]
            k = lambda c: jnp.concatenate([halo[:half, cols(c)], kv[: 2 * half, cols(c)]], axis=0)
            v = lambda c: jnp.concatenate([halo[:half, vcols(c)], kv[: 2 * half, vcols(c)]], axis=0)
            flags, start = flags_low, 0
        else:
            q = lambda c: q_edge[half:, cols(c)]
            k = lambda c: jnp.concatenate([kv[tail:, cols(c)], halo[half:, cols(c)]], axis=0)
            v = lambda c: jnp.concatenate([kv[tail:, vcols(c)], halo[half:, vcols(c)]], axis=0)
            flags, start = flags_high, rows - half
        attend_block(q, k, v, flags, store, width // LANES)
        fields = decode(x_ref[start : start + half, :], att[...], w_proj[...], w_fields[...])
        live = iota(fields.shape, 1) + start < own
        out[:, side * half : (side + 1) * half] = jnp.where(live, fields, 0.0).astype(BF16)


def score_values(mine, others, truth, live):
    total = 1 + len(others)
    eps = (1.0 - alpha_fair) / total
    mine = mine.astype(F32)
    others = [o.astype(F32) for o in others]

    def smooth(d):
        return jnp.sqrt(d * d + smooth_sq)

    d = mine - truth
    a = smooth(d)
    grad = d / a
    truth_sum = a
    for o in others:
        truth_sum = truth_sum + smooth(o - truth)
    pair_sum = jnp.zeros_like(a)
    pair_grad = jnp.zeros_like(a)
    for o in others:
        d = mine - o
        a = smooth(d)
        pair_sum = pair_sum + 2.0 * a
        pair_grad = pair_grad + d / a
    for i in range(len(others)):
        for j in range(i + 1, len(others)):
            pair_sum = pair_sum + 2.0 * smooth(others[i] - others[j])
    score = truth_sum * (1.0 / total) - (1.0 - eps) / (2.0 * total * (total - 1)) * pair_sum
    deriv = grad - (1.0 - eps) / (total - 1) * pair_grad
    return jnp.where(live, score, 0.0), jnp.where(live, deriv, 0.0)


def score_kernel(others, carried, place_of, counts, *refs):
    mine, rest, truth = refs[0], refs[1 : 1 + others], refs[1 + others]
    pred, score, deriv = refs[2 + others + carried :]
    width = mine.shape[1]
    own = counts[lax.axis_index("node")]
    start = place_of(pl.program_id(0)) * width
    live = iota(mine.shape, 1) + start < own
    pred[...] = mine[...]
    score[...], deriv[...] = score_values(mine[...], [r[...] for r in rest], truth[...], live)


def score_call(counts, mine, others, truth, carried, place_of, blocks):
    half = HALF_WINDOW
    fields, nodes = truth.shape
    part = pl.BlockSpec((fields, half), lambda i: (0, i))
    whole = pl.BlockSpec((fields, half), lambda i: (0, place_of(i)))
    shapes = [
        jax.ShapeDtypeStruct((fields, nodes), BF16),
        jax.ShapeDtypeStruct((fields, nodes), F32),
        jax.ShapeDtypeStruct((fields, nodes), F32),
    ]
    count = len(others)
    return pl.pallas_call(
        functools.partial(score_kernel, count, len(carried), place_of),
        grid=(blocks,),
        in_specs=[SMEM] + [part] * (1 + count) + [whole] + [ANY] * len(carried),
        out_specs=[whole] * 3,
        out_shape=shapes,
        input_output_aliases={3 + count + i: i for i in range(len(carried))},
        cost_estimate=pl.CostEstimate(
            flops=40 * fields * half * blocks, bytes_accessed=20 * fields * half * blocks, transcendentals=0
        ),
    )(counts, mine, *others, truth, *carried)


def on_device(hidden, pert, gain, w_qkv, w_proj, w_fields, truth, counts):
    _, rows, width = hidden.shape
    fields = w_fields.shape[1]
    half = HALF_WINDOW
    blocks = rows // half
    x = hidden[0]
    gain = gain.reshape(1, width)
    shards = lax.axis_size("node")
    members = lax.axis_size("ens")
    up = [(i, i + 1) for i in range(shards - 1)]
    down = [(t, s) for s, t in up]
    low = lax.ppermute(x[rows - half :], "node", up)
    high = lax.ppermute(x[:half], "node", down)

    inner = rows - 2 * half
    pred_in, q_edge, kv = pl.pallas_call(
        inner_kernel,
        in_specs=[SMEM, VMEM, VMEM, VMEM, VMEM, VMEM, VMEM],
        out_specs=[VMEM, VMEM, VMEM],
        out_shape=[
            jax.ShapeDtypeStruct((fields, inner), BF16),
            jax.ShapeDtypeStruct((2 * half, width), BF16),
            jax.ShapeDtypeStruct((rows, 2 * width), BF16),
        ],
        scratch_shapes=[
            pltpu.VMEM((rows, width), BF16),
            pltpu.VMEM((inner, width), BF16),
            pltpu.VMEM((half, width), BF16),
        ],
        cost_estimate=pl.CostEstimate(
            flops=2 * rows * width * 3 * width + 2 * inner * width * width + 12 * inner * width * half,
            bytes_accessed=10 * width * width,
            transcendentals=inner * HEADS * 3 * half,
        ),
        name="inner_blocks",
    )(counts, x, pert, gain, w_qkv, w_proj, w_fields)

    def exchange(part):
        return [
            lax.ppermute(part, "ens", [(i, (i + s) % members) for i in range(members)])
            for s in range(1, members)
        ]

    others_in = exchange(pred_in)
    pred_edge = pl.pallas_call(
        edge_kernel,
        in_specs=[SMEM] + [VMEM] * 10,
        out_specs=VMEM,
        out_shape=jax.ShapeDtypeStruct((fields, 2 * half), BF16),
        scratch_shapes=[
            pltpu.VMEM((2 * half, width), BF16),
            pltpu.VMEM((2 * half, 2 * width), BF16),
            pltpu.VMEM((half, width), BF16),
        ],
        cost_estimate=pl.CostEstimate(
            flops=2 * 2 * half * width * 3 * width + 12 * 2 * half * width * half,
            bytes_accessed=10 * width * width,
            transcendentals=2 * half * HEADS * 3 * half,
        ),
        name="edge_blocks",
    )(counts, low, high, x, pert, gain, w_qkv, w_proj, w_fields, q_edge, kv)
    others_edge = exchange(pred_edge)
    partial = score_call(counts, pred_in, others_in, truth, [], lambda i: i + 1, blocks - 2)
    pred, score, deriv = score_call(
        counts, pred_edge, others_edge, truth, partial, lambda i: i * (blocks - 1), 2
    )
    return pred[None], score, deriv[None]


def solution(mesh):
    return jax.shard_map(
        on_device,
        mesh=mesh,
        in_specs=(P("ens", "node", None), P("ens", None), P(), P(), P(), P(), P(None, "node"), P()),
        out_specs=(P("ens", None, "node"), P(None, "node"), P("ens", None, "node")),
        check_vma=False,
    )
```

time: 176 us -> 69.2 us (0.39)
  the two profiles are of different devices: /device:TPU:25 before, /device:TPU:0 now
where the time goes in v1:
time: 69.2 us; the launch traced here: 68.9 us
  Pallas kernels  51 us (74%)
  starting transfers between devices  7.34 us (11%)
  local copies, waits for them, and re-layouts  6.62 us (10%)
  waiting for transfers between devices  3.21 us (5%)
  between operations  0.7 us (1%)
    pallas_call x1, Pallas kernels, on_device(): pl.pallas_call(inner_kernel, in_specs=[SMEM, VMEM, VMEM, VMEM, VMEM, VMEM...  26.1 us
    pallas_call x1, Pallas kernels, on_device(): pl.pallas_call(edge_kernel, in_specs=[SMEM] + [VMEM] * 10, out_specs=VMEM...  20.8 us
    unnamed x12, local copies, waits for them, and re-layouts  5.31 us
    pallas_call x2, Pallas kernels, score_call(): pl.pallas_call(functools.partial(score_kernel, count, len(carried), place...  4.17 us
    ppermute x2, waiting for transfers between devices, exchange(): lax.ppermute(part, 'ens', [(i, (i + s) % members) for i in range(members)])  3.2 us
    ppermute x1, starting transfers between devices, on_device(): low = lax.ppermute(x[rows - half:], 'node', up)  3.06 us
    ppermute x2, starting transfers between devices, exchange(): lax.ppermute(part, 'ens', [(i, (i + s) % members) for i in range(members)])  2.99 us
  transfers between devices with their start and end apart: 4, of which 1 were waited for; matrix products, arithmetic and copies ran while one was open for 1% of the time, Pallas kernels for 71%

profile of v1, /device:TPU:0, one launch (start us, length us, event | category | flops | bytes accessed | tf_op | source)
XLA Modules:
  0.0 68.9 jit_solution(1262710378353443649)
XLA Ops:
  0.6 0.0 copy-start
  0.6 1.3 %slice_bitcast_fusion = (bf16[256,1024]{1,0:T(8,128)(2,1)S(1)}, bf16[256,1024]{1,0:T(8,128)(2,1)S(1)}) fusion(bf16[1,1024,1024]{2,1,0:T(8,128)(2,1)} %param.8), kind=kLoop, calls=%fused_computation | loop fusion | bytes 2097152 | tf_op jit(solution)/shard_map/slice | solution.py:261
  2.0 1.3 %collective-permute-start.1 = (bf16[256,1024]{1,0:T(8,128)(2,1)S(1)}, bf16[256,1024]{1,0:T(8,128)(2,1)S(1)}, u32[]{:S(2)}, u32[]{:S(2)}) collective-permute-start(bf16[256,1024]{1,0:T(8,128)(2,1)S(1)} %get-tuple-element.24), channel_id=1, source_target_pairs={{1,0},{2,1},{3,2},{4,3},{5,4},{6,5},{7,6},{8,7},{9,8},{10,9},{11,1... | collective-permute-start | bytes 1572872 | tf_op jit(solution)/shard_map/ppermute | solution.py:261
  3.3 3.1 %collective-permute-start = (bf16[256,1024]{1,0:T(8,128)(2,1)S(1)}, bf16[256,1024]{1,0:T(8,128)(2,1)S(1)}, u32[]{:S(2)}, u32[]{:S(2)}) collective-permute-start(bf16[256,1024]{1,0:T(8,128)(2,1)S(1)} %get-tuple-element.25), channel_id=1, source_target_pairs={{0,1},{1,2},{2,3},{3,4},{4,5},{5,6},{6,7},{7,8},{8,9},{9,10},{10,1... | collective-permute-start | bytes 1572872 | tf_op jit(solution)/shard_map/ppermute | solution.py:260
  6.3 0.0 copy-done
  6.3 0.9 %copy.15.w_fields = bf16[1024,100]{1,0:T(8,128)(2,1)} copy(bf16[1024,100]{0,1:T(8,128)(2,1)S(1)} %copy-done) | data formatting | bytes 409600 | tf_op args[5]
  7.2 26.1 %inner_blocks.1 = (bf16[100,512]{1,0:T(8,128)(2,1)}, bf16[512,1024]{1,0:T(8,128)(2,1)}, bf16[1024,2048]{1,0:T(8,128)(2,1)}) custom-call(s32[16]{0:T(128)} %counts.7, bf16[1024,1024]{1,0:T(8,128)(2,1)} %bitcast.9, bf16[1,1024]{1,0:T(2,128)(2,1)} %pert.3, f32[1,1024]{1,0:T(1,128)} %bitcast.12, bf16[1024,3072]{1,0:T(8,128)(2,1)} %w_qkv.3, ...), custom_call_target="tpu_custom_call" | custom-call | flops 9126805504 | bytes 10485760 | tf_op jit(solution)/shard_map/inner_blocks/pallas_call | solution.py:264
  33.2 3.0 %collective-permute-start.3 = (bf16[100,512]{1,0:T(8,128)(2,1)}, bf16[100,512]{1,0:T(8,128)(2,1)S(1)}, u32[]{:S(2)}, u32[]{:S(2)}) collective-permute-start(bf16[100,512]{1,0:T(8,128)(2,1)} %get-tuple-element.14.refs_0_), channel_id=1, source_target_pairs={{0,16},{16,0},{1,17},{17,1},{2,18},{18,2},{3,19},{19,3},{4,20},{20... | collective-permute-start | bytes 307208 | tf_op jit(solution)/shard_map/ppermute | solution.py:288
  36.2 0.0 collective-permute-done.1.high
  36.2 0.0 copy-start.3
  36.2 0.0 collective-permute-done.low
  36.2 0.0 copy-start.4
  36.3 0.8 %copy-done.3 = bf16[256,1024]{1,0:T(8,128)(2,1)} copy-done((bf16[256,1024]{1,0:T(8,128)(2,1)}, bf16[256,1024]{1,0:T(8,128)(2,1)S(1)}, u32[]{:S(2)}) %copy-start.3) | copy-done | bytes 524312
  37.0 0.2 copy-done.4
  37.2 20.8 %edge_blocks.1.refs_0_ = bf16[100,512]{1,0:T(8,128)(2,1)} custom-call(s32[16]{0:T(128)} %counts.7, bf16[256,1024]{1,0:T(8,128)(2,1)} %copy-done.4, bf16[256,1024]{1,0:T(8,128)(2,1)} %copy-done.3, bf16[1024,1024]{1,0:T(8,128)(2,1)} %bitcast.10, bf16[1,1024]{1,0:T(2,128)(2,1)} %pert.3, f32[1,1024]{1,0:T(1,128)} %bitcast.13, bf16[1024,3072]{1,0:T(8,128)(2,1)} %w_qkv.3, ...), custom_call_target="tpu_custom_call" | custom-call | flops 4831838208 | bytes 10485760 | tf_op jit(solution)/shard_map/edge_blocks/pallas_call | solution.py:293
  58.0 0.0 collective-permute-start.2
  58.0 0.0 collective-permute-done.3.refs_1_
  58.0 0.0 copy-start.2
  58.1 0.6 copy-done.2
  58.7 2.1 %shard_map.103 = (bf16[100,1024]{1,0:T(8,128)(2,1)}, f32[100,1024]{1,0:T(8,128)}, f32[100,1024]{1,0:T(8,128)}) custom-call(s32[16]{0:T(128)} %counts.7, bf16[100,512]{1,0:T(8,128)(2,1)} %get-tuple-element.14.refs_0_, bf16[100,512]{1,0:T(8,128)(2,1)} %copy-done.2, f32[100,1024]{1,0:T(8,128)} %refs_2_.3), custom_call_target="tpu_custom_call" | custom-call | flops 2048000 | bytes 1024000 | tf_op jit(solution)/shard_map/pallas_call | solution.py:236
  60.8 3.2 %collective-permute-done.2.refs_1_ = bf16[100,512]{1,0:T(8,128)(2,1)S(1)} collective-permute-done((bf16[100,512]{1,0:T(8,128)(2,1)}, bf16[100,512]{1,0:T(8,128)(2,1)S(1)}, u32[]{:S(2)}, u32[]{:S(2)}) %collective-permute-start.2) | collective-permute-done | bytes 102432 | tf_op jit(solution)/shard_map/ppermute | solution.py:288
  64.0 0.0 copy-start.1
  64.0 0.6 copy-done.1
  64.6 2.1 %shard_map.104 = (bf16[100,1024]{1,0:T(8,128)(2,1)}, f32[100,1024]{1,0:T(8,128)}, f32[100,1024]{1,0:T(8,128)}) custom-call(s32[16]{0:T(128)} %counts.7, bf16[100,512]{1,0:T(8,128)(2,1)} %edge_blocks.1.refs_0_, bf16[100,512]{1,0:T(8,128)(2,1)} %copy-done.1, f32[100,1024]{1,0:T(8,128)} %refs_2_.3, ...), custom_call_target="tpu_custom_call", output_to_operand_aliasing={{0}: (4, {}), {1}: (5, {}), {2}: (6, {})} | custom-call | flops 2048000 | bytes 1024000 | tf_op jit(solution)/shard_map/pallas_call | solution.py:236
  66.7 2.2 %copy.16 = f32[1,100,1024]{2,0,1:T(1,128)} copy(f32[1,100,1024]{2,1,0:T(8,128)} %bitcast.8) | data formatting | bytes 819200
Async XLA Ops:
  0.6 5.7 %copy-start = (bf16[1024,100]{0,1:T(8,128)(2,1)S(1)}, bf16[1024,100]{0,1:T(8,128)(2,1)}, u32[]{:S(2)}) copy-start(bf16[1024,100]{0,1:T(8,128)(2,1)} %param.13) | copy-start | bytes 614404
  2.0 34.3 %collective-permute-start.1 = (bf16[256,1024]{1,0:T(8,128)(2,1)S(1)}, bf16[256,1024]{1,0:T(8,128)(2,1)S(1)}, u32[]{:S(2)}, u32[]{:S(2)}) collective-permute-start(bf16[256,1024]{1,0:T(8,128)(2,1)S(1)} %get-tuple-element.24), channel_id=1, source_target_pairs={{1,0},{2,1},{3,2},{4,3},{5,4},{6,5},{7,6},{8,7},{9,8},{10,9},{11,1... | collective-permute-start | bytes 1572872 | tf_op jit(solution)/shard_map/ppermute | solution.py:261
  3.3 33.0 %collective-permute-start = (bf16[256,1024]{1,0:T(8,128)(2,1)S(1)}, bf16[256,1024]{1,0:T(8,128)(2,1)S(1)}, u32[]{:S(2)}, u32[]{:S(2)}) collective-permute-start(bf16[256,1024]{1,0:T(8,128)(2,1)S(1)} %get-tuple-element.25), channel_id=1, source_target_pairs={{0,1},{1,2},{2,3},{3,4},{4,5},{5,6},{6,7},{7,8},{8,9},{9,10},{10,1... | collective-permute-start | bytes 1572872 | tf_op jit(solution)/shard_map/ppermute | solution.py:260
  33.2 24.8 %collective-permute-start.3 = (bf16[100,512]{1,0:T(8,128)(2,1)}, bf16[100,512]{1,0:T(8,128)(2,1)S(1)}, u32[]{:S(2)}, u32[]{:S(2)}) collective-permute-start(bf16[100,512]{1,0:T(8,128)(2,1)} %get-tuple-element.14.refs_0_), channel_id=1, source_target_pairs={{0,16},{16,0},{1,17},{17,1},{2,18},{18,2},{3,19},{19,3},{4,20},{20... | collective-permute-start | bytes 307208 | tf_op jit(solution)/shard_map/ppermute | solution.py:288
  36.2 0.8 %copy-start.3 = (bf16[256,1024]{1,0:T(8,128)(2,1)}, bf16[256,1024]{1,0:T(8,128)(2,1)S(1)}, u32[]{:S(2)}) copy-start(bf16[256,1024]{1,0:T(8,128)(2,1)S(1)} %collective-permute-done.1.high) | copy-start | bytes 1572868
  36.2 1.0 %copy-start.4 = (bf16[256,1024]{1,0:T(8,128)(2,1)}, bf16[256,1024]{1,0:T(8,128)(2,1)S(1)}, u32[]{:S(2)}) copy-start(bf16[256,1024]{1,0:T(8,128)(2,1)S(1)} %collective-permute-done.low) | copy-start | bytes 1572868
  58.0 5.9 %collective-permute-start.2 = (bf16[100,512]{1,0:T(8,128)(2,1)}, bf16[100,512]{1,0:T(8,128)(2,1)S(1)}, u32[]{:S(2)}, u32[]{:S(2)}) collective-permute-start(bf16[100,512]{1,0:T(8,128)(2,1)} %edge_blocks.1.refs_0_), channel_id=1, source_target_pairs={{0,16},{16,0},{1,17},{17,1},{2,18},{18,2},{3,19},{19,3},{4,20},{20... | collective-permute-start | bytes 307208 | tf_op jit(solution)/shard_map/ppermute | solution.py:288
  58.0 0.6 copy-start.2
  64.0 0.6 copy-start.1

commit v2 on v1

--- a/solution.py
+++ b/solution.py
@@ -72,40 +72,78 @@
 
 def decode(x, attended, w_proj, w_fields):
     updated = (x.astype(F32) + jnp.dot(attended, w_proj, preferred_element_type=F32)).astype(BF16)
-    return lax.dot_general(w_fields, updated, (((0,), (1,)), ((), ())), preferred_element_type=F32)
+    return lax.dot_general(w_fields, updated, (((1,), (1,)), ((), ())), preferred_element_type=F32)
 
 
 def cols(c):
     return slice(c * LANES, (c + 1) * LANES)
 
 
-def inner_kernel(counts, x_ref, pert, gain, w_qkv, w_proj, w_fields, out, q_edge, kv, normed, q_in, att):
-    rows, width = x_ref.shape
+def copies(pairs, sems, base=0):
+    return [pltpu.make_async_copy(src, dst, sems.at[base + i]) for i, (src, dst) in enumerate(pairs)]
+
+
+STEP = 256
+
+
+def chunk(j, offset=0):
+    return pl.ds(pl.multiple_of(offset + j * STEP, STEP), STEP)
+
+
+def inner_kernel(
+    counts, pert, gain, w_fields, x_hbm, w_qkv_hbm, w_proj_hbm,
+    out, q_edge_hbm, kv_hbm,
+    x, w_qkv, w_proj, normed, q_in, q_edge, kv, att, x_sem, w_sem, p_sem, q_sem, kv_sem,
+):
+    rows, width = x.shape
     half = HALF_WINDOW
+    chunks = width // STEP
     own = counts[lax.axis_index("node")]
+
+    def part(b):
+        return slice(b * half, (b + 1) * half)
+
+    x_in = copies([(x_hbm.at[part(b), :], x.at[part(b), :]) for b in range(rows // half)], x_sem)
+    for c in x_in:
+        c.start()
+
+    def weight(j):
+        return pltpu.make_async_copy(w_qkv_hbm.at[:, chunk(j)], w_qkv.at[:, chunk(j)], w_sem.at[j])
+
+    for j in range(3 * chunks):
+        weight(j).start()
+    proj_in = pltpu.make_async_copy(w_proj_hbm, w_proj, p_sem)
+    proj_in.start()
     scale = channel_scale(gain, pert)
     for b in range(rows // half):
-        normed[b * half : (b + 1) * half, :] = normalize(x_ref[b * half : (b + 1) * half, :], scale)
-    step = 256
+        x_in[b].wait()
+        normed[part(b), :] = normalize(x[part(b), :], scale)
 
     def project(j, _):
-        at = pl.ds(pl.multiple_of(j * step, step), step)
-        q = jnp.dot(normed[...], w_qkv[:, at], preferred_element_type=F32).astype(BF16)
+        weight(j).wait()
+        q = jnp.dot(normed[...], w_qkv[:, chunk(j)], preferred_element_type=F32).astype(BF16)
         q = q * jnp.asarray((width // HEADS) ** -0.5, BF16)
-        q_edge[:half, at] = q[:half]
-        q_in[:, at] = q[half : rows - half]
-        q_edge[half:, at] = q[rows - half :]
+        q_edge[:half, chunk(j)] = q[:half]
+        q_in[:, chunk(j)] = q[half : rows - half]
+        q_edge[half:, chunk(j)] = q[rows - half :]
         return 0
 
-    lax.fori_loop(0, width // step, project, 0)
+    lax.fori_loop(0, chunks, project, 0)
+    q_out = pltpu.make_async_copy(q_edge, q_edge_hbm, q_sem)
+    q_out.start()
+
+    def kv_out(j):
+        return pltpu.make_async_copy(kv.at[:, chunk(j)], kv_hbm.at[:, chunk(j)], kv_sem.at[j])
 
     def project_kv(j, _):
-        at = pl.ds(pl.multiple_of(j * step, step), step)
-        src = pl.ds(pl.multiple_of(width + j * step, step), step)
-        kv[:, at] = jnp.dot(normed[...], w_qkv[:, src], preferred_element_type=F32).astype(BF16)
+        weight(chunks + j).wait()
+        w = w_qkv[:, chunk(j, width)]
+        kv[:, chunk(j)] = jnp.dot(normed[...], w, preferred_element_type=F32).astype(BF16)
+        kv_out(j).start()
         return 0
 
-    lax.fori_loop(0, 2 * width // step, project_kv, 0)
+    lax.fori_loop(0, 2 * chunks, project_kv, 0)
+    proj_in.wait()
 
     def block(b, _):
         start = pl.multiple_of(b * half, half)
@@ -123,18 +161,42 @@
             store,
             width // LANES,
         )
-        x = x_ref[pl.ds(pl.multiple_of(start + half, half), half), :]
-        fields = decode(x, att[...], w_proj[...], w_fields[...])
+        rest = x[pl.ds(pl.multiple_of(start + half, half), half), :]
+        fields = decode(rest, att[...], w_proj[...], w_fields[...])
         live = iota(fields.shape, 1) + start + half < own
         out[:, pl.ds(start, half)] = jnp.where(live, fields, 0.0).astype(BF16)
         return 0
 
     lax.fori_loop(0, rows // half - 2, block, 0)
-
-
-def edge_kernel(counts, low, high, x_ref, pert, gain, w_qkv, w_proj, w_fields, q_edge, kv, out, normed, halo, att):
-    rows, width = x_ref.shape
+    q_out.wait()
+    for j in range(2 * chunks):
+        kv_out(j).wait()
+
+
+def edge_kernel(
+    counts, pert, gain, w_fields, low, high, x_hbm, w_qkv_hbm, w_proj_hbm, q_edge_hbm, kv_hbm,
+    out,
+    x, w_kv, w_proj, normed, halo, q_edge, kv, att, x_sem, w_sem, p_sem, q_sem, kv_sem,
+):
+    rows, width = kv_hbm.shape[0], w_proj.shape[0]
     half = HALF_WINDOW
+    chunks = width // STEP
+    tail = rows - 2 * half
+
+    def weight(j):
+        return pltpu.make_async_copy(w_qkv_hbm.at[:, chunk(j, width)], w_kv.at[:, chunk(j)], w_sem.at[j])
+
+    for j in range(2 * chunks):
+        weight(j).start()
+    late = [
+        pltpu.make_async_copy(q_edge_hbm, q_edge, q_sem),
+        pltpu.make_async_copy(kv_hbm, kv, kv_sem),
+        pltpu.make_async_copy(w_proj_hbm, w_proj, p_sem),
+    ] + copies(
+        [(x_hbm.at[:half, :], x.at[:half, :]), (x_hbm.at[rows - half :, :], x.at[half:, :])], x_sem
+    )
+    for c in late:
+        c.start()
     place = lax.axis_index("node")
     shards = counts.shape[0]
     own = counts[place]
@@ -143,15 +205,15 @@
     scale = channel_scale(gain, pert)
     normed[:half, :] = normalize(low[...], scale)
     normed[half:, :] = normalize(high[...], scale)
-    step = 256
 
     def project_kv(j, _):
-        at = pl.ds(pl.multiple_of(j * step, step), step)
-        src = pl.ds(pl.multiple_of(width + j * step, step), step)
-        halo[:, at] = jnp.dot(normed[...], w_qkv[:, src], preferred_element_type=F32).astype(BF16)
+        weight(j).wait()
+        halo[:, chunk(j)] = jnp.dot(normed[...], w_kv[:, chunk(j)], preferred_element_type=F32).astype(BF16)
         return 0
 
-    lax.fori_loop(0, 2 * width // step, project_kv, 0)
+    lax.fori_loop(0, 2 * chunks, project_kv, 0)
+    for c in late:
+        c.wait()
 
     def store(c, value):
         att[:, cols(c)] = value
@@ -160,10 +222,7 @@
         return slice(width + c * LANES, width + (c + 1) * LANES)
 
     flags_low = jnp.concatenate([dead_flags(half, low_live - (rows - half)), dead_flags(2 * half, own)], axis=0)
-    flags_high = jnp.concatenate(
-        [dead_flags(2 * half, own - (rows - 2 * half)), dead_flags(half, high_live)], axis=0
-    )
-    tail = rows - 2 * half
+    flags_high = jnp.concatenate([dead_flags(2 * half, own - tail), dead_flags(half, high_live)], axis=0)
     for side in range(2):
         if side == 0:
             q = lambda c: q_edge[:half, cols(c)]
@@ -176,7 +235,8 @@
             v = lambda c: jnp.concatenate([kv[tail:, vcols(c)], halo[half:, vcols(c)]], axis=0)
             flags, start = flags_high, rows - half
         attend_block(q, k, v, flags, store, width // LANES)
-        fields = decode(x_ref[start : start + half, :], att[...], w_proj[...], w_fields[...])
+        rest = x[side * half : (side + 1) * half, :]
+        fields = decode(rest, att[...], w_proj[...], w_fields[...])
         live = iota(fields.shape, 1) + start < own
         out[:, side * half : (side + 1) * half] = jnp.where(live, fields, 0.0).astype(BF16)
 
@@ -219,7 +279,8 @@
     start = place_of(pl.program_id(0)) * width
     live = iota(mine.shape, 1) + start < own
     pred[...] = mine[...]
-    score[...], deriv[...] = score_values(mine[...], [r[...] for r in rest], truth[...], live)
+    score[...], d = score_values(mine[...], [r[...] for r in rest], truth[...], live)
+    deriv[...] = d[:, None, :]
 
 
 def score_call(counts, mine, others, truth, carried, place_of, blocks):
@@ -227,17 +288,19 @@
     fields, nodes = truth.shape
     part = pl.BlockSpec((fields, half), lambda i: (0, i))
     whole = pl.BlockSpec((fields, half), lambda i: (0, place_of(i)))
+    flat = pl.BlockSpec((fields, 1, half), lambda i: (0, 0, place_of(i)))
     shapes = [
         jax.ShapeDtypeStruct((fields, nodes), BF16),
         jax.ShapeDtypeStruct((fields, nodes), F32),
-        jax.ShapeDtypeStruct((fields, nodes), F32),
+        jax.ShapeDtypeStruct((fields, 1, nodes), F32),
     ]
     count = len(others)
     return pl.pallas_call(
         functools.partial(score_kernel, count, len(carried), place_of),
         grid=(blocks,),
         in_specs=[SMEM] + [part] * (1 + count) + [whole] + [ANY] * len(carried),
-        out_specs=[whole] * 3,
+        out_specs=[whole, whole, flat],
+        compiler_params=pltpu.CompilerParams(vmem_limit_bytes=8 << 20),
         out_shape=shapes,
         input_output_aliases={3 + count + i: i for i in range(len(carried))},
         cost_estimate=pl.CostEstimate(
@@ -250,9 +313,11 @@
     _, rows, width = hidden.shape
     fields = w_fields.shape[1]
     half = HALF_WINDOW
+    chunks = width // STEP
     blocks = rows // half
     x = hidden[0]
     gain = gain.reshape(1, width)
+    w_fields = w_fields.T
     shards = lax.axis_size("node")
     members = lax.axis_size("ens")
     up = [(i, i + 1) for i in range(shards - 1)]
@@ -261,10 +326,11 @@
     high = lax.ppermute(x[:half], "node", down)
 
     inner = rows - 2 * half
+    dma = pltpu.SemaphoreType.DMA
     pred_in, q_edge, kv = pl.pallas_call(
         inner_kernel,
-        in_specs=[SMEM, VMEM, VMEM, VMEM, VMEM, VMEM, VMEM],
-        out_specs=[VMEM, VMEM, VMEM],
+        in_specs=[SMEM, VMEM, VMEM, VMEM, ANY, ANY, ANY],
+        out_specs=[VMEM, ANY, ANY],
         out_shape=[
             jax.ShapeDtypeStruct((fields, inner), BF16),
             jax.ShapeDtypeStruct((2 * half, width), BF16),
@@ -272,16 +338,27 @@
         ],
         scratch_shapes=[
             pltpu.VMEM((rows, width), BF16),
+            pltpu.VMEM((width, 3 * width), BF16),
+            pltpu.VMEM((width, width), BF16),
+            pltpu.VMEM((rows, width), BF16),
             pltpu.VMEM((inner, width), BF16),
+            pltpu.VMEM((2 * half, width), BF16),
+            pltpu.VMEM((rows, 2 * width), BF16),
             pltpu.VMEM((half, width), BF16),
+            dma((blocks,)),
+            dma((3 * chunks,)),
+            dma,
+            dma,
+            dma((2 * chunks,)),
         ],
+        compiler_params=pltpu.CompilerParams(vmem_limit_bytes=48 << 20),
         cost_estimate=pl.CostEstimate(
             flops=2 * rows * width * 3 * width + 2 * inner * width * width + 12 * inner * width * half,
             bytes_accessed=10 * width * width,
             transcendentals=inner * HEADS * 3 * half,
         ),
         name="inner_blocks",
-    )(counts, x, pert, gain, w_qkv, w_proj, w_fields)
+    )(counts, pert, gain, w_fields, x, w_qkv, w_proj)
 
     def exchange(part):
         return [
@@ -292,27 +369,38 @@
     others_in = exchange(pred_in)
     pred_edge = pl.pallas_call(
         edge_kernel,
-        in_specs=[SMEM] + [VMEM] * 10,
+        in_specs=[SMEM] + [VMEM] * 5 + [ANY] * 5,
         out_specs=VMEM,
         out_shape=jax.ShapeDtypeStruct((fields, 2 * half), BF16),
         scratch_shapes=[
             pltpu.VMEM((2 * half, width), BF16),
+            pltpu.VMEM((width, 2 * width), BF16),
+            pltpu.VMEM((width, width), BF16),
+            pltpu.VMEM((2 * half, width), BF16),
             pltpu.VMEM((2 * half, 2 * width), BF16),
+            pltpu.VMEM((2 * half, width), BF16),
+            pltpu.VMEM((rows, 2 * width), BF16),
             pltpu.VMEM((half, width), BF16),
+            dma((2,)),
+            dma((2 * chunks,)),
+            dma,
+            dma,
+            dma,
         ],
+        compiler_params=pltpu.CompilerParams(vmem_limit_bytes=48 << 20),
         cost_estimate=pl.CostEstimate(
             flops=2 * 2 * half * width * 3 * width + 12 * 2 * half * width * half,
             bytes_accessed=10 * width * width,
             transcendentals=2 * half * HEADS * 3 * half,
         ),
         name="edge_blocks",
-    )(counts, low, high, x, pert, gain, w_qkv, w_proj, w_fields, q_edge, kv)
+    )(counts, pert, gain, w_fields, low, high, x, w_qkv, w_proj, q_edge, kv)
     others_edge = exchange(pred_edge)
     partial = score_call(counts, pred_in, others_in, truth, [], lambda i: i + 1, blocks - 2)
     pred, score, deriv = score_call(
         counts, pred_edge, others_edge, truth, partial, lambda i: i * (blocks - 1), 2
     )
-    return pred[None], score, deriv[None]
+    return pred[None], score, deriv.transpose(1, 0, 2)
 
 
 def solution(mesh):

time: 69.2 us -> 56.4 us (0.82)
  Pallas kernels: 51 us -> 40 us
  local copies, waits for them, and re-layouts: 6.62 us -> 3.95 us
  waiting for transfers between devices: 3.21 us -> 3.94 us
    pallas_call x2, Pallas kernels: 46.9 us -> 36.6 us  [the longest x1 21.3 us: on_device(): pl.pallas_call(inner_kernel, in_specs=[SMEM, VMEM, VMEM, VMEM, ANY, ANY,...]
    unnamed x12 -> x14, local copies, waits for them, and re-layouts: 5.31 us -> 2.54 us
    pallas_call x2, Pallas kernels: 4.17 us -> 3.39 us  [score_call(): pl.pallas_call(functools.partial(score_kernel, count, len(carried), place...]
    ppermute x2, waiting for transfers between devices: 3.2 us -> 3.93 us  [exchange(): lax.ppermute(part, 'ens', [(i, (i + s) % members) for i in range(members)])]
  transfers between devices with their start and end apart: 4 -> 4, of which waited for: 1 -> 1; matrix products, arithmetic and copies ran while one was open for 1% -> 0% of each run, Pallas kernels for 71% -> 68%
where the time goes in v2:
time: 56.4 us; the launch traced here: 56.2 us
  Pallas kernels  40 us (71%)
  starting transfers between devices  7.52 us (13%)
  local copies, waits for them, and re-layouts  3.95 us (7%)
  waiting for transfers between devices  3.94 us (7%)
  between operations  0.75 us (1%)
    pallas_call x1, Pallas kernels, on_device(): pl.pallas_call(inner_kernel, in_specs=[SMEM, VMEM, VMEM, VMEM, ANY, ANY,...  21.3 us
    pallas_call x1, Pallas kernels, on_device(): pl.pallas_call(edge_kernel, in_specs=[SMEM] + [VMEM] * 5 + [ANY] * 5, out...  15.3 us
    ppermute x2, waiting for transfers between devices, exchange(): lax.ppermute(part, 'ens', [(i, (i + s) % members) for i in range(members)])  3.93 us
    pallas_call x2, Pallas kernels, score_call(): pl.pallas_call(functools.partial(score_kernel, count, len(carried), place...  3.39 us
    ppermute x2, starting transfers between devices, exchange(): lax.ppermute(part, 'ens', [(i, (i + s) % members) for i in range(members)])  3.17 us
    ppermute x1, starting transfers between devices, on_device(): low = lax.ppermute(x[rows - half:], 'node', up)  3.06 us
    unnamed x14, local copies, waits for them, and re-layouts  2.54 us
    slice x1, local copies, waits for them, and re-layouts, on_device(): high = lax.ppermute(x[:half], 'node', down)  1.41 us
  transfers between devices with their start and end apart: 4, of which 1 were waited for; matrix products, arithmetic and copies ran while one was open for 0% of the time, Pallas kernels for 68%

profile of v2, /device:TPU:0, one launch (start us, length us, event | category | flops | bytes accessed | tf_op | source)
XLA Modules:
  0.0 56.2 jit_solution(5871670175309682457)
XLA Ops:
  0.6 0.0 copy-start.1
  0.6 0.0 copy-start.2
  0.7 0.0 copy-start.5
  0.7 0.0 copy-start.6
  0.7 1.4 %slice_bitcast_fusion = (bf16[256,1024]{1,0:T(8,128)(2,1)S(1)}, bf16[256,1024]{1,0:T(8,128)(2,1)S(1)}) fusion(bf16[1,1024,1024]{2,1,0:T(8,128)(2,1)} %param.8), kind=kLoop, calls=%fused_computation | loop fusion | bytes 2097152 | tf_op jit(solution)/shard_map/slice | solution.py:326
  2.1 1.3 %collective-permute-start.1 = (bf16[256,1024]{1,0:T(8,128)(2,1)S(1)}, bf16[256,1024]{1,0:T(8,128)(2,1)S(1)}, u32[]{:S(2)}, u32[]{:S(2)}) collective-permute-start(bf16[256,1024]{1,0:T(8,128)(2,1)S(1)} %get-tuple-element.21), channel_id=1, source_target_pairs={{1,0},{2,1},{3,2},{4,3},{5,4},{6,5},{7,6},{8,7},{9,8},{10,9},{11,1... | collective-permute-start | bytes 1572872 | tf_op jit(solution)/shard_map/ppermute | solution.py:326
  3.4 3.1 %collective-permute-start = (bf16[256,1024]{1,0:T(8,128)(2,1)S(1)}, bf16[256,1024]{1,0:T(8,128)(2,1)S(1)}, u32[]{:S(2)}, u32[]{:S(2)}) collective-permute-start(bf16[256,1024]{1,0:T(8,128)(2,1)S(1)} %get-tuple-element.22), channel_id=1, source_target_pairs={{0,1},{1,2},{2,3},{3,4},{4,5},{5,6},{6,7},{7,8},{8,9},{9,10},{10,1... | collective-permute-start | bytes 1572872 | tf_op jit(solution)/shard_map/ppermute | solution.py:325
  6.5 0.0 copy-done.1
  6.5 0.0 copy-done.2
  6.5 0.0 copy-done.5
  6.5 0.0 copy-done.6
  6.5 0.0 copy-start.3
  6.5 1.6 %copy-done.3 = bf16[1024,1024]{1,0:T(8,128)(2,1)S(1)} copy-done((bf16[1024,1024]{1,0:T(8,128)(2,1)S(1)}, bf16[1024,1024]{1,0:T(8,128)(2,1)}, u32[]{:S(2)}) %copy-start.3) | copy-done | bytes 2097176
  8.1 0.0 copy-start.4
  8.1 0.9 %copy-done.4 = bf16[1024,100]{0,1:T(8,128)(2,1)S(1)} copy-done((bf16[1024,100]{0,1:T(8,128)(2,1)S(1)}, bf16[1024,100]{0,1:T(8,128)(2,1)}, u32[]{:S(2)}) %copy-start.4) | copy-done | bytes 204824
  9.0 21.3 %inner_blocks.1 = (bf16[100,512]{1,0:T(8,128)(2,1)S(1)}, bf16[512,1024]{1,0:T(8,128)(2,1)S(1)}, bf16[1024,2048]{1,0:T(8,128)(2,1)}) custom-call(s32[16]{0:T(128)S(1)} %copy-done.2, bf16[1,1024]{1,0:T(2,128)(2,1)S(1)} %copy-done.5, f32[1,1024]{1,0:T(1,128)S(1)} %bitcast.13, bf16[100,1024]{1,0:T(8,128)(2,1)S(1)} %bitcast.11, bf16[1024,1024]{1,0:T(8,128)(2,1)S(1)} %bitcast.9, ...), custom_call_target="tpu_custom_call" | custom-call | flops 9126805504 | bytes 10485760 | tf_op jit(solution)/shard_map/inner_blocks/pallas_call | solution.py:330
  30.4 3.1 %collective-permute-start.3 = (bf16[100,512]{1,0:T(8,128)(2,1)S(1)}, bf16[100,512]{1,0:T(8,128)(2,1)S(1)}, u32[]{:S(2)}, u32[]{:S(2)}) collective-permute-start(bf16[100,512]{1,0:T(8,128)(2,1)S(1)} %get-tuple-element.14.refs_0_), channel_id=1, source_target_pairs={{0,16},{16,0},{1,17},{17,1},{2,18},{18,2},{3,19},{19,3},{4,20},{20... | collective-permute-start | bytes 307208 | tf_op jit(solution)/shard_map/ppermute | solution.py:365
  33.4 0.0 collective-permute-done.1.high
  33.4 0.0 collective-permute-done.low
  33.4 0.0 copy-start
  33.4 15.3 %edge_blocks.1.refs_0_ = bf16[100,512]{1,0:T(8,128)(2,1)S(1)} custom-call(s32[16]{0:T(128)S(1)} %copy-done.2, bf16[1,1024]{1,0:T(2,128)(2,1)S(1)} %copy-done.5, f32[1,1024]{1,0:T(1,128)S(1)} %bitcast.14, bf16[100,1024]{1,0:T(8,128)(2,1)S(1)} %bitcast.12, bf16[256,1024]{1,0:T(8,128)(2,1)S(1)} %collective-permute-done.low, ...), custom_call_target="tpu_custom_call" | custom-call | flops 4831838208 | bytes 10485760 | tf_op jit(solution)/shard_map/edge_blocks/pallas_call | solution.py:370
  48.7 0.1 collective-permute-start.2
  48.8 0.0 collective-permute-done.3.refs_1_
  48.8 0.0 copy-done
  48.9 1.7 %shard_map.103 = (bf16[100,1024]{1,0:T(8,128)(2,1)}, f32[100,1024]{1,0:T(8,128)}, f32[100,1,1024]{2,1,0:T(1,128)}) custom-call(s32[16]{0:T(128)S(1)} %copy-done.2, bf16[100,512]{1,0:T(8,128)(2,1)S(1)} %get-tuple-element.14.refs_0_, bf16[100,512]{1,0:T(8,128)(2,1)S(1)} %collective-permute-done.3.refs_1_, f32[100,1024]{1,0:T(8,128)S(1)} %copy-done), custom_call_target="tpu_custom_call" | custom-call | flops 2048000 | bytes 1024000 | tf_op jit(solution)/shard_map/pallas_call | solution.py:298
  50.6 3.9 %collective-permute-done.2.refs_1_ = bf16[100,512]{1,0:T(8,128)(2,1)S(1)} collective-permute-done((bf16[100,512]{1,0:T(8,128)(2,1)S(1)}, bf16[100,512]{1,0:T(8,128)(2,1)S(1)}, u32[]{:S(2)}, u32[]{:S(2)}) %collective-permute-start.2) | collective-permute-done | bytes 102432 | tf_op jit(solution)/shard_map/ppermute | solution.py:365
  54.5 1.7 %shard_map.104 = (bf16[100,1024]{1,0:T(8,128)(2,1)}, f32[100,1024]{1,0:T(8,128)}, f32[100,1,1024]{2,1,0:T(1,128)}) custom-call(s32[16]{0:T(128)S(1)} %copy-done.2, bf16[100,512]{1,0:T(8,128)(2,1)S(1)} %edge_blocks.1.refs_0_, bf16[100,512]{1,0:T(8,128)(2,1)S(1)} %collective-permute-done.2.refs_1_, ...), custom_call_target="tpu_custom_call", output_to_operand_aliasing={{0}: (4, {}), {1}: (5, {}), {2}: (6, {})} | custom-call | flops 2048000 | bytes 1024000 | tf_op jit(solution)/shard_map/pallas_call | solution.py:298
Async XLA Ops:
  0.6 5.8 %copy-start.1 = (bf16[1,1024,1024]{2,1,0:T(8,128)(2,1)S(1)}, bf16[1,1024,1024]{2,1,0:T(8,128)(2,1)}, u32[]{:S(2)}) copy-start(bf16[1,1024,1024]{2,1,0:T(8,128)(2,1)} %param.8) | copy-start | bytes 6291460
  0.6 5.8 %copy-start.2 = (s32[16]{0:T(128)S(1)}, s32[16]{0:T(128)}, u32[]{:S(2)}) copy-start(s32[16]{0:T(128)} %counts.7) | copy-start | bytes 196
  0.7 5.8 %copy-start.5 = (bf16[1,1024]{1,0:T(2,128)(2,1)S(1)}, bf16[1,1024]{1,0:T(2,128)(2,1)}, u32[]{:S(2)}) copy-start(bf16[1,1024]{1,0:T(2,128)(2,1)} %pert.3) | copy-start | bytes 6148
  0.7 5.8 %copy-start.6 = (f32[1024]{0:T(1024)S(1)}, f32[1024]{0:T(1024)}, u32[]{:S(2)}) copy-start(f32[1024]{0:T(1024)} %param.10) | copy-start | bytes 12292
  2.1 31.3 %collective-permute-start.1 = (bf16[256,1024]{1,0:T(8,128)(2,1)S(1)}, bf16[256,1024]{1,0:T(8,128)(2,1)S(1)}, u32[]{:S(2)}, u32[]{:S(2)}) collective-permute-start(bf16[256,1024]{1,0:T(8,128)(2,1)S(1)} %get-tuple-element.21), channel_id=1, source_target_pairs={{1,0},{2,1},{3,2},{4,3},{5,4},{6,5},{7,6},{8,7},{9,8},{10,9},{11,1... | collective-permute-start | bytes 1572872 | tf_op jit(solution)/shard_map/ppermute | solution.py:326
  3.4 30.0 %collective-permute-start = (bf16[256,1024]{1,0:T(8,128)(2,1)S(1)}, bf16[256,1024]{1,0:T(8,128)(2,1)S(1)}, u32[]{:S(2)}, u32[]{:S(2)}) collective-permute-start(bf16[256,1024]{1,0:T(8,128)(2,1)S(1)} %get-tuple-element.22), channel_id=1, source_target_pairs={{0,1},{1,2},{2,3},{3,4},{4,5},{5,6},{6,7},{7,8},{8,9},{9,10},{10,1... | collective-permute-start | bytes 1572872 | tf_op jit(solution)/shard_map/ppermute | solution.py:325
  6.5 1.6 %copy-start.3 = (bf16[1024,1024]{1,0:T(8,128)(2,1)S(1)}, bf16[1024,1024]{1,0:T(8,128)(2,1)}, u32[]{:S(2)}) copy-start(bf16[1024,1024]{1,0:T(8,128)(2,1)} %w_proj_hbm.3) | copy-start | bytes 6291460
  8.1 0.9 %copy-start.4 = (bf16[1024,100]{0,1:T(8,128)(2,1)S(1)}, bf16[1024,100]{0,1:T(8,128)(2,1)}, u32[]{:S(2)}) copy-start(bf16[1024,100]{0,1:T(8,128)(2,1)} %param.13) | copy-start | bytes 614404
  30.4 18.5 %collective-permute-start.3 = (bf16[100,512]{1,0:T(8,128)(2,1)S(1)}, bf16[100,512]{1,0:T(8,128)(2,1)S(1)}, u32[]{:S(2)}, u32[]{:S(2)}) collective-permute-start(bf16[100,512]{1,0:T(8,128)(2,1)S(1)} %get-tuple-element.14.refs_0_), channel_id=1, source_target_pairs={{0,16},{16,0},{1,17},{17,1},{2,18},{18,2},{3,19},{19,3},{4,20},{20... | collective-permute-start | bytes 307208 | tf_op jit(solution)/shard_map/ppermute | solution.py:365
  33.4 15.4 %copy-start = (f32[100,1024]{1,0:T(8,128)S(1)}, f32[100,1024]{1,0:T(8,128)}, u32[]{:S(2)}) copy-start(f32[100,1024]{1,0:T(8,128)} %refs_2_.3) | copy-start | bytes 1228804
  48.7 5.7 %collective-permute-start.2 = (bf16[100,512]{1,0:T(8,128)(2,1)S(1)}, bf16[100,512]{1,0:T(8,128)(2,1)S(1)}, u32[]{:S(2)}, u32[]{:S(2)}) collective-permute-start(bf16[100,512]{1,0:T(8,128)(2,1)S(1)} %edge_blocks.1.refs_0_), channel_id=1, source_target_pairs={{0,16},{16,0},{1,17},{17,1},{2,18},{18,2},{3,19},{19,3},{4,20},{20... | collective-permute-start | bytes 307208 | tf_op jit(solution)/shard_map/ppermute | solution.py:365

commit v3 on v1

v3 whole, which is shorter than its diff:
```python
import functools

import jax
import jax.numpy as jnp
from jax import lax
from jax.experimental import pallas as pl
from jax.experimental.pallas import tpu as pltpu
from jax.sharding import PartitionSpec as P

HEADS = 16
HALF_WINDOW = 256
LANES = 128

smooth_sq = 0.01
alpha_fair = 0.95
NEG = -1e30
LOG2E = 1.4426950408889634
KERNEL_VMEM = 32 << 20

F32 = jnp.float32
BF16 = jnp.bfloat16
VMEM = pl.BlockSpec(memory_space=pltpu.VMEM)
SMEM = pl.BlockSpec(memory_space=pltpu.SMEM)
ANY = pl.BlockSpec(memory_space=pl.ANY)


def iota(shape, dim):
    return lax.broadcasted_iota(jnp.int32, shape, dim)


def normalize(x, scale):
    x32 = x.astype(F32)
    mean = jnp.mean(x32, axis=-1, keepdims=True)
    centred = x32 - mean
    var = jnp.mean(centred * centred, axis=-1, keepdims=True)
    return (centred * lax.rsqrt(var + 1e-05) * scale).astype(BF16)


def channel_scale(gain_ref, pert_ref):
    return gain_ref[...] * (1.0 + pert_ref[...].astype(F32))


def dead_flags(rows, live):
    return jnp.where((iota((rows, LANES), 0) >= live) & (iota((rows, LANES), 1) == 0), 1.0, 0.0).astype(BF16)


def attend_block(query, keys, values, flags, store, pairs):
    half = HALF_WINDOW
    row = iota((2 * half, half), 0) % half
    col = iota((2 * half, half), 1)
    near = jnp.where(col >= row, 0.0, NEG)
    far = jnp.where(col < row, 0.0, NEG)
    bias = jnp.where(iota((2 * half, LANES), 1) == 0, NEG, 0.0).astype(BF16)
    ones = jnp.ones((3 * half, LANES), BF16)
    lane = iota((half, LANES), 1)
    first = lane < LANES // 2
    for c in range(pairs):
        q = query(c)
        zero = jnp.zeros_like(q)
        both = jnp.concatenate([jnp.where(first, q, zero), jnp.where(first, zero, q)], axis=0)
        both = jnp.concatenate([both, bias], axis=1)
        k = jnp.concatenate([keys(c), flags], axis=1)
        s = lax.dot_general(both, k, (((1,), (1,)), ((), ())), preferred_element_type=F32)
        s = jnp.concatenate([s[:, :half] + near, s[:, half : 2 * half], s[:, 2 * half :] + far], axis=1)
        top = jnp.max(s, axis=1, keepdims=True)
        p = jnp.exp2((s - top) * LOG2E).astype(BF16)
        v = jnp.concatenate([values(c), ones], axis=1)
        o = jnp.dot(p, v, preferred_element_type=F32)
        num = jnp.where(first, o[:half, :LANES], o[half:, :LANES])
        den = jnp.where(first, o[:half, LANES:], o[half:, LANES:])
        store(c, (num / den).astype(BF16))


def decode(x, attended, w_proj, w_fields):
    updated = (x.astype(F32) + jnp.dot(attended, w_proj, preferred_element_type=F32)).astype(BF16)
    return lax.dot_general(w_fields, updated, (((1,), (1,)), ((), ())), preferred_element_type=F32)


def cols(c):
    return slice(c * LANES, (c + 1) * LANES)


def attend_side(q, kv, flags, att, q_at, k_at, width):
    def store(c, value):
        att[:, cols(c)] = value

    attend_block(
        lambda c: q[q_at, cols(c)],
        lambda c: kv[k_at, cols(c)],
        lambda c: kv[k_at, slice(width + c * LANES, width + (c + 1) * LANES)],
        flags,
        store,
        width // LANES,
    )


def inner_kernel(
    counts, x, pert_hbm, gain_hbm, w_fields_hbm, w_qkv_hbm, w_proj_hbm, out, q_edge, kv,
    pert, gain, w_fields, w_qkv, w_proj, normed, q_in, att, w_sem, s_sem,
):
    rows, width = x.shape
    scale_in = [
        pltpu.make_async_copy(pert_hbm, pert, s_sem.at[0]),
        pltpu.make_async_copy(gain_hbm, gain, s_sem.at[1]),
    ]
    w_in = [
        pltpu.make_async_copy(
            w_qkv_hbm.at[:, n * width : (n + 1) * width], w_qkv.at[:, n * width : (n + 1) * width], w_sem.at[n]
        )
        for n in range(3)
    ]
    late = [
        pltpu.make_async_copy(w_fields_hbm, w_fields, s_sem.at[2]),
        pltpu.make_async_copy(w_proj_hbm, w_proj, s_sem.at[3]),
    ]
    for c in scale_in + w_in + late:
        c.start()
    half = HALF_WINDOW
    blocks = rows // half
    own = counts[lax.axis_index("node")]
    head_scale = jnp.asarray((width // HEADS) ** -0.5, BF16)

    def part(b):
        return slice(b * half, (b + 1) * half)

    for c in scale_in:
        c.wait()
    scale = channel_scale(gain, pert)
    normed[part(0), :] = normalize(x[part(0), :], scale)
    for b in range(blocks):
        if b + 1 < blocks:
            normed[part(b + 1), :] = normalize(x[part(b + 1), :], scale)
        here = normed[part(b), :]
        for n in range(3):
            if b == 0:
                w_in[n].wait()
            res = jnp.dot(here, w_qkv[:, n * width : (n + 1) * width], preferred_element_type=F32).astype(BF16)
            if n > 0:
                kv[part(b), (n - 1) * width : n * width] = res
            elif b == 0:
                q_edge[:half, :] = res * head_scale
            elif b == blocks - 1:
                q_edge[half:, :] = res * head_scale
            else:
                q_in[part(b - 1), :] = res * head_scale

    for c in late:
        c.wait()

    def block(b, _):
        start = pl.multiple_of(b * half, half)
        attend_side(
            q_in, kv, dead_flags(3 * half, own - start), att, pl.ds(start, half), pl.ds(start, 3 * half), width
        )
        rest = x[pl.ds(pl.multiple_of(start + half, half), half), :]
        fields = decode(rest, att[...], w_proj[...], w_fields[...])
        live = iota(fields.shape, 1) + start + half < own
        out[:, pl.ds(start, half)] = jnp.where(live, fields, 0.0).astype(BF16)
        return 0

    lax.fori_loop(0, blocks - 2, block, 0)


def edge_kernel(
    counts, pert, gain, w_fields, first, second, x, w_qkv, w_proj, q_edge, kv_own, out, normed, kv, flags, att,
):
    rows, width = x.shape
    half = HALF_WINDOW
    place = lax.axis_index("node")
    shards = counts.shape[0]
    own = counts[place]
    low_live = jnp.where(place > 0, counts[jnp.maximum(place - 1, 0)], 0)
    high_live = jnp.where(place < shards - 1, counts[jnp.minimum(place + 1, shards - 1)], 0)
    scale = channel_scale(gain, pert)
    odd = lax.rem(place, 2)
    far = rows + half
    first_at = pl.ds(pl.multiple_of((1 - odd) * far, half), half)
    second_at = pl.ds(pl.multiple_of(odd * far, half), half)
    normed[:half, :] = normalize(first[...], scale)
    normed[half:, :] = normalize(second[...], scale)
    for n in range(2):
        w = w_qkv[:, (n + 1) * width : (n + 2) * width]
        at = slice(n * width, (n + 1) * width)
        kv[first_at, at] = jnp.dot(normed[:half, :], w, preferred_element_type=F32).astype(BF16)
        kv[second_at, at] = jnp.dot(normed[half:, :], w, preferred_element_type=F32).astype(BF16)
    kv[half:far, :] = kv_own[...]
    flags[:half, :] = dead_flags(half, low_live - (rows - half))
    flags[half:far, :] = dead_flags(rows, own)
    flags[far:, :] = dead_flags(half, high_live)

    def side(b, _):
        here = pl.ds(pl.multiple_of(b * half, half), half)
        start = pl.multiple_of(b * (rows - half), half)
        window = pl.ds(start, 3 * half)
        attend_side(q_edge, kv, flags[window, :], att, here, window, width)
        fields = decode(x[pl.ds(start, half), :], att[...], w_proj[...], w_fields[...])
        live = iota(fields.shape, 1) + start < own
        out[:, here] = jnp.where(live, fields, 0.0).astype(BF16)
        return 0

    lax.fori_loop(0, 2, side, 0)


def score_values(mine, others, truth, live):
    total = 1 + len(others)
    eps = (1.0 - alpha_fair) / total
    mine = mine.astype(F32)
    others = [o.astype(F32) for o in others]

    def smooth(d):
        return jnp.sqrt(d * d + smooth_sq)

    d = mine - truth
    a = smooth(d)
    grad = d / a
    truth_sum = a
    for o in others:
        truth_sum = truth_sum + smooth(o - truth)
    pair_sum = jnp.zeros_like(a)
    pair_grad = jnp.zeros_like(a)
    for o in others:
        d = mine - o
        a = smooth(d)
        pair_sum = pair_sum + 2.0 * a
        pair_grad = pair_grad + d / a
    for i in range(len(others)):
        for j in range(i + 1, len(others)):
            pair_sum = pair_sum + 2.0 * smooth(others[i] - others[j])
    score = truth_sum * (1.0 / total) - (1.0 - eps) / (2.0 * total * (total - 1)) * pair_sum
    deriv = grad - (1.0 - eps) / (total - 1) * pair_grad
    return jnp.where(live, score, 0.0), jnp.where(live, deriv, 0.0)


def score_kernel(others, carried, place_of, counts, *refs):
    mine, rest, truth = refs[0], refs[1 : 1 + others], refs[1 + others]
    pred, score, deriv = refs[2 + others + carried :]
    width = mine.shape[1]
    own = counts[lax.axis_index("node")]
    start = place_of(pl.program_id(0)) * width
    live = iota(mine.shape, 1) + start < own
    pred[...] = mine[...]
    score[...], d = score_values(mine[...], [r[...] for r in rest], truth[...], live)
    deriv[...] = d[:, None, :]


def score_call(counts, mine, others, truth, carried, place_of, blocks):
    half = HALF_WINDOW
    fields, nodes = truth.shape
    part = pl.BlockSpec((fields, half), lambda i: (0, i))
    whole = pl.BlockSpec((fields, half), lambda i: (0, place_of(i)))
    flat = pl.BlockSpec((fields, 1, half), lambda i: (0, 0, place_of(i)))
    shapes = [
        jax.ShapeDtypeStruct((fields, nodes), BF16),
        jax.ShapeDtypeStruct((fields, nodes), F32),
        jax.ShapeDtypeStruct((fields, 1, nodes), F32),
    ]
    count = len(others)
    return pl.pallas_call(
        functools.partial(score_kernel, count, len(carried), place_of),
        grid=(blocks,),
        in_specs=[SMEM] + [part] * (1 + count) + [whole] + [ANY] * len(carried),
        out_specs=[whole, whole, flat],
        compiler_params=pltpu.CompilerParams(vmem_limit_bytes=8 << 20),
        out_shape=shapes,
        input_output_aliases={3 + count + i: i for i in range(len(carried))},
        cost_estimate=pl.CostEstimate(
            flops=40 * fields * half * blocks, bytes_accessed=20 * fields * half * blocks, transcendentals=0
        ),
    )(counts, mine, *others, truth, *carried)


def neighbours(count, start):
    pairs = [(i, i + 1) for i in range(start, count - 1, 2)]
    return pairs + [(t, s) for s, t in pairs]


def on_device(hidden, pert, gain, w_qkv, w_proj, w_fields, truth, counts):
    _, rows, width = hidden.shape
    fields = w_fields.shape[1]
    half = HALF_WINDOW
    blocks = rows // half
    x = hidden[0]
    gain = gain.reshape(1, width)
    w_fields = w_fields.T
    shards = lax.axis_size("node")
    members = lax.axis_size("ens")
    odd = lax.axis_index("node") % 2
    facing = lax.dynamic_slice_in_dim(x, (1 - odd) * (rows - half), half, 0)
    first = lax.ppermute(facing, "node", neighbours(shards, 0))
    facing = lax.dynamic_slice_in_dim(x, odd * (rows - half), half, 0)
    second = lax.ppermute(facing, "node", neighbours(shards, 1))

    inner = rows - 2 * half
    pred_in, q_edge, kv = pl.pallas_call(
        inner_kernel,
        in_specs=[SMEM, VMEM] + [ANY] * 5,
        out_specs=[VMEM] * 3,
        out_shape=[
            jax.ShapeDtypeStruct((fields, inner), BF16),
            jax.ShapeDtypeStruct((2 * half, width), BF16),
            jax.ShapeDtypeStruct((rows, 2 * width), BF16),
        ],
        scratch_shapes=[
            pltpu.VMEM((1, width), BF16),
            pltpu.VMEM((1, width), F32),
            pltpu.VMEM((fields, width), BF16),
            pltpu.VMEM((width, 3 * width), BF16),
            pltpu.VMEM((width, width), BF16),
            pltpu.VMEM((rows, width), BF16),
            pltpu.VMEM((inner, width), BF16),
            pltpu.VMEM((half, width), BF16),
            pltpu.SemaphoreType.DMA((3,)),
            pltpu.SemaphoreType.DMA((4,)),
        ],
        compiler_params=pltpu.CompilerParams(vmem_limit_bytes=KERNEL_VMEM),
        cost_estimate=pl.CostEstimate(
            flops=2 * rows * width * 3 * width + 2 * inner * width * width + 12 * inner * width * half,
            bytes_accessed=10 * width * width,
            transcendentals=inner * HEADS * 3 * half,
        ),
        name="inner_blocks",
    )(counts, x, *[pltpu.with_memory_space_constraint(w, pltpu.HBM) for w in (pert, gain, w_fields, w_qkv, w_proj)])

    def exchange(part):
        return [
            lax.ppermute(part, "ens", [(i, (i + s) % members) for i in range(members)])
            for s in range(1, members)
        ]

    others_in = exchange(pred_in)
    pred_edge = pl.pallas_call(
        edge_kernel,
        in_specs=[SMEM] + [VMEM] * 10,
        out_specs=VMEM,
        out_shape=jax.ShapeDtypeStruct((fields, 2 * half), BF16),
        scratch_shapes=[
            pltpu.VMEM((2 * half, width), BF16),
            pltpu.VMEM((rows + 2 * half, 2 * width), BF16),
            pltpu.VMEM((rows + 2 * half, LANES), BF16),
            pltpu.VMEM((half, width), BF16),
        ],
        compiler_params=pltpu.CompilerParams(vmem_limit_bytes=KERNEL_VMEM),
        cost_estimate=pl.CostEstimate(
            flops=2 * 2 * half * width * 3 * width + 12 * 2 * half * width * half,
            bytes_accessed=10 * width * width,
            transcendentals=2 * half * HEADS * 3 * half,
        ),
        name="edge_blocks",
    )(counts, pert, gain, w_fields, first, second, x, w_qkv, w_proj, q_edge, kv)
    others_edge = exchange(pred_edge)
    partial = score_call(counts, pred_in, others_in, truth, [], lambda i: i + 1, blocks - 2)
    pred, score, deriv = score_call(
        counts, pred_edge, others_edge, truth, partial, lambda i: i * (blocks - 1), 2
    )
    return pred[None], score, deriv.transpose(1, 0, 2)


def solution(mesh):
    return jax.shard_map(
        on_device,
        mesh=mesh,
        in_specs=(P("ens", "node", None), P("ens", None), P(), P(), P(), P(), P(None, "node"), P()),
        out_specs=(P("ens", None, "node"), P(None, "node"), P("ens", None, "node")),
        check_vma=False,
    )
```

time: 69.2 us -> 50.3 us (0.73)
  Pallas kernels: 51 us -> 38 us
  local copies, waits for them, and re-layouts: 6.62 us -> 1.47 us
  waiting for transfers between devices: 3.21 us -> 2.5 us
    pallas_call x1, Pallas kernels: 20.8 us -> 14.1 us  [on_device(): pl.pallas_call(edge_kernel, in_specs=[SMEM] + [VMEM] * 10, out_specs=VMEM...]
    pallas_call x1, Pallas kernels: 26.1 us -> 20.5 us  [on_device(): pl.pallas_call(inner_kernel, in_specs=[SMEM, VMEM] + [ANY] * 5, out_specs...]
    unnamed x12 -> x18, local copies, waits for them, and re-layouts: 5.31 us -> 0.05 us
    dynamic_slice x0 -> x1, local copies, waits for them, and re-layouts: none -> 1.42 us  [on_device(): facing = lax.dynamic_slice_in_dim(x, odd * (rows - half), half, 0)]
    slice x1 -> x0, local copies, waits for them, and re-layouts: 1.31 us -> none  [on_device(): high = lax.ppermute(x[:half], 'node', down)]
    ppermute x2, starting transfers between devices: 4.36 us -> 5.19 us  [the longest x1 4.36 us: on_device(): first = lax.ppermute(facing, 'node', neighbours(shards, 0))]
    ppermute x2, starting transfers between devices: 2.99 us -> 2.16 us  [exchange(): lax.ppermute(part, 'ens', [(i, (i + s) % members) for i in range(members)])]
    pallas_call x2, Pallas kernels: 4.17 us -> 3.39 us  [score_call(): pl.pallas_call(functools.partial(score_kernel, count, len(carried), place...]
  transfers between devices with their start and end apart: 4 -> 4, of which waited for: 1 -> 1; matrix products, arithmetic and copies ran while one was open for 1% -> 0% of each run, Pallas kernels for 71% -> 72%
where the time goes in v3:
time: 50.3 us; the launch traced here: 50.1 us
  Pallas kernels  38 us (76%)
  starting transfers between devices  7.34 us (15%)
  waiting for transfers between devices  2.5 us (5%)
  local copies, waits for them, and re-layouts  1.47 us (3%)
  between operations  0.79 us (2%)
    pallas_call x1, Pallas kernels, on_device(): pl.pallas_call(inner_kernel, in_specs=[SMEM, VMEM] + [ANY] * 5, out_specs...  20.5 us
    pallas_call x1, Pallas kernels, on_device(): pl.pallas_call(edge_kernel, in_specs=[SMEM] + [VMEM] * 10, out_specs=VMEM...  14.1 us
    ppermute x1, starting transfers between devices, on_device(): first = lax.ppermute(facing, 'node', neighbours(shards, 0))  4.36 us
    pallas_call x2, Pallas kernels, score_call(): pl.pallas_call(functools.partial(score_kernel, count, len(carried), place...  3.39 us
    ppermute x2, waiting for transfers between devices, exchange(): lax.ppermute(part, 'ens', [(i, (i + s) % members) for i in range(members)])  2.49 us
    ppermute x2, starting transfers between devices, exchange(): lax.ppermute(part, 'ens', [(i, (i + s) % members) for i in range(members)])  2.16 us
    dynamic_slice x1, local copies, waits for them, and re-layouts, on_device(): facing = lax.dynamic_slice_in_dim(x, odd * (rows - half), half, 0)  1.42 us
  transfers between devices with their start and end apart: 4, of which 1 were waited for; matrix products, arithmetic and copies ran while one was open for 0% of the time, Pallas kernels for 72%

profile of v3, /device:TPU:0, one launch (start us, length us, event | category | flops | bytes accessed | tf_op | source)
XLA Modules:
  0.0 50.1 jit_solution(6508533222659680907)
XLA Ops:
  0.6 0.0 copy-start.1
  0.6 0.0 copy-start.2
  0.7 0.0 slice-start
  0.7 1.4 %dynamic-slice_bitcast_fusion = (bf16[256,1024]{1,0:T(8,128)(2,1)S(1)}, bf16[256,1024]{1,0:T(8,128)(2,1)S(1)}) fusion(bf16[1,1024,1024]{2,1,0:T(8,128)(2,1)} %param.8, s32[]{:T(128)S(6)} %select_n.15, s32[]{:T(128)S(6)} %select_n.14), kind=kLoop, calls=%fused_computation | loop fusion | bytes 2097160 | tf_op jit(solution)/shard_map/dynamic_slice | solution.py:290
  2.1 0.8 %collective-permute-start.1 = (bf16[256,1024]{1,0:T(8,128)(2,1)S(1)}, bf16[256,1024]{1,0:T(8,128)(2,1)S(1)}, u32[]{:S(2)}, u32[]{:S(2)}) collective-permute-start(bf16[256,1024]{1,0:T(8,128)(2,1)S(1)} %get-tuple-element.21), channel_id=1, source_target_pairs={{1,2},{3,4},{5,6},{7,8},{9,10},{11,12},{13,14},{2,1},{4,3},{6,5},{... | collective-permute-start | bytes 1572872 | tf_op jit(solution)/shard_map/ppermute | solution.py:291
  2.9 4.4 %collective-permute-start = (bf16[256,1024]{1,0:T(8,128)(2,1)S(1)}, bf16[256,1024]{1,0:T(8,128)(2,1)S(1)}, u32[]{:S(2)}, u32[]{:S(2)}) collective-permute-start(bf16[256,1024]{1,0:T(8,128)(2,1)S(1)} %get-tuple-element.22), channel_id=1, source_target_pairs={{0,1},{2,3},{4,5},{6,7},{8,9},{10,11},{12,13},{14,15},{1,0},{3,2},... | collective-permute-start | bytes 1572872 | tf_op jit(solution)/shard_map/ppermute | solution.py:289
  7.3 0.0 copy-done.1
  7.3 0.0 copy-done.2
  7.3 0.0 slice-start.1
  7.3 0.0 copy-start.3
  7.3 0.0 copy-start.4
  7.3 0.0 copy-start.5
  7.3 0.0 copy-start.6
  7.4 20.5 %inner_blocks.1 = (bf16[100,512]{1,0:T(8,128)(2,1)S(1)}, bf16[512,1024]{1,0:T(8,128)(2,1)S(1)}, bf16[1024,2048]{1,0:T(8,128)(2,1)S(1)}) custom-call(s32[16]{0:T(128)S(1)} %copy-done.2, bf16[1024,1024]{1,0:T(8,128)(2,1)S(1)} %bitcast.9, bf16[1,1024]{1,0:T(2,128)(2,1)} %pert.1, f32[1,1024]{1,0:T(1,128)} %bitcast.15, bf16[100,1024]{1,0:T(8,128)(2,1)} %bitcast.13, ...), custom_call_target="tpu_custom_call" | custom-call | flops 9126805504 | bytes 10485760 | tf_op jit(solution)/shard_map/inner_blocks/pallas_call | solution.py:294
  27.9 1.6 %collective-permute-start.3 = (bf16[100,512]{1,0:T(8,128)(2,1)S(1)}, bf16[100,512]{1,0:T(8,128)(2,1)S(1)}, u32[]{:S(2)}, u32[]{:S(2)}) collective-permute-start(bf16[100,512]{1,0:T(8,128)(2,1)S(1)} %get-tuple-element.14.refs_0_), channel_id=1, source_target_pairs={{0,16},{16,0},{1,17},{17,1},{2,18},{18,2},{3,19},{19,3},{4,20},{20... | collective-permute-start | bytes 307208 | tf_op jit(solution)/shard_map/ppermute | solution.py:326
  29.5 0.0 collective-permute-done.1.second
  29.5 0.0 collective-permute-done.first
  29.5 0.0 slice-done
  29.5 0.0 slice-done.1
  29.5 0.0 copy-done.3
  29.5 0.0 copy-done.4
  29.5 0.0 copy-done.5
  29.5 0.0 copy-done.6
  29.5 0.0 copy-start
  29.5 14.1 %edge_blocks.1.refs_0_ = bf16[100,512]{1,0:T(8,128)(2,1)S(1)} custom-call(s32[16]{0:T(128)S(1)} %copy-done.2, bf16[1,1024]{1,0:T(2,128)(2,1)S(1)} %copy-done.5, f32[1,1024]{1,0:T(1,128)S(1)} %bitcast.16, bf16[100,1024]{1,0:T(8,128)(2,1)S(1)} %bitcast.14, bf16[256,1024]{1,0:T(8,128)(2,1)S(1)} %collective-permute-done.first, ...), custom_call_target="tpu_custom_call" | custom-call | flops 4831838208 | bytes 10485760 | tf_op jit(solution)/shard_map/edge_blocks/pallas_call | solution.py:331
  43.6 0.6 %collective-permute-start.2 = (bf16[100,512]{1,0:T(8,128)(2,1)S(1)}, bf16[100,512]{1,0:T(8,128)(2,1)S(1)}, u32[]{:S(2)}, u32[]{:S(2)}) collective-permute-start(bf16[100,512]{1,0:T(8,128)(2,1)S(1)} %edge_blocks.1.refs_0_), channel_id=1, source_target_pairs={{0,16},{16,0},{1,17},{17,1},{2,18},{18,2},{3,19},{19,3},{4,20},{20... | collective-permute-start | bytes 307208 | tf_op jit(solution)/shard_map/ppermute | solution.py:326
  44.2 0.0 collective-permute-done.3.refs_1_
  44.2 0.0 copy-done
  44.2 1.7 %shard_map.103 = (bf16[100,1024]{1,0:T(8,128)(2,1)}, f32[100,1024]{1,0:T(8,128)}, f32[100,1,1024]{2,1,0:T(1,128)}) custom-call(s32[16]{0:T(128)S(1)} %copy-done.2, bf16[100,512]{1,0:T(8,128)(2,1)S(1)} %get-tuple-element.14.refs_0_, bf16[100,512]{1,0:T(8,128)(2,1)S(1)} %collective-permute-done.3.refs_1_, f32[100,1024]{1,0:T(8,128)S(1)} %copy-done), custom_call_target="tpu_custom_call" | custom-call | flops 2048000 | bytes 1024000 | tf_op jit(solution)/shard_map/pallas_call | solution.py:258
  45.9 2.5 %collective-permute-done.2.refs_1_ = bf16[100,512]{1,0:T(8,128)(2,1)S(1)} collective-permute-done((bf16[100,512]{1,0:T(8,128)(2,1)S(1)}, bf16[100,512]{1,0:T(8,128)(2,1)S(1)}, u32[]{:S(2)}, u32[]{:S(2)}) %collective-permute-start.2) | collective-permute-done | bytes 102432 | tf_op jit(solution)/shard_map/ppermute | solution.py:326
  48.4 1.7 %shard_map.104 = (bf16[100,1024]{1,0:T(8,128)(2,1)}, f32[100,1024]{1,0:T(8,128)}, f32[100,1,1024]{2,1,0:T(1,128)}) custom-call(s32[16]{0:T(128)S(1)} %copy-done.2, bf16[100,512]{1,0:T(8,128)(2,1)S(1)} %edge_blocks.1.refs_0_, bf16[100,512]{1,0:T(8,128)(2,1)S(1)} %collective-permute-done.2.refs_1_, ...), custom_call_target="tpu_custom_call", output_to_operand_aliasing={{0}: (4, {}), {1}: (5, {}), {2}: (6, {})} | custom-call | flops 2048000 | bytes 1024000 | tf_op jit(solution)/shard_map/pallas_call | solution.py:258
  (1 shorter events, 0.0 us)
Async XLA Ops:
  0.6 6.7 %copy-start.1 = (bf16[1,1024,1024]{2,1,0:T(8,128)(2,1)S(1)}, bf16[1,1024,1024]{2,1,0:T(8,128)(2,1)}, u32[]{:S(2)}) copy-start(bf16[1,1024,1024]{2,1,0:T(8,128)(2,1)} %param.8) | copy-start | bytes 6291460
  0.6 6.7 %copy-start.2 = (s32[16]{0:T(128)S(1)}, s32[16]{0:T(128)}, u32[]{:S(2)}) copy-start(s32[16]{0:T(128)} %counts.7) | copy-start | bytes 196
  0.7 28.8 %slice-start = ((s8[6291456]{0:T(1024)(128)(4,1)}), s8[4194304]{0:T(1024)(128)(4,1)S(1)}, s32[]{:S(2)}) async-start(s8[6291456]{0:T(1024)(128)(4,1)} %bitcast.11), calls=%async_computation | async-start | bytes 8388608
  2.1 27.3 %collective-permute-start.1 = (bf16[256,1024]{1,0:T(8,128)(2,1)S(1)}, bf16[256,1024]{1,0:T(8,128)(2,1)S(1)}, u32[]{:S(2)}, u32[]{:S(2)}) collective-permute-start(bf16[256,1024]{1,0:T(8,128)(2,1)S(1)} %get-tuple-element.21), channel_id=1, source_target_pairs={{1,2},{3,4},{5,6},{7,8},{9,10},{11,12},{13,14},{2,1},{4,3},{6,5},{... | collective-permute-start | bytes 1572872 | tf_op jit(solution)/shard_map/ppermute | solution.py:291
  2.9 26.5 %collective-permute-start = (bf16[256,1024]{1,0:T(8,128)(2,1)S(1)}, bf16[256,1024]{1,0:T(8,128)(2,1)S(1)}, u32[]{:S(2)}, u32[]{:S(2)}) collective-permute-start(bf16[256,1024]{1,0:T(8,128)(2,1)S(1)} %get-tuple-element.22), channel_id=1, source_target_pairs={{0,1},{2,3},{4,5},{6,7},{8,9},{10,11},{12,13},{14,15},{1,0},{3,2},... | collective-permute-start | bytes 1572872 | tf_op jit(solution)/shard_map/ppermute | solution.py:289
  7.3 22.2 %slice-start.1 = ((s8[6291456]{0:T(1024)(128)(4,1)}), s8[2097152]{0:T(1024)(128)(4,1)S(1)}, s32[]{:S(2)}) async-start(s8[6291456]{0:T(1024)(128)(4,1)} %bitcast.11), calls=%async_computation.1 | async-start | bytes 4194304
  7.3 22.2 %copy-start.3 = (bf16[1024,1024]{1,0:T(8,128)(2,1)S(1)}, bf16[1024,1024]{1,0:T(8,128)(2,1)}, u32[]{:S(2)}) copy-start(bf16[1024,1024]{1,0:T(8,128)(2,1)} %w_proj.1) | copy-start | bytes 6291460
  7.3 22.2 %copy-start.4 = (bf16[1024,100]{0,1:T(8,128)(2,1)S(1)}, bf16[1024,100]{0,1:T(8,128)(2,1)}, u32[]{:S(2)}) copy-start(bf16[1024,100]{0,1:T(8,128)(2,1)} %param.13) | copy-start | bytes 614404
  7.3 22.2 %copy-start.5 = (bf16[1,1024]{1,0:T(2,128)(2,1)S(1)}, bf16[1,1024]{1,0:T(2,128)(2,1)}, u32[]{:S(2)}) copy-start(bf16[1,1024]{1,0:T(2,128)(2,1)} %pert.1) | copy-start | bytes 6148
  7.3 22.2 %copy-start.6 = (f32[1024]{0:T(1024)S(1)}, f32[1024]{0:T(1024)}, u32[]{:S(2)}) copy-start(f32[1024]{0:T(1024)} %param.10) | copy-start | bytes 12292
  27.9 16.4 %collective-permute-start.3 = (bf16[100,512]{1,0:T(8,128)(2,1)S(1)}, bf16[100,512]{1,0:T(8,128)(2,1)S(1)}, u32[]{:S(2)}, u32[]{:S(2)}) collective-permute-start(bf16[100,512]{1,0:T(8,128)(2,1)S(1)} %get-tuple-element.14.refs_0_), channel_id=1, source_target_pairs={{0,16},{16,0},{1,17},{17,1},{2,18},{18,2},{3,19},{19,3},{4,20},{20... | collective-permute-start | bytes 307208 | tf_op jit(solution)/shard_map/ppermute | solution.py:326
  29.5 14.7 %copy-start = (f32[100,1024]{1,0:T(8,128)S(1)}, f32[100,1024]{1,0:T(8,128)}, u32[]{:S(2)}) copy-start(f32[100,1024]{1,0:T(8,128)} %refs_2_.3) | copy-start | bytes 1228804
  43.6 4.8 %collective-permute-start.2 = (bf16[100,512]{1,0:T(8,128)(2,1)S(1)}, bf16[100,512]{1,0:T(8,128)(2,1)S(1)}, u32[]{:S(2)}, u32[]{:S(2)}) collective-permute-start(bf16[100,512]{1,0:T(8,128)(2,1)S(1)} %edge_blocks.1.refs_0_), channel_id=1, source_target_pairs={{0,16},{16,0},{1,17},{17,1},{2,18},{18,2},{3,19},{19,3},{4,20},{20... | collective-permute-start | bytes 307208 | tf_op jit(solution)/shard_map/ppermute | solution.py:326

commit v4 on v3

--- a/solution.py
+++ b/solution.py
@@ -16,6 +16,7 @@
 NEG = -1e30
 LOG2E = 1.4426950408889634
 KERNEL_VMEM = 32 << 20
+FACING_FLOPS = 8_000_000_000
 
 F32 = jnp.float32
 BF16 = jnp.bfloat16
@@ -94,27 +95,23 @@
     )
 
 
-def inner_kernel(
-    counts, x, pert_hbm, gain_hbm, w_fields_hbm, w_qkv_hbm, w_proj_hbm, out, q_edge, kv,
-    pert, gain, w_fields, w_qkv, w_proj, normed, q_in, att, w_sem, s_sem,
-):
+def facing_kernel(x, first, second, sem):
+    rows = x.shape[0]
+    half = first.shape[0]
+    odd = lax.rem(lax.axis_index("node"), 2)
+    at = [pl.multiple_of(o * (rows - half), half) for o in (1 - odd, odd)]
+    moves = [
+        pltpu.make_async_copy(x.at[pl.ds(a, half), :], out, sem.at[i])
+        for i, (a, out) in enumerate(zip(at, (first, second)))
+    ]
+    for c in moves:
+        c.start()
+    for c in moves:
+        c.wait()
+
+
+def inner_kernel(counts, x, pert, gain, w_fields, w_qkv, w_proj, out, q_edge, kv, normed, q_in, att):
     rows, width = x.shape
-    scale_in = [
-        pltpu.make_async_copy(pert_hbm, pert, s_sem.at[0]),
-        pltpu.make_async_copy(gain_hbm, gain, s_sem.at[1]),
-    ]
-    w_in = [
-        pltpu.make_async_copy(
-            w_qkv_hbm.at[:, n * width : (n + 1) * width], w_qkv.at[:, n * width : (n + 1) * width], w_sem.at[n]
-        )
-        for n in range(3)
-    ]
-    late = [
-        pltpu.make_async_copy(w_fields_hbm, w_fields, s_sem.at[2]),
-        pltpu.make_async_copy(w_proj_hbm, w_proj, s_sem.at[3]),
-    ]
-    for c in scale_in + w_in + late:
-        c.start()
     half = HALF_WINDOW
     blocks = rows // half
     own = counts[lax.axis_index("node")]
@@ -123,8 +120,6 @@
     def part(b):
         return slice(b * half, (b + 1) * half)
 
-    for c in scale_in:
-        c.wait()
     scale = channel_scale(gain, pert)
     normed[part(0), :] = normalize(x[part(0), :], scale)
     for b in range(blocks):
@@ -132,8 +127,6 @@
             normed[part(b + 1), :] = normalize(x[part(b + 1), :], scale)
         here = normed[part(b), :]
         for n in range(3):
-            if b == 0:
-                w_in[n].wait()
             res = jnp.dot(here, w_qkv[:, n * width : (n + 1) * width], preferred_element_type=F32).astype(BF16)
             if n > 0:
                 kv[part(b), (n - 1) * width : n * width] = res
@@ -143,9 +136,6 @@
                 q_edge[half:, :] = res * head_scale
             else:
                 q_in[part(b - 1), :] = res * head_scale
-
-    for c in late:
-        c.wait()
 
     def block(b, _):
         start = pl.multiple_of(b * half, half)
@@ -231,41 +221,57 @@
     return jnp.where(live, score, 0.0), jnp.where(live, deriv, 0.0)
 
 
-def score_kernel(others, carried, place_of, counts, *refs):
+def score_kernel(others, carried, places, counts, *refs):
     mine, rest, truth = refs[0], refs[1 : 1 + others], refs[1 + others]
-    pred, score, deriv = refs[2 + others + carried :]
-    width = mine.shape[1]
+    pred, score, deriv = refs[2 + others + carried : 5 + others + carried]
+    score_buf, deriv_buf, sem = refs[5 + others + carried :]
+    half = HALF_WINDOW
     own = counts[lax.axis_index("node")]
-    start = place_of(pl.program_id(0)) * width
-    live = iota(mine.shape, 1) + start < own
-    pred[...] = mine[...]
-    score[...], d = score_values(mine[...], [r[...] for r in rest], truth[...], live)
-    deriv[...] = d[:, None, :]
-
-
-def score_call(counts, mine, others, truth, carried, place_of, blocks):
+    moves = []
+    for i, place in enumerate(places):
+        here, there = slice(i * half, (i + 1) * half), slice(place * half, (place + 1) * half)
+        moves.append(pltpu.make_async_copy(mine.at[:, here], pred.at[:, there], sem.at[0, i]))
+        moves[-1].start()
+    for i, place in enumerate(places):
+        here, there = slice(i * half, (i + 1) * half), slice(place * half, (place + 1) * half)
+        f = mine[:, here]
+        live = iota(f.shape, 1) + place * half < own
+        score_buf[i], d = score_values(f, [r[:, here] for r in rest], truth[:, there], live)
+        moves.append(pltpu.make_async_copy(score_buf.at[i], score.at[:, there], sem.at[1, i]))
+        moves[-1].start()
+        deriv_buf[i] = d[:, None, :]
+        moves.append(pltpu.make_async_copy(deriv_buf.at[i], deriv.at[:, :, there], sem.at[2, i]))
+        moves[-1].start()
+    for c in moves:
+        c.wait()
+
+
+def score_call(counts, mine, others, truth, carried, places):
     half = HALF_WINDOW
     fields, nodes = truth.shape
-    part = pl.BlockSpec((fields, half), lambda i: (0, i))
-    whole = pl.BlockSpec((fields, half), lambda i: (0, place_of(i)))
-    flat = pl.BlockSpec((fields, 1, half), lambda i: (0, 0, place_of(i)))
     shapes = [
         jax.ShapeDtypeStruct((fields, nodes), BF16),
         jax.ShapeDtypeStruct((fields, nodes), F32),
         jax.ShapeDtypeStruct((fields, 1, nodes), F32),
     ]
     count = len(others)
+    parts = len(places)
     return pl.pallas_call(
-        functools.partial(score_kernel, count, len(carried), place_of),
-        grid=(blocks,),
-        in_specs=[SMEM] + [part] * (1 + count) + [whole] + [ANY] * len(carried),
-        out_specs=[whole, whole, flat],
+        functools.partial(score_kernel, count, len(carried), places),
+        in_specs=[SMEM] + [VMEM] * (2 + count) + [ANY] * len(carried),
+        out_specs=[ANY] * 3,
+        out_shape=shapes,
+        scratch_shapes=[
+            pltpu.VMEM((parts, fields, half), F32),
+            pltpu.VMEM((parts, fields, 1, half), F32),
+            pltpu.SemaphoreType.DMA((3, parts)),
+        ],
         compiler_params=pltpu.CompilerParams(vmem_limit_bytes=8 << 20),
-        out_shape=shapes,
         input_output_aliases={3 + count + i: i for i in range(len(carried))},
         cost_estimate=pl.CostEstimate(
-            flops=40 * fields * half * blocks, bytes_accessed=20 * fields * half * blocks, transcendentals=0
+            flops=40 * fields * half * parts, bytes_accessed=20 * fields * half * parts, transcendentals=0
         ),
+        name="score",
     )(counts, mine, *others, truth, *carried)
 
 
@@ -284,16 +290,23 @@
     w_fields = w_fields.T
     shards = lax.axis_size("node")
     members = lax.axis_size("ens")
-    odd = lax.axis_index("node") % 2
-    facing = lax.dynamic_slice_in_dim(x, (1 - odd) * (rows - half), half, 0)
-    first = lax.ppermute(facing, "node", neighbours(shards, 0))
-    facing = lax.dynamic_slice_in_dim(x, odd * (rows - half), half, 0)
-    second = lax.ppermute(facing, "node", neighbours(shards, 1))
+    halves = pl.pallas_call(
+        facing_kernel,
+        in_specs=[ANY],
+        out_specs=[VMEM] * 2,
+        out_shape=[jax.ShapeDtypeStruct((half, width), BF16)] * 2,
+        scratch_shapes=[pltpu.SemaphoreType.DMA((2,))],
+        compiler_params=pltpu.CompilerParams(vmem_limit_bytes=4 << 20),
+        cost_estimate=pl.CostEstimate(flops=FACING_FLOPS, bytes_accessed=4 * half * width, transcendentals=0),
+        name="facing",
+    )(pltpu.with_memory_space_constraint(x, pltpu.HBM))
+    first = lax.ppermute(halves[0], "node", neighbours(shards, 0))
+    second = lax.ppermute(halves[1], "node", neighbours(shards, 1))
 
     inner = rows - 2 * half
     pred_in, q_edge, kv = pl.pallas_call(
         inner_kernel,
-        in_specs=[SMEM, VMEM] + [ANY] * 5,
+        in_specs=[SMEM] + [VMEM] * 6,
         out_specs=[VMEM] * 3,
         out_shape=[
             jax.ShapeDtypeStruct((fields, inner), BF16),
@@ -301,16 +314,9 @@
             jax.ShapeDtypeStruct((rows, 2 * width), BF16),
         ],
         scratch_shapes=[
-            pltpu.VMEM((1, width), BF16),
-            pltpu.VMEM((1, width), F32),
-            pltpu.VMEM((fields, width), BF16),
-            pltpu.VMEM((width, 3 * width), BF16),
-            pltpu.VMEM((width, width), BF16),
             pltpu.VMEM((rows, width), BF16),
             pltpu.VMEM((inner, width), BF16),
             pltpu.VMEM((half, width), BF16),
-            pltpu.SemaphoreType.DMA((3,)),
-            pltpu.SemaphoreType.DMA((4,)),
         ],
         compiler_params=pltpu.CompilerParams(vmem_limit_bytes=KERNEL_VMEM),
         cost_estimate=pl.CostEstimate(
@@ -319,7 +325,7 @@
             transcendentals=inner * HEADS * 3 * half,
         ),
         name="inner_blocks",
-    )(counts, x, *[pltpu.with_memory_space_constraint(w, pltpu.HBM) for w in (pert, gain, w_fields, w_qkv, w_proj)])
+    )(counts, x, pert, gain, w_fields, w_qkv, w_proj)
 
     def exchange(part):
         return [
@@ -348,10 +354,8 @@
         name="edge_blocks",
     )(counts, pert, gain, w_fields, first, second, x, w_qkv, w_proj, q_edge, kv)
     others_edge = exchange(pred_edge)
-    partial = score_call(counts, pred_in, others_in, truth, [], lambda i: i + 1, blocks - 2)
-    pred, score, deriv = score_call(
-        counts, pred_edge, others_edge, truth, partial, lambda i: i * (blocks - 1), 2
-    )
+    partial = score_call(counts, pred_in, others_in, truth, [], list(range(1, blocks - 1)))
+    pred, score, deriv = score_call(counts, pred_edge, others_edge, truth, partial, [0, blocks - 1])
     return pred[None], score, deriv.transpose(1, 0, 2)
 
 

time: 50.3 us -> 48.5 us (0.964)
  starting transfers between devices: 7.34 us -> 4.53 us
  waiting for transfers between devices: 2.5 us -> 3.94 us
  Pallas kernels: 38 us -> 37.4 us
    ppermute x2, starting transfers between devices: 5.19 us -> 1.37 us  [the longest x1 0.81 us: on_device(): second = lax.ppermute(halves[1], 'node', neighbours(shards, 1))]
    unnamed x18 -> x16, local copies, waits for them, and re-layouts: 0.05 us -> 1.52 us
    ppermute x2, waiting for transfers between devices: 2.49 us -> 3.93 us  [exchange(): lax.ppermute(part, 'ens', [(i, (i + s) % members) for i in range(members)])]
    dynamic_slice x1 -> x0, local copies, waits for them, and re-layouts: 1.42 us -> none  [on_device(): facing = lax.dynamic_slice_in_dim(x, odd * (rows - half), half, 0)]
    ppermute x2, starting transfers between devices: 2.16 us -> 3.16 us  [exchange(): lax.ppermute(part, 'ens', [(i, (i + s) % members) for i in range(members)])]
    pallas_call x1 -> x2, Pallas kernels: 20.5 us -> 20 us  [the longest x1 18.7 us: on_device(): pl.pallas_call(inner_kernel, in_specs=[SMEM] + [VMEM] * 6, out_specs=[VME...]
  transfers between devices with their start and end apart: 4 -> 4, of which waited for: 1 -> 1; matrix products, arithmetic and copies ran while one was open for 0% -> 0% of each run, Pallas kernels for 72% -> 71%
where the time goes in v4:
time: 48.5 us; the launch traced here: 48.3 us
  Pallas kernels  37.4 us (77%)
  starting transfers between devices  4.53 us (9%)
  waiting for transfers between devices  3.94 us (8%)
  local copies, waits for them, and re-layouts  1.52 us (3%)
  between operations  0.91 us (2%)
    pallas_call x1, Pallas kernels, on_device(): pl.pallas_call(inner_kernel, in_specs=[SMEM] + [VMEM] * 6, out_specs=[VME...  18.7 us
    pallas_call x1, Pallas kernels, on_device(): pl.pallas_call(edge_kernel, in_specs=[SMEM] + [VMEM] * 10, out_specs=VMEM...  14 us
    ppermute x2, waiting for transfers between devices, exchange(): lax.ppermute(part, 'ens', [(i, (i + s) % members) for i in range(members)])  3.93 us
    pallas_call x2, Pallas kernels, score_call(): pl.pallas_call(functools.partial(score_kernel, count, len(carried), place...  3.31 us
    ppermute x2, starting transfers between devices, exchange(): lax.ppermute(part, 'ens', [(i, (i + s) % members) for i in range(members)])  3.16 us
    unnamed x16, local copies, waits for them, and re-layouts  1.52 us
    pallas_call x1, Pallas kernels, on_device(): pl.pallas_call(facing_kernel, in_specs=[ANY], out_specs=[VMEM] * 2, out_s...  1.38 us
  transfers between devices with their start and end apart: 4, of which 1 were waited for; matrix products, arithmetic and copies ran while one was open for 0% of the time, Pallas kernels for 71%

profile of v4, /device:TPU:0, one launch (start us, length us, event | category | flops | bytes accessed | tf_op | source)
XLA Modules:
  0.0 48.3 jit_solution(234472477252687358)
XLA Ops:
  0.6 0.0 copy-start.1
  0.6 0.0 copy-start.2
  0.7 0.0 copy-start.3
  0.7 0.0 copy-start.4
  0.7 0.0 copy-start.5
  0.7 0.0 copy-start.6
  0.7 0.0 copy-start.7
  0.7 1.4 %facing.1 = (bf16[256,1024]{1,0:T(8,128)(2,1)S(1)}, bf16[256,1024]{1,0:T(8,128)(2,1)S(1)}) custom-call(bf16[1024,1024]{1,0:T(8,128)(2,1)} %bitcast.5), custom_call_target="tpu_custom_call" | custom-call | flops 8000000000 | bytes 1048576 | tf_op jit(solution)/shard_map/facing/pallas_call | solution.py:293
  2.1 0.6 %collective-permute-start = (bf16[256,1024]{1,0:T(8,128)(2,1)S(1)}, bf16[256,1024]{1,0:T(8,128)(2,1)S(1)}, u32[]{:S(2)}, u32[]{:S(2)}) collective-permute-start(bf16[256,1024]{1,0:T(8,128)(2,1)S(1)} %get-tuple-element.14), channel_id=1, source_target_pairs={{0,1},{2,3},{4,5},{6,7},{8,9},{10,11},{12,13},{14,15},{1,0},{3,2},... | collective-permute-start | bytes 1572872 | tf_op jit(solution)/shard_map/ppermute | solution.py:303
  2.6 0.8 %collective-permute-start.1 = (bf16[256,1024]{1,0:T(8,128)(2,1)S(1)}, bf16[256,1024]{1,0:T(8,128)(2,1)S(1)}, u32[]{:S(2)}, u32[]{:S(2)}) collective-permute-start(bf16[256,1024]{1,0:T(8,128)(2,1)S(1)} %get-tuple-element.15), channel_id=1, source_target_pairs={{1,2},{3,4},{5,6},{7,8},{9,10},{11,12},{13,14},{2,1},{4,3},{6,5},{... | collective-permute-start | bytes 1572872 | tf_op jit(solution)/shard_map/ppermute | solution.py:304
  3.5 0.0 copy-done.1
  3.5 0.3 copy-done.2
  3.7 0.6 %copy-done.3 = bf16[1,1024,1024]{2,1,0:T(8,128)(2,1)S(1)} copy-done((bf16[1,1024,1024]{2,1,0:T(8,128)(2,1)S(1)}, bf16[1,1024,1024]{2,1,0:T(8,128)(2,1)}, u32[]{:S(2)}) %copy-start.3) | copy-done | bytes 2097176
  4.4 0.6 %copy-done.4 = bf16[1024,1024]{1,0:T(8,128)(2,1)S(1)} copy-done((bf16[1024,1024]{1,0:T(8,128)(2,1)S(1)}, bf16[1024,1024]{1,0:T(8,128)(2,1)}, u32[]{:S(2)}) %copy-start.4) | copy-done | bytes 2097176
  5.0 0.0 copy-done.5
  5.0 0.0 copy-done.6
  5.0 0.0 copy-done.7
  5.0 18.7 %inner_blocks.1 = (bf16[100,512]{1,0:T(8,128)(2,1)S(1)}, bf16[512,1024]{1,0:T(8,128)(2,1)S(1)}, bf16[1024,2048]{1,0:T(8,128)(2,1)S(1)}) custom-call(s32[16]{0:T(128)S(1)} %copy-done.1, bf16[1024,1024]{1,0:T(8,128)(2,1)S(1)} %bitcast.6, bf16[1,1024]{1,0:T(2,128)(2,1)S(1)} %copy-done.6, f32[1,1024]{1,0:T(1,128)S(1)} %bitcast.10, ...), custom_call_target="tpu_custom_call" | custom-call | flops 9126805504 | bytes 10485760 | tf_op jit(solution)/shard_map/inner_blocks/pallas_call | solution.py:307
  23.6 3.1 %collective-permute-start.3 = (bf16[100,512]{1,0:T(8,128)(2,1)S(1)}, bf16[100,512]{1,0:T(8,128)(2,1)S(1)}, u32[]{:S(2)}, u32[]{:S(2)}) collective-permute-start(bf16[100,512]{1,0:T(8,128)(2,1)S(1)} %get-tuple-element.18.refs_0_), channel_id=1, source_target_pairs={{0,16},{16,0},{1,17},{17,1},{2,18},{18,2},{3,19},{19,3},{4,20},{20... | collective-permute-start | bytes 307208 | tf_op jit(solution)/shard_map/ppermute | solution.py:332
  26.7 0.0 collective-permute-done.first
  26.7 0.0 collective-permute-done.1.second
  26.7 0.0 copy-start
  26.7 14.0 %edge_blocks.1.refs_0_ = bf16[100,512]{1,0:T(8,128)(2,1)S(1)} custom-call(s32[16]{0:T(128)S(1)} %copy-done.1, bf16[1,1024]{1,0:T(2,128)(2,1)S(1)} %copy-done.6, f32[1,1024]{1,0:T(1,128)S(1)} %bitcast.11, bf16[100,1024]{1,0:T(8,128)(2,1)S(1)} %bitcast.9, bf16[256,1024]{1,0:T(8,128)(2,1)S(1)} %collective-permute-done.first, ...), custom_call_target="tpu_custom_call" | custom-call | flops 4831838208 | bytes 10485760 | tf_op jit(solution)/shard_map/edge_blocks/pallas_call | solution.py:337
  40.8 0.1 collective-permute-start.2
  40.9 0.0 collective-permute-done.3.refs_1_
  40.9 0.0 copy-done
  40.9 1.7 %score.2 = (bf16[100,1024]{1,0:T(8,128)(2,1)}, f32[100,1024]{1,0:T(8,128)}, f32[100,1,1024]{2,1,0:T(1,128)}) custom-call(s32[16]{0:T(128)S(1)} %copy-done.1, bf16[100,512]{1,0:T(8,128)(2,1)S(1)} %get-tuple-element.18.refs_0_, bf16[100,512]{1,0:T(8,128)(2,1)S(1)} %collective-permute-done.3.refs_1_, f32[100,1024]{1,0:T(8,128)S(1)} %copy-done), custom_call_target="tpu_custom_call" | custom-call | flops 2048000 | bytes 1024000 | tf_op jit(solution)/shard_map/score/pallas_call | solution.py:259
  42.5 3.9 %collective-permute-done.2.refs_1_ = bf16[100,512]{1,0:T(8,128)(2,1)S(1)} collective-permute-done((bf16[100,512]{1,0:T(8,128)(2,1)S(1)}, bf16[100,512]{1,0:T(8,128)(2,1)S(1)}, u32[]{:S(2)}, u32[]{:S(2)}) %collective-permute-start.2) | collective-permute-done | bytes 102432 | tf_op jit(solution)/shard_map/ppermute | solution.py:332
  46.5 1.7 %score.3 = (bf16[100,1024]{1,0:T(8,128)(2,1)}, f32[100,1024]{1,0:T(8,128)}, f32[100,1,1024]{2,1,0:T(1,128)}) custom-call(s32[16]{0:T(128)S(1)} %copy-done.1, bf16[100,512]{1,0:T(8,128)(2,1)S(1)} %edge_blocks.1.refs_0_, bf16[100,512]{1,0:T(8,128)(2,1)S(1)} %collective-permute-done.2.refs_1_, ...), custom_call_target="tpu_custom_call", output_to_operand_aliasing={{0}: (4, {}), {1}: (5, {}), {2}: (6, {})} | custom-call | flops 2048000 | bytes 1024000 | tf_op jit(solution)/shard_map/score/pallas_call | solution.py:259
Async XLA Ops:
  0.6 2.8 %copy-start.1 = (s32[16]{0:T(128)S(1)}, s32[16]{0:T(128)}, u32[]{:S(2)}) copy-start(s32[16]{0:T(128)} %counts.7) | copy-start | bytes 196
  0.6 3.1 %copy-start.2 = (bf16[1024,3072]{1,0:T(8,128)(2,1)S(1)}, bf16[1024,3072]{1,0:T(8,128)(2,1)}, u32[]{:S(2)}) copy-start(bf16[1024,3072]{1,0:T(8,128)(2,1)} %w_qkv.3) | copy-start | bytes 18874372
  0.7 3.7 %copy-start.3 = (bf16[1,1024,1024]{2,1,0:T(8,128)(2,1)S(1)}, bf16[1,1024,1024]{2,1,0:T(8,128)(2,1)}, u32[]{:S(2)}) copy-start(bf16[1,1024,1024]{2,1,0:T(8,128)(2,1)} %param.8) | copy-start | bytes 6291460
  0.7 4.3 %copy-start.4 = (bf16[1024,1024]{1,0:T(8,128)(2,1)S(1)}, bf16[1024,1024]{1,0:T(8,128)(2,1)}, u32[]{:S(2)}) copy-start(bf16[1024,1024]{1,0:T(8,128)(2,1)} %w_proj.3) | copy-start | bytes 6291460
  0.7 4.3 %copy-start.5 = (bf16[1024,100]{0,1:T(8,128)(2,1)S(1)}, bf16[1024,100]{0,1:T(8,128)(2,1)}, u32[]{:S(2)}) copy-start(bf16[1024,100]{0,1:T(8,128)(2,1)} %param.13) | copy-start | bytes 614404
  0.7 4.3 %copy-start.6 = (bf16[1,1024]{1,0:T(2,128)(2,1)S(1)}, bf16[1,1024]{1,0:T(2,128)(2,1)}, u32[]{:S(2)}) copy-start(bf16[1,1024]{1,0:T(2,128)(2,1)} %pert.3) | copy-start | bytes 6148
  0.7 4.3 %copy-start.7 = (f32[1024]{0:T(1024)S(1)}, f32[1024]{0:T(1024)}, u32[]{:S(2)}) copy-start(f32[1024]{0:T(1024)} %param.10) | copy-start | bytes 12292
  2.1 24.6 %collective-permute-start = (bf16[256,1024]{1,0:T(8,128)(2,1)S(1)}, bf16[256,1024]{1,0:T(8,128)(2,1)S(1)}, u32[]{:S(2)}, u32[]{:S(2)}) collective-permute-start(bf16[256,1024]{1,0:T(8,128)(2,1)S(1)} %get-tuple-element.14), channel_id=1, source_target_pairs={{0,1},{2,3},{4,5},{6,7},{8,9},{10,11},{12,13},{14,15},{1,0},{3,2},... | collective-permute-start | bytes 1572872 | tf_op jit(solution)/shard_map/ppermute | solution.py:303
  2.6 24.1 %collective-permute-start.1 = (bf16[256,1024]{1,0:T(8,128)(2,1)S(1)}, bf16[256,1024]{1,0:T(8,128)(2,1)S(1)}, u32[]{:S(2)}, u32[]{:S(2)}) collective-permute-start(bf16[256,1024]{1,0:T(8,128)(2,1)S(1)} %get-tuple-element.15), channel_id=1, source_target_pairs={{1,2},{3,4},{5,6},{7,8},{9,10},{11,12},{13,14},{2,1},{4,3},{6,5},{... | collective-permute-start | bytes 1572872 | tf_op jit(solution)/shard_map/ppermute | solution.py:304
  23.6 17.2 %collective-permute-start.3 = (bf16[100,512]{1,0:T(8,128)(2,1)S(1)}, bf16[100,512]{1,0:T(8,128)(2,1)S(1)}, u32[]{:S(2)}, u32[]{:S(2)}) collective-permute-start(bf16[100,512]{1,0:T(8,128)(2,1)S(1)} %get-tuple-element.18.refs_0_), channel_id=1, source_target_pairs={{0,16},{16,0},{1,17},{17,1},{2,18},{18,2},{3,19},{19,3},{4,20},{20... | collective-permute-start | bytes 307208 | tf_op jit(solution)/shard_map/ppermute | solution.py:332
  26.7 14.2 %copy-start = (f32[100,1024]{1,0:T(8,128)S(1)}, f32[100,1024]{1,0:T(8,128)}, u32[]{:S(2)}) copy-start(f32[100,1024]{1,0:T(8,128)} %refs_2_.3) | copy-start | bytes 1228804
  40.8 5.7 %collective-permute-start.2 = (bf16[100,512]{1,0:T(8,128)(2,1)S(1)}, bf16[100,512]{1,0:T(8,128)(2,1)S(1)}, u32[]{:S(2)}, u32[]{:S(2)}) collective-permute-start(bf16[100,512]{1,0:T(8,128)(2,1)S(1)} %edge_blocks.1.refs_0_), channel_id=1, source_target_pairs={{0,16},{16,0},{1,17},{17,1},{2,18},{18,2},{3,19},{19,3},{4,20},{20... | collective-permute-start | bytes 307208 | tf_op jit(solution)/shard_map/ppermute | solution.py:332

commit v5 on v4

--- a/solution.py
+++ b/solution.py
@@ -45,7 +45,7 @@
     return jnp.where((iota((rows, LANES), 0) >= live) & (iota((rows, LANES), 1) == 0), 1.0, 0.0).astype(BF16)
 
 
-def attend_block(query, keys, values, flags, store, pairs):
+def attend_blocks(blocks, pairs):
     half = HALF_WINDOW
     row = iota((2 * half, half), 0) % half
     col = iota((2 * half, half), 1)
@@ -55,14 +55,24 @@
     ones = jnp.ones((3 * half, LANES), BF16)
     lane = iota((half, LANES), 1)
     first = lane < LANES // 2
-    for c in range(pairs):
+
+    def scores(block, c):
+        query, keys, _, flags, _, _ = block
         q = query(c)
         zero = jnp.zeros_like(q)
         both = jnp.concatenate([jnp.where(first, q, zero), jnp.where(first, zero, q)], axis=0)
         both = jnp.concatenate([both, bias], axis=1)
         k = jnp.concatenate([keys(c), flags], axis=1)
         s = lax.dot_general(both, k, (((1,), (1,)), ((), ())), preferred_element_type=F32)
-        s = jnp.concatenate([s[:, :half] + near, s[:, half : 2 * half], s[:, 2 * half :] + far], axis=1)
+        return jnp.concatenate([s[:, :half] + near, s[:, half : 2 * half], s[:, 2 * half :] + far], axis=1)
+
+    steps = [(block, c) for block in blocks for c in range(pairs)]
+    later = scores(*steps[0])
+    for n, (block, c) in enumerate(steps):
+        s = later
+        if n + 1 < len(steps):
+            later = scores(*steps[n + 1])
+        _, _, values, _, store, finish = block
         top = jnp.max(s, axis=1, keepdims=True)
         p = jnp.exp2((s - top) * LOG2E).astype(BF16)
         v = jnp.concatenate([values(c), ones], axis=1)
@@ -70,6 +80,8 @@
         num = jnp.where(first, o[:half, :LANES], o[half:, :LANES])
         den = jnp.where(first, o[:half, LANES:], o[half:, LANES:])
         store(c, (num / den).astype(BF16))
+        if c == pairs - 1:
+            finish()
 
 
 def decode(x, attended, w_proj, w_fields):
@@ -81,17 +93,17 @@
     return slice(c * LANES, (c + 1) * LANES)
 
 
-def attend_side(q, kv, flags, att, q_at, k_at, width):
+def block_of(q, kv, flags, att, q_at, k_at, width, finish):
     def store(c, value):
         att[:, cols(c)] = value
 
-    attend_block(
+    return (
         lambda c: q[q_at, cols(c)],
         lambda c: kv[k_at, cols(c)],
         lambda c: kv[k_at, slice(width + c * LANES, width + (c + 1) * LANES)],
         flags,
         store,
-        width // LANES,
+        finish,
     )
 
 
@@ -123,8 +135,6 @@
     scale = channel_scale(gain, pert)
     normed[part(0), :] = normalize(x[part(0), :], scale)
     for b in range(blocks):
-        if b + 1 < blocks:
-            normed[part(b + 1), :] = normalize(x[part(b + 1), :], scale)
         here = normed[part(b), :]
         for n in range(3):
             res = jnp.dot(here, w_qkv[:, n * width : (n + 1) * width], preferred_element_type=F32).astype(BF16)
@@ -136,59 +146,78 @@
                 q_edge[half:, :] = res * head_scale
             else:
                 q_in[part(b - 1), :] = res * head_scale
-
-    def block(b, _):
-        start = pl.multiple_of(b * half, half)
-        attend_side(
-            q_in, kv, dead_flags(3 * half, own - start), att, pl.ds(start, half), pl.ds(start, 3 * half), width
-        )
-        rest = x[pl.ds(pl.multiple_of(start + half, half), half), :]
-        fields = decode(rest, att[...], w_proj[...], w_fields[...])
-        live = iota(fields.shape, 1) + start + half < own
-        out[:, pl.ds(start, half)] = jnp.where(live, fields, 0.0).astype(BF16)
-        return 0
-
-    lax.fori_loop(0, blocks - 2, block, 0)
+            if n == 0 and b + 1 < blocks:
+                normed[part(b + 1), :] = normalize(x[part(b + 1), :], scale)
+
+    def block(b):
+        start = b * half
+
+        def finish():
+            fields = decode(x[part(b + 1), :], att[b % 2], w_proj[...], w_fields[...])
+            live = iota(fields.shape, 1) + start + half < own
+            out[:, part(b)] = jnp.where(live, fields, 0.0).astype(BF16)
+
+        window = slice(start, start + 3 * half)
+        return block_of(q_in, kv, dead_flags(3 * half, own - start), att.at[b % 2], part(b), window, width, finish)
+
+    attend_blocks([block(b) for b in range(blocks - 2)], width // LANES)
 
 
 def edge_kernel(
-    counts, pert, gain, w_fields, first, second, x, w_qkv, w_proj, q_edge, kv_own, out, normed, kv, flags, att,
+    side, counts, pert, gain, w_fields, first, second, x, w_qkv, w_proj, q_edge, kv, *rest,
 ):
+    *done, out, normed, halo, att = rest
     rows, width = x.shape
     half = HALF_WINDOW
     place = lax.axis_index("node")
     shards = counts.shape[0]
     own = counts[place]
-    low_live = jnp.where(place > 0, counts[jnp.maximum(place - 1, 0)], 0)
-    high_live = jnp.where(place < shards - 1, counts[jnp.minimum(place + 1, shards - 1)], 0)
+    odd = lax.rem(place, 2)
     scale = channel_scale(gain, pert)
-    odd = lax.rem(place, 2)
-    far = rows + half
-    first_at = pl.ds(pl.multiple_of((1 - odd) * far, half), half)
-    second_at = pl.ds(pl.multiple_of(odd * far, half), half)
-    normed[:half, :] = normalize(first[...], scale)
-    normed[half:, :] = normalize(second[...], scale)
+    mine = jnp.where(odd == 1 - side, first[...].astype(F32), second[...].astype(F32))
+    normed[...] = normalize(mine, scale)
     for n in range(2):
+        at = slice(n * width, (n + 1) * width)
         w = w_qkv[:, (n + 1) * width : (n + 2) * width]
-        at = slice(n * width, (n + 1) * width)
-        kv[first_at, at] = jnp.dot(normed[:half, :], w, preferred_element_type=F32).astype(BF16)
-        kv[second_at, at] = jnp.dot(normed[half:, :], w, preferred_element_type=F32).astype(BF16)
-    kv[half:far, :] = kv_own[...]
-    flags[:half, :] = dead_flags(half, low_live - (rows - half))
-    flags[half:far, :] = dead_flags(rows, own)
-    flags[far:, :] = dead_flags(half, high_live)
-
-    def side(b, _):
-        here = pl.ds(pl.multiple_of(b * half, half), half)
-        start = pl.multiple_of(b * (rows - half), half)
-        window = pl.ds(start, 3 * half)
-        attend_side(q_edge, kv, flags[window, :], att, here, window, width)
-        fields = decode(x[pl.ds(start, half), :], att[...], w_proj[...], w_fields[...])
+        halo[:, at] = jnp.dot(normed[...], w, preferred_element_type=F32).astype(BF16)
+    if side == 0:
+        near = slice(0, 2 * half)
+        there = jnp.where(place > 0, counts[jnp.maximum(place - 1, 0)], 0) - (rows - half)
+        flags = [dead_flags(half, there), dead_flags(2 * half, own)]
+    else:
+        near = slice(rows - 2 * half, rows)
+        there = jnp.where(place < shards - 1, counts[jnp.minimum(place + 1, shards - 1)], 0)
+        flags = [dead_flags(2 * half, own - (rows - 2 * half)), dead_flags(half, there)]
+    start = side * (rows - half)
+    here = slice(side * half, (side + 1) * half)
+
+    def window(c):
+        parts = [halo[:, cols(c)], kv[near, cols(c)]]
+        return jnp.concatenate(parts if side == 0 else parts[::-1], axis=0)
+
+    def store(c, value):
+        att[:, cols(c)] = value
+
+    def finish():
+        fields = decode(x[start : start + half, :], att[...], w_proj[...], w_fields[...])
         live = iota(fields.shape, 1) + start < own
-        out[:, here] = jnp.where(live, fields, 0.0).astype(BF16)
-        return 0
-
-    lax.fori_loop(0, 2, side, 0)
+        out[:, :half] = jnp.where(live, fields, 0.0).astype(BF16)
+
+    if done:
+        out[:, half:] = done[0][...]
+    attend_blocks(
+        [
+            (
+                lambda c: q_edge[here, cols(c)],
+                window,
+                lambda c: window(c + width // LANES),
+                jnp.concatenate(flags, axis=0),
+                store,
+                finish,
+            )
+        ],
+        width // LANES,
+    )
 
 
 def score_values(mine, others, truth, live):
@@ -316,7 +345,7 @@
         scratch_shapes=[
             pltpu.VMEM((rows, width), BF16),
             pltpu.VMEM((inner, width), BF16),
-            pltpu.VMEM((half, width), BF16),
+            pltpu.VMEM((2, half, width), BF16),
         ],
         compiler_params=pltpu.CompilerParams(vmem_limit_bytes=KERNEL_VMEM),
         cost_estimate=pl.CostEstimate(
@@ -333,29 +362,32 @@
             for s in range(1, members)
         ]
 
-    others_in = exchange(pred_in)
-    pred_edge = pl.pallas_call(
-        edge_kernel,
-        in_specs=[SMEM] + [VMEM] * 10,
-        out_specs=VMEM,
-        out_shape=jax.ShapeDtypeStruct((fields, 2 * half), BF16),
-        scratch_shapes=[
-            pltpu.VMEM((2 * half, width), BF16),
-            pltpu.VMEM((rows + 2 * half, 2 * width), BF16),
-            pltpu.VMEM((rows + 2 * half, LANES), BF16),
-            pltpu.VMEM((half, width), BF16),
-        ],
-        compiler_params=pltpu.CompilerParams(vmem_limit_bytes=KERNEL_VMEM),
-        cost_estimate=pl.CostEstimate(
-            flops=2 * 2 * half * width * 3 * width + 12 * 2 * half * width * half,
-            bytes_accessed=10 * width * width,
-            transcendentals=2 * half * HEADS * 3 * half,
-        ),
-        name="edge_blocks",
-    )(counts, pert, gain, w_fields, first, second, x, w_qkv, w_proj, q_edge, kv)
-    others_edge = exchange(pred_edge)
-    partial = score_call(counts, pred_in, others_in, truth, [], list(range(1, blocks - 1)))
-    pred, score, deriv = score_call(counts, pred_edge, others_edge, truth, partial, [0, blocks - 1])
+    def edge(side, *done):
+        return pl.pallas_call(
+            functools.partial(edge_kernel, side),
+            in_specs=[SMEM] + [VMEM] * (10 + len(done)),
+            out_specs=VMEM,
+            out_shape=jax.ShapeDtypeStruct((fields, half + sum(d.shape[1] for d in done)), BF16),
+            scratch_shapes=[
+                pltpu.VMEM((half, width), BF16),
+                pltpu.VMEM((half, 2 * width), BF16),
+                pltpu.VMEM((half, width), BF16),
+            ],
+            compiler_params=pltpu.CompilerParams(vmem_limit_bytes=KERNEL_VMEM),
+            cost_estimate=pl.CostEstimate(
+                flops=2 * half * width * 3 * width + 12 * half * width * half,
+                bytes_accessed=10 * width * width,
+                transcendentals=half * HEADS * 3 * half,
+            ),
+            name="edge_block",
+        )(counts, pert, gain, w_fields, first, second, x, w_qkv, w_proj, q_edge, kv, *done)
+
+    pred_most = edge(0, pred_in)
+    others_most = exchange(pred_most)
+    pred_last = edge(1)
+    others_last = exchange(pred_last)
+    partial = score_call(counts, pred_most, others_most, truth, [], list(range(blocks - 1)))
+    pred, score, deriv = score_call(counts, pred_last, others_last, truth, partial, [blocks - 1])
     return pred[None], score, deriv.transpose(1, 0, 2)
 
 

time: 48.5 us -> 45.9 us (0.946)
  waiting for transfers between devices: 3.94 us -> 2.58 us
  Pallas kernels: 37.4 us -> 36.1 us
    ppermute x2, waiting for transfers between devices: 3.93 us -> 2.57 us  [exchange(): lax.ppermute(part, 'ens', [(i, (i + s) % members) for i in range(members)])]
    pallas_call x1, Pallas kernels: 18.7 us -> 17.5 us  [on_device(): pl.pallas_call(inner_kernel, in_specs=[SMEM] + [VMEM] * 6, out_specs=[VME...]
    pallas_call x1 -> x2, Pallas kernels: 14 us -> 14 us  [edge(): pl.pallas_call(functools.partial(edge_kernel, side), in_specs=[SMEM] + [V...]
  transfers between devices with their start and end apart: 4 -> 4, of which waited for: 1 -> 1; matrix products, arithmetic and copies ran while one was open for 0% -> 0% of each run, Pallas kernels for 71% -> 58%
where the time goes in v5:
time: 45.9 us; the launch traced here: 45.7 us
  Pallas kernels  36.1 us (79%)
  starting transfers between devices  4.51 us (10%)
  waiting for transfers between devices  2.58 us (6%)
  local copies, waits for them, and re-layouts  1.52 us (3%)
  between operations  0.96 us (2%)
    pallas_call x1, Pallas kernels, on_device(): pl.pallas_call(inner_kernel, in_specs=[SMEM] + [VMEM] * 6, out_specs=[VME...  17.5 us
    pallas_call x2, Pallas kernels, edge(): pl.pallas_call(functools.partial(edge_kernel, side), in_specs=[SMEM] + [V...  14 us
    pallas_call x2, Pallas kernels, score_call(): pl.pallas_call(functools.partial(score_kernel, count, len(carried), place...  3.3 us
    ppermute x2, starting transfers between devices, exchange(): lax.ppermute(part, 'ens', [(i, (i + s) % members) for i in range(members)])  3.14 us
    ppermute x2, waiting for transfers between devices, exchange(): lax.ppermute(part, 'ens', [(i, (i + s) % members) for i in range(members)])  2.57 us
    unnamed x16, local copies, waits for them, and re-layouts  1.52 us
    pallas_call x1, Pallas kernels, on_device(): pl.pallas_call(facing_kernel, in_specs=[ANY], out_specs=[VMEM] * 2, out_s...  1.38 us
  transfers between devices with their start and end apart: 4, of which 1 were waited for; matrix products, arithmetic and copies ran while one was open for 0% of the time, Pallas kernels for 58%

profile of v5, /device:TPU:0, one launch (start us, length us, event | category | flops | bytes accessed | tf_op | source)
XLA Modules:
  0.0 45.7 jit_solution(6271820856460125603)
XLA Ops:
  0.6 0.0 copy-start
  0.6 0.0 copy-start.1
  0.7 0.0 copy-start.2
  0.7 0.0 copy-start.4
  0.7 0.0 copy-start.5
  0.7 0.0 copy-start.6
  0.7 0.0 copy-start.7
  0.7 1.4 %facing.1 = (bf16[256,1024]{1,0:T(8,128)(2,1)S(1)}, bf16[256,1024]{1,0:T(8,128)(2,1)S(1)}) custom-call(bf16[1024,1024]{1,0:T(8,128)(2,1)} %bitcast.5), custom_call_target="tpu_custom_call" | custom-call | flops 8000000000 | bytes 1048576 | tf_op jit(solution)/shard_map/facing/pallas_call | solution.py:322
  2.1 0.6 %collective-permute-start = (bf16[256,1024]{1,0:T(8,128)(2,1)S(1)}, bf16[256,1024]{1,0:T(8,128)(2,1)S(1)}, u32[]{:S(2)}, u32[]{:S(2)}) collective-permute-start(bf16[256,1024]{1,0:T(8,128)(2,1)S(1)} %get-tuple-element.14), channel_id=1, source_target_pairs={{0,1},{2,3},{4,5},{6,7},{8,9},{10,11},{12,13},{14,15},{1,0},{3,2},... | collective-permute-start | bytes 1572872 | tf_op jit(solution)/shard_map/ppermute | solution.py:332
  2.6 0.8 %collective-permute-start.1 = (bf16[256,1024]{1,0:T(8,128)(2,1)S(1)}, bf16[256,1024]{1,0:T(8,128)(2,1)S(1)}, u32[]{:S(2)}, u32[]{:S(2)}) collective-permute-start(bf16[256,1024]{1,0:T(8,128)(2,1)S(1)} %get-tuple-element.15), channel_id=1, source_target_pairs={{1,2},{3,4},{5,6},{7,8},{9,10},{11,12},{13,14},{2,1},{4,3},{6,5},{... | collective-permute-start | bytes 1572872 | tf_op jit(solution)/shard_map/ppermute | solution.py:333
  3.5 0.3 copy-done
  3.7 0.6 %copy-done.1 = bf16[1,1024,1024]{2,1,0:T(8,128)(2,1)S(1)} copy-done((bf16[1,1024,1024]{2,1,0:T(8,128)(2,1)S(1)}, bf16[1,1024,1024]{2,1,0:T(8,128)(2,1)}, u32[]{:S(2)}) %copy-start.1) | copy-done | bytes 2097176
  4.4 0.6 %copy-done.2 = bf16[1024,1024]{1,0:T(8,128)(2,1)S(1)} copy-done((bf16[1024,1024]{1,0:T(8,128)(2,1)S(1)}, bf16[1024,1024]{1,0:T(8,128)(2,1)}, u32[]{:S(2)}) %copy-start.2) | copy-done | bytes 2097176
  5.0 0.0 copy-done.4
  5.0 0.0 copy-done.5
  5.0 0.0 copy-done.6
  5.0 0.0 copy-done.7
  5.0 17.5 %inner_blocks.1 = (bf16[100,512]{1,0:T(8,128)(2,1)S(1)}, bf16[512,1024]{1,0:T(8,128)(2,1)S(1)}, bf16[1024,2048]{1,0:T(8,128)(2,1)S(1)}) custom-call(s32[16]{0:T(128)S(1)} %copy-done.7, bf16[1024,1024]{1,0:T(8,128)(2,1)S(1)} %bitcast.6, bf16[1,1024]{1,0:T(2,128)(2,1)S(1)} %copy-done.5, f32[1,1024]{1,0:T(1,128)S(1)} %bitcast.12, ...), custom_call_target="tpu_custom_call" | custom-call | flops 9126805504 | bytes 10485760 | tf_op jit(solution)/shard_map/inner_blocks/pallas_call | solution.py:336
  22.4 0.0 collective-permute-done.first
  22.5 0.0 collective-permute-done.1.second
  22.5 6.9 %edge_block.3.refs_0_ = bf16[100,768]{1,0:T(8,128)(2,1)S(1)} custom-call(s32[16]{0:T(128)S(1)} %copy-done.7, bf16[1,1024]{1,0:T(2,128)(2,1)S(1)} %copy-done.5, f32[1,1024]{1,0:T(1,128)S(1)} %bitcast.13, bf16[100,1024]{1,0:T(8,128)(2,1)S(1)} %bitcast.10, bf16[256,1024]{1,0:T(8,128)(2,1)S(1)} %collective-permute-done.first, ...), custom_call_target="tpu_custom_call" | custom-call | flops 2415919104 | bytes 10485760 | tf_op jit(solution)/shard_map/edge_block/pallas_call | solution.py:366
  29.3 0.0 copy-start.3
  29.4 3.1 %collective-permute-start.3 = (bf16[100,768]{1,0:T(8,128)(2,1)S(1)}, bf16[100,768]{1,0:T(8,128)(2,1)S(1)}, u32[]{:S(2)}, u32[]{:S(2)}) collective-permute-start(bf16[100,768]{1,0:T(8,128)(2,1)S(1)} %edge_block.3.refs_0_), channel_id=1, source_target_pairs={{0,16},{16,0},{1,17},{17,1},{2,18},{18,2},{3,19},{19,3},{4,20},{20... | collective-permute-start | bytes 460808 | tf_op jit(solution)/shard_map/ppermute | solution.py:361
  32.4 7.1 %edge_block.2.refs_0_ = bf16[100,256]{1,0:T(8,128)(2,1)S(1)} custom-call(s32[16]{0:T(128)S(1)} %copy-done.7, bf16[1,1024]{1,0:T(2,128)(2,1)S(1)} %copy-done.5, f32[1,1024]{1,0:T(1,128)S(1)} %bitcast.14, bf16[100,1024]{1,0:T(8,128)(2,1)S(1)} %bitcast.11, bf16[256,1024]{1,0:T(8,128)(2,1)S(1)} %collective-permute-done.first, ...), custom_call_target="tpu_custom_call" | custom-call | flops 2415919104 | bytes 10485760 | tf_op jit(solution)/shard_map/edge_block/pallas_call | solution.py:366
  39.5 0.1 collective-permute-start.2
  39.6 0.0 collective-permute-done.3.refs_1_
  39.6 0.0 copy-done.3
  39.6 1.9 %score.2 = (bf16[100,1024]{1,0:T(8,128)(2,1)}, f32[100,1024]{1,0:T(8,128)}, f32[100,1,1024]{2,1,0:T(1,128)}) custom-call(s32[16]{0:T(128)S(1)} %copy-done.7, bf16[100,768]{1,0:T(8,128)(2,1)S(1)} %edge_block.3.refs_0_, bf16[100,768]{1,0:T(8,128)(2,1)S(1)} %collective-permute-done.3.refs_1_, f32[100,1024]{1,0:T(8,128)S(1)} %copy-done.3), custom_call_target="tpu_custom_call" | custom-call | flops 3072000 | bytes 1536000 | tf_op jit(solution)/shard_map/score/pallas_call | solution.py:288
  41.5 2.6 %collective-permute-done.2.refs_1_ = bf16[100,256]{1,0:T(8,128)(2,1)S(1)} collective-permute-done((bf16[100,256]{1,0:T(8,128)(2,1)S(1)}, bf16[100,256]{1,0:T(8,128)(2,1)S(1)}, u32[]{:S(2)}, u32[]{:S(2)}) %collective-permute-start.2) | collective-permute-done | bytes 51232 | tf_op jit(solution)/shard_map/ppermute | solution.py:361
  44.1 1.4 %score.3 = (bf16[100,1024]{1,0:T(8,128)(2,1)}, f32[100,1024]{1,0:T(8,128)}, f32[100,1,1024]{2,1,0:T(1,128)}) custom-call(s32[16]{0:T(128)S(1)} %copy-done.7, bf16[100,256]{1,0:T(8,128)(2,1)S(1)} %edge_block.2.refs_0_, bf16[100,256]{1,0:T(8,128)(2,1)S(1)} %collective-permute-done.2.refs_1_, ...), custom_call_target="tpu_custom_call", output_to_operand_aliasing={{0}: (4, {}), {1}: (5, {}), {2}: (6, {})} | custom-call | flops 1024000 | bytes 512000 | tf_op jit(solution)/shard_map/score/pallas_call | solution.py:288
Async XLA Ops:
  0.6 3.1 %copy-start = (bf16[1024,3072]{1,0:T(8,128)(2,1)S(1)}, bf16[1024,3072]{1,0:T(8,128)(2,1)}, u32[]{:S(2)}) copy-start(bf16[1024,3072]{1,0:T(8,128)(2,1)} %w_qkv.5) | copy-start | bytes 18874372
  0.6 3.7 %copy-start.1 = (bf16[1,1024,1024]{2,1,0:T(8,128)(2,1)S(1)}, bf16[1,1024,1024]{2,1,0:T(8,128)(2,1)}, u32[]{:S(2)}) copy-start(bf16[1,1024,1024]{2,1,0:T(8,128)(2,1)} %param.8) | copy-start | bytes 6291460
  0.7 4.3 %copy-start.2 = (bf16[1024,1024]{1,0:T(8,128)(2,1)S(1)}, bf16[1024,1024]{1,0:T(8,128)(2,1)}, u32[]{:S(2)}) copy-start(bf16[1024,1024]{1,0:T(8,128)(2,1)} %w_proj.5) | copy-start | bytes 6291460
  0.7 4.3 %copy-start.4 = (bf16[1024,100]{0,1:T(8,128)(2,1)S(1)}, bf16[1024,100]{0,1:T(8,128)(2,1)}, u32[]{:S(2)}) copy-start(bf16[1024,100]{0,1:T(8,128)(2,1)} %param.13) | copy-start | bytes 614404
  0.7 4.3 %copy-start.5 = (bf16[1,1024]{1,0:T(2,128)(2,1)S(1)}, bf16[1,1024]{1,0:T(2,128)(2,1)}, u32[]{:S(2)}) copy-start(bf16[1,1024]{1,0:T(2,128)(2,1)} %pert.5) | copy-start | bytes 6148
  0.7 4.3 %copy-start.6 = (f32[1024]{0:T(1024)S(1)}, f32[1024]{0:T(1024)}, u32[]{:S(2)}) copy-start(f32[1024]{0:T(1024)} %param.10) | copy-start | bytes 12292
  0.7 4.3 %copy-start.7 = (s32[16]{0:T(128)S(1)}, s32[16]{0:T(128)}, u32[]{:S(2)}) copy-start(s32[16]{0:T(128)} %counts.9) | copy-start | bytes 196
  2.1 20.4 %collective-permute-start = (bf16[256,1024]{1,0:T(8,128)(2,1)S(1)}, bf16[256,1024]{1,0:T(8,128)(2,1)S(1)}, u32[]{:S(2)}, u32[]{:S(2)}) collective-permute-start(bf16[256,1024]{1,0:T(8,128)(2,1)S(1)} %get-tuple-element.14), channel_id=1, source_target_pairs={{0,1},{2,3},{4,5},{6,7},{8,9},{10,11},{12,13},{14,15},{1,0},{3,2},... | collective-permute-start | bytes 1572872 | tf_op jit(solution)/shard_map/ppermute | solution.py:332
  2.6 19.8 %collective-permute-start.1 = (bf16[256,1024]{1,0:T(8,128)(2,1)S(1)}, bf16[256,1024]{1,0:T(8,128)(2,1)S(1)}, u32[]{:S(2)}, u32[]{:S(2)}) collective-permute-start(bf16[256,1024]{1,0:T(8,128)(2,1)S(1)} %get-tuple-element.15), channel_id=1, source_target_pairs={{1,2},{3,4},{5,6},{7,8},{9,10},{11,12},{13,14},{2,1},{4,3},{6,5},{... | collective-permute-start | bytes 1572872 | tf_op jit(solution)/shard_map/ppermute | solution.py:333
  29.3 10.3 %copy-start.3 = (f32[100,1024]{1,0:T(8,128)S(1)}, f32[100,1024]{1,0:T(8,128)}, u32[]{:S(2)}) copy-start(f32[100,1024]{1,0:T(8,128)} %refs_2_.3) | copy-start | bytes 1228804
  29.4 10.3 %collective-permute-start.3 = (bf16[100,768]{1,0:T(8,128)(2,1)S(1)}, bf16[100,768]{1,0:T(8,128)(2,1)S(1)}, u32[]{:S(2)}, u32[]{:S(2)}) collective-permute-start(bf16[100,768]{1,0:T(8,128)(2,1)S(1)} %edge_block.3.refs_0_), channel_id=1, source_target_pairs={{0,16},{16,0},{1,17},{17,1},{2,18},{18,2},{3,19},{19,3},{4,20},{20... | collective-permute-start | bytes 460808 | tf_op jit(solution)/shard_map/ppermute | solution.py:361
  39.5 4.6 %collective-permute-start.2 = (bf16[100,256]{1,0:T(8,128)(2,1)S(1)}, bf16[100,256]{1,0:T(8,128)(2,1)S(1)}, u32[]{:S(2)}, u32[]{:S(2)}) collective-permute-start(bf16[100,256]{1,0:T(8,128)(2,1)S(1)} %edge_block.2.refs_0_), channel_id=1, source_target_pairs={{0,16},{16,0},{1,17},{17,1},{2,18},{18,2},{3,19},{19,3},{4,20},{20... | collective-permute-start | bytes 153608 | tf_op jit(solution)/shard_map/ppermute | solution.py:361

commit v6 on v5

--- a/solution.py
+++ b/solution.py
@@ -21,7 +21,6 @@
 F32 = jnp.float32
 BF16 = jnp.bfloat16
 VMEM = pl.BlockSpec(memory_space=pltpu.VMEM)
-SMEM = pl.BlockSpec(memory_space=pltpu.SMEM)
 ANY = pl.BlockSpec(memory_space=pl.ANY)
 
 
@@ -47,12 +46,14 @@
 
 def attend_blocks(blocks, pairs):
     half = HALF_WINDOW
-    row = iota((2 * half, half), 0) % half
-    col = iota((2 * half, half), 1)
+    sub = half // 2
+    row = iota((sub, sub), 0)
+    col = iota((sub, sub), 1)
     near = jnp.where(col >= row, 0.0, NEG)
     far = jnp.where(col < row, 0.0, NEG)
     bias = jnp.where(iota((2 * half, LANES), 1) == 0, NEG, 0.0).astype(BF16)
     ones = jnp.ones((3 * half, LANES), BF16)
+    outside = jnp.zeros((sub, sub), BF16)
     lane = iota((half, LANES), 1)
     first = lane < LANES // 2
 
@@ -63,8 +64,17 @@
         both = jnp.concatenate([jnp.where(first, q, zero), jnp.where(first, zero, q)], axis=0)
         both = jnp.concatenate([both, bias], axis=1)
         k = jnp.concatenate([keys(c), flags], axis=1)
-        s = lax.dot_general(both, k, (((1,), (1,)), ((), ())), preferred_element_type=F32)
-        return jnp.concatenate([s[:, :half] + near, s[:, half : 2 * half], s[:, 2 * half :] + far], axis=1)
+        return lax.dot_general(both, k, (((1,), (1,)), ((), ())), preferred_element_type=F32)
+
+    def weights(s):
+        groups = []
+        for g in range(4):
+            t = s[g * sub : (g + 1) * sub, (g % 2) * sub : (g % 2) * sub + 5 * sub]
+            t = jnp.concatenate([t[:, :sub] + near, t[:, sub : 4 * sub], t[:, 4 * sub :] + far], axis=1)
+            top = jnp.max(t, axis=1, keepdims=True)
+            p = jnp.exp2((t - top) * LOG2E).astype(BF16)
+            groups.append(jnp.concatenate([p, outside] if g % 2 == 0 else [outside, p], axis=1))
+        return jnp.concatenate(groups, axis=0)
 
     steps = [(block, c) for block in blocks for c in range(pairs)]
     later = scores(*steps[0])
@@ -73,10 +83,8 @@
         if n + 1 < len(steps):
             later = scores(*steps[n + 1])
         _, _, values, _, store, finish = block
-        top = jnp.max(s, axis=1, keepdims=True)
-        p = jnp.exp2((s - top) * LOG2E).astype(BF16)
         v = jnp.concatenate([values(c), ones], axis=1)
-        o = jnp.dot(p, v, preferred_element_type=F32)
+        o = jnp.dot(weights(s), v, preferred_element_type=F32)
         num = jnp.where(first, o[:half, :LANES], o[half:, :LANES])
         den = jnp.where(first, o[:half, LANES:], o[half:, LANES:])
         store(c, (num / den).astype(BF16))
@@ -122,11 +130,23 @@
         c.wait()
 
 
-def inner_kernel(counts, x, pert, gain, w_fields, w_qkv, w_proj, out, q_edge, kv, normed, q_in, att):
+def inner_kernel(
+    counts, x, pert, gain, w_fields, w_qkv, w_proj, out, q_edge, kv, flags, alive, normed, q_in, att,
+):
     rows, width = x.shape
     half = HALF_WINDOW
     blocks = rows // half
-    own = counts[lax.axis_index("node")]
+    place = lax.axis_index("node")
+    shard = iota(counts.shape, 1)
+
+    def count(at):
+        return jnp.sum(jnp.where(shard == at, counts[...], 0), axis=1, keepdims=True)
+
+    own, low_live, high_live = count(place), count(place - 1), count(place + 1)
+    flags[:half, :] = dead_flags(half, low_live - (rows - half))
+    flags[half : half + rows, :] = dead_flags(rows, own)
+    flags[half + rows :, :] = dead_flags(half, high_live)
+    alive[...] = jnp.where(iota(alive.shape, 1) < own, 1.0, 0.0)
     head_scale = jnp.asarray((width // HEADS) ** -0.5, BF16)
 
     def part(b):
@@ -164,30 +184,30 @@
 
 
 def edge_kernel(
-    side, counts, pert, gain, w_fields, first, second, x, w_qkv, w_proj, q_edge, kv, *rest,
+    side, alive, flags, w_fields, x, w_proj, q_edge, kv, *refs,
 ):
-    *done, out, normed, halo, att = rest
     rows, width = x.shape
     half = HALF_WINDOW
-    place = lax.axis_index("node")
-    shards = counts.shape[0]
-    own = counts[place]
-    odd = lax.rem(place, 2)
-    scale = channel_scale(gain, pert)
-    mine = jnp.where(odd == 1 - side, first[...].astype(F32), second[...].astype(F32))
-    normed[...] = normalize(mine, scale)
-    for n in range(2):
-        at = slice(n * width, (n + 1) * width)
-        w = w_qkv[:, (n + 1) * width : (n + 2) * width]
-        halo[:, at] = jnp.dot(normed[...], w, preferred_element_type=F32).astype(BF16)
     if side == 0:
+        pert, gain, first, second, w_qkv, done, out, halo_high, normed, halo, att = refs
+        odd = lax.rem(lax.axis_index("node"), 2)
+        scale = channel_scale(gain, pert)
+        low = jnp.where(odd == 1, first[...].astype(F32), second[...].astype(F32))
+        normed[:half, :] = normalize(low, scale)
+        for h, target in enumerate((halo, halo_high)):
+            for n in range(2):
+                at = slice(n * width, (n + 1) * width)
+                w = w_qkv[:, (n + 1) * width : (n + 2) * width]
+                rows_in = normed[h * half : (h + 1) * half, :]
+                target[:, at] = jnp.dot(rows_in, w, preferred_element_type=F32).astype(BF16)
+                if h == 0 and n == 0:
+                    high = jnp.where(odd == 1, second[...].astype(F32), first[...].astype(F32))
+                    normed[half:, :] = normalize(high, scale)
         near = slice(0, 2 * half)
-        there = jnp.where(place > 0, counts[jnp.maximum(place - 1, 0)], 0) - (rows - half)
-        flags = [dead_flags(half, there), dead_flags(2 * half, own)]
+        out[:, half:] = done[...]
     else:
+        halo, out, att = refs
         near = slice(rows - 2 * half, rows)
-        there = jnp.where(place < shards - 1, counts[jnp.minimum(place + 1, shards - 1)], 0)
-        flags = [dead_flags(2 * half, own - (rows - 2 * half)), dead_flags(half, there)]
     start = side * (rows - half)
     here = slice(side * half, (side + 1) * half)
 
@@ -200,18 +220,15 @@
 
     def finish():
         fields = decode(x[start : start + half, :], att[...], w_proj[...], w_fields[...])
-        live = iota(fields.shape, 1) + start < own
-        out[:, :half] = jnp.where(live, fields, 0.0).astype(BF16)
-
-    if done:
-        out[:, half:] = done[0][...]
+        out[:, :half] = jnp.where(alive[:, start : start + half] > 0.0, fields, 0.0).astype(BF16)
+
     attend_blocks(
         [
             (
                 lambda c: q_edge[here, cols(c)],
                 window,
                 lambda c: window(c + width // LANES),
-                jnp.concatenate(flags, axis=0),
+                flags[start : start + 3 * half, :],
                 store,
                 finish,
             )
@@ -250,12 +267,11 @@
     return jnp.where(live, score, 0.0), jnp.where(live, deriv, 0.0)
 
 
-def score_kernel(others, carried, places, counts, *refs):
+def score_kernel(others, carried, places, alive, *refs):
     mine, rest, truth = refs[0], refs[1 : 1 + others], refs[1 + others]
     pred, score, deriv = refs[2 + others + carried : 5 + others + carried]
     score_buf, deriv_buf, sem = refs[5 + others + carried :]
     half = HALF_WINDOW
-    own = counts[lax.axis_index("node")]
     moves = []
     for i, place in enumerate(places):
         here, there = slice(i * half, (i + 1) * half), slice(place * half, (place + 1) * half)
@@ -264,7 +280,7 @@
     for i, place in enumerate(places):
         here, there = slice(i * half, (i + 1) * half), slice(place * half, (place + 1) * half)
         f = mine[:, here]
-        live = iota(f.shape, 1) + place * half < own
+        live = alive[:, there] > 0.0
         score_buf[i], d = score_values(f, [r[:, here] for r in rest], truth[:, there], live)
         moves.append(pltpu.make_async_copy(score_buf.at[i], score.at[:, there], sem.at[1, i]))
         moves[-1].start()
@@ -275,7 +291,7 @@
         c.wait()
 
 
-def score_call(counts, mine, others, truth, carried, places):
+def score_call(alive, mine, others, truth, carried, places):
     half = HALF_WINDOW
     fields, nodes = truth.shape
     shapes = [
@@ -287,7 +303,7 @@
     parts = len(places)
     return pl.pallas_call(
         functools.partial(score_kernel, count, len(carried), places),
-        in_specs=[SMEM] + [VMEM] * (2 + count) + [ANY] * len(carried),
+        in_specs=[VMEM] * (3 + count) + [ANY] * len(carried),
         out_specs=[ANY] * 3,
         out_shape=shapes,
         scratch_shapes=[
@@ -301,7 +317,7 @@
             flops=40 * fields * half * parts, bytes_accessed=20 * fields * half * parts, transcendentals=0
         ),
         name="score",
-    )(counts, mine, *others, truth, *carried)
+    )(alive, mine, *others, truth, *carried)
 
 
 def neighbours(count, start):
@@ -333,14 +349,16 @@
     second = lax.ppermute(halves[1], "node", neighbours(shards, 1))
 
     inner = rows - 2 * half
-    pred_in, q_edge, kv = pl.pallas_call(
+    pred_in, q_edge, kv, flags, alive = pl.pallas_call(
         inner_kernel,
-        in_specs=[SMEM] + [VMEM] * 6,
-        out_specs=[VMEM] * 3,
+        in_specs=[VMEM] * 7,
+        out_specs=[VMEM] * 5,
         out_shape=[
             jax.ShapeDtypeStruct((fields, inner), BF16),
             jax.ShapeDtypeStruct((2 * half, width), BF16),
             jax.ShapeDtypeStruct((rows, 2 * width), BF16),
+            jax.ShapeDtypeStruct((rows + 2 * half, LANES), BF16),
+            jax.ShapeDtypeStruct((1, rows), F32),
         ],
         scratch_shapes=[
             pltpu.VMEM((rows, width), BF16),
@@ -354,7 +372,7 @@
             transcendentals=inner * HEADS * 3 * half,
         ),
         name="inner_blocks",
-    )(counts, x, pert, gain, w_fields, w_qkv, w_proj)
+    )(counts.reshape(1, -1), x, pert, gain, w_fields, w_qkv, w_proj)
 
     def exchange(part):
         return [
@@ -362,32 +380,34 @@
             for s in range(1, members)
         ]
 
-    def edge(side, *done):
+    def edge(side, out_shape, scratch, flops, *extra):
         return pl.pallas_call(
             functools.partial(edge_kernel, side),
-            in_specs=[SMEM] + [VMEM] * (10 + len(done)),
-            out_specs=VMEM,
-            out_shape=jax.ShapeDtypeStruct((fields, half + sum(d.shape[1] for d in done)), BF16),
-            scratch_shapes=[
-                pltpu.VMEM((half, width), BF16),
-                pltpu.VMEM((half, 2 * width), BF16),
-                pltpu.VMEM((half, width), BF16),
-            ],
+            in_specs=[VMEM] * (7 + len(extra)),
+            out_specs=[VMEM] * len(out_shape),
+            out_shape=[jax.ShapeDtypeStruct(shape, BF16) for shape in out_shape],
+            scratch_shapes=[pltpu.VMEM(shape, BF16) for shape in scratch],
             compiler_params=pltpu.CompilerParams(vmem_limit_bytes=KERNEL_VMEM),
             cost_estimate=pl.CostEstimate(
-                flops=2 * half * width * 3 * width + 12 * half * width * half,
+                flops=flops + 12 * half * width * half,
                 bytes_accessed=10 * width * width,
                 transcendentals=half * HEADS * 3 * half,
             ),
             name="edge_block",
-        )(counts, pert, gain, w_fields, first, second, x, w_qkv, w_proj, q_edge, kv, *done)
-
-    pred_most = edge(0, pred_in)
+        )(alive, flags, w_fields, x, w_proj, q_edge, kv, *extra)
+
+    pred_most, halo_high = edge(
+        0,
+        [(fields, rows - half), (half, 2 * width)],
+        [(2 * half, width), (half, 2 * width), (half, width)],
+        10 * half * width * width,
+        pert, gain, first, second, w_qkv, pred_in,
+    )
     others_most = exchange(pred_most)
-    pred_last = edge(1)
+    (pred_last,) = edge(1, [(fields, half)], [(half, width)], 2 * half * width * width, halo_high)
     others_last = exchange(pred_last)
-    partial = score_call(counts, pred_most, others_most, truth, [], list(range(blocks - 1)))
-    pred, score, deriv = score_call(counts, pred_last, others_last, truth, partial, [blocks - 1])
+    partial = score_call(alive, pred_most, others_most, truth, [], list(range(blocks - 1)))
+    pred, score, deriv = score_call(alive, pred_last, others_last, truth, partial, [blocks - 1])
     return pred[None], score, deriv.transpose(1, 0, 2)
 
 

time: 45.9 us -> 42.1 us (0.917)
  Pallas kernels: 36.1 us -> 31.8 us
  waiting for transfers between devices: 2.58 us -> 3.09 us
    pallas_call x3, Pallas kernels: 31.5 us -> 28.2 us  [the longest x1 16.1 us: on_device(): pl.pallas_call(inner_kernel, in_specs=[VMEM] * 7, out_specs=[VMEM] * 5, o...]
    pallas_call x2, Pallas kernels: 3.3 us -> 2.23 us  [score_call(): pl.pallas_call(functools.partial(score_kernel, count, len(carried), place...]
    ppermute x2, waiting for transfers between devices: 2.57 us -> 3.09 us  [exchange(): lax.ppermute(part, 'ens', [(i, (i + s) % members) for i in range(members)])]
  transfers between devices with their start and end apart: 4 -> 4, of which waited for: 1 -> 1; matrix products, arithmetic and copies ran while one was open for 0% -> 0% of each run, Pallas kernels for 58% -> 53%
where the time goes in v6:
time: 42.1 us; the launch traced here: 41.9 us
  Pallas kernels  31.8 us (76%)
  starting transfers between devices  4.52 us (11%)
  waiting for transfers between devices  3.09 us (7%)
  local copies, waits for them, and re-layouts  1.55 us (4%)
  between operations  0.95 us (2%)
    pallas_call x1, Pallas kernels, on_device(): pl.pallas_call(inner_kernel, in_specs=[VMEM] * 7, out_specs=[VMEM] * 5, o...  16.1 us
    pallas_call x2, Pallas kernels, edge(): pl.pallas_call(functools.partial(edge_kernel, side), in_specs=[VMEM] * (7...  12.1 us
    ppermute x2, starting transfers between devices, exchange(): lax.ppermute(part, 'ens', [(i, (i + s) % members) for i in range(members)])  3.15 us
    ppermute x2, waiting for transfers between devices, exchange(): lax.ppermute(part, 'ens', [(i, (i + s) % members) for i in range(members)])  3.09 us
    pallas_call x2, Pallas kernels, score_call(): pl.pallas_call(functools.partial(score_kernel, count, len(carried), place...  2.23 us
    unnamed x16, local copies, waits for them, and re-layouts  1.55 us
    pallas_call x1, Pallas kernels, on_device(): pl.pallas_call(facing_kernel, in_specs=[ANY], out_specs=[VMEM] * 2, out_s...  1.38 us
  transfers between devices with their start and end apart: 4, of which 1 were waited for; matrix products, arithmetic and copies ran while one was open for 0% of the time, Pallas kernels for 53%

profile of v6, /device:TPU:0, one launch (start us, length us, event | category | flops | bytes accessed | tf_op | source)
XLA Modules:
  0.0 41.9 jit_solution(16474640815838820923)
XLA Ops:
  0.6 0.0 copy-start
  0.6 0.0 copy-start.1
  0.7 0.0 copy-start.2
  0.7 0.0 copy-start.4
  0.7 0.0 copy-start.5
  0.7 0.0 copy-start.6
  0.7 0.0 copy-start.7
  0.7 1.4 %facing.1 = (bf16[256,1024]{1,0:T(8,128)(2,1)S(1)}, bf16[256,1024]{1,0:T(8,128)(2,1)S(1)}) custom-call(bf16[1024,1024]{1,0:T(8,128)(2,1)} %bitcast.6), custom_call_target="tpu_custom_call" | custom-call | flops 8000000000 | bytes 1048576 | tf_op jit(solution)/shard_map/facing/pallas_call | solution.py:338
  2.1 0.6 %collective-permute-start = (bf16[256,1024]{1,0:T(8,128)(2,1)S(1)}, bf16[256,1024]{1,0:T(8,128)(2,1)S(1)}, u32[]{:S(2)}, u32[]{:S(2)}) collective-permute-start(bf16[256,1024]{1,0:T(8,128)(2,1)S(1)} %get-tuple-element.22), channel_id=1, source_target_pairs={{0,1},{2,3},{4,5},{6,7},{8,9},{10,11},{12,13},{14,15},{1,0},{3,2},... | collective-permute-start | bytes 1572872 | tf_op jit(solution)/shard_map/ppermute | solution.py:348
  2.6 0.8 %collective-permute-start.1 = (bf16[256,1024]{1,0:T(8,128)(2,1)S(1)}, bf16[256,1024]{1,0:T(8,128)(2,1)S(1)}, u32[]{:S(2)}, u32[]{:S(2)}) collective-permute-start(bf16[256,1024]{1,0:T(8,128)(2,1)S(1)} %get-tuple-element.23), channel_id=1, source_target_pairs={{1,2},{3,4},{5,6},{7,8},{9,10},{11,12},{13,14},{2,1},{4,3},{6,5},{... | collective-permute-start | bytes 1572872 | tf_op jit(solution)/shard_map/ppermute | solution.py:349
  3.5 0.0 copy-done
  3.5 0.0 copy-done.1
  3.5 1.5 %copy-done.2 = bf16[1024,3072]{1,0:T(8,128)(2,1)S(1)} copy-done((bf16[1024,3072]{1,0:T(8,128)(2,1)S(1)}, bf16[1024,3072]{1,0:T(8,128)(2,1)}, u32[]{:S(2)}) %copy-start.2) | copy-done | bytes 6291480
  5.0 0.0 copy-done.4
  5.0 0.0 copy-done.5
  5.0 0.0 copy-done.6
  5.0 0.0 copy-done.7
  5.0 16.1 %inner_blocks.1 = (bf16[100,512]{1,0:T(8,128)(2,1)S(1)}, bf16[512,1024]{1,0:T(8,128)(2,1)S(1)}, bf16[1024,2048]{1,0:T(8,128)(2,1)S(1)}, bf16[1536,128]{1,0:T(8,128)(2,1)S(1)}, f32[1,1024]{1,0:T(1,128)S(1)}) custom-call(s32[1,16]{1,0:T(1,128)S(1)} %bitcast.15, bf16[1024,1024]{1,0:T(8,128)(2,1)S(1)} %bitcast.7, bf16[1,1024]{1,0:T(2,128)(2,1)S(1)} %copy-done.5, ...), custom_call_target="tpu_custom_call" | custom-call | flops 9126805504 | bytes 10485760 | tf_op jit(solution)/shard_map/inner_blocks/pallas_call | solution.py:352
  21.1 0.0 collective-permute-done.refs_2_
  21.1 0.0 collective-permute-done.1.refs_3_
  21.1 7.2 %edge_block.2 = (bf16[100,768]{1,0:T(8,128)(2,1)S(1)}, bf16[256,2048]{1,0:T(8,128)(2,1)S(1)}) custom-call(f32[1,1024]{1,0:T(1,128)S(1)} %get-tuple-element.18.alive, bf16[1536,128]{1,0:T(8,128)(2,1)S(1)} %get-tuple-element.19.flags, bf16[100,1024]{1,0:T(8,128)(2,1)S(1)} %bitcast.11, bf16[1024,1024]{1,0:T(8,128)(2,1)S(1)} %bitcast.8, ...), custom_call_target="tpu_custom_call" | custom-call | flops 3489660928 | bytes 10485760 | tf_op jit(solution)/shard_map/edge_block/pallas_call | solution.py:384
  28.3 3.1 %collective-permute-start.3 = (bf16[100,768]{1,0:T(8,128)(2,1)S(1)}, bf16[100,768]{1,0:T(8,128)(2,1)S(1)}, u32[]{:S(2)}, u32[]{:S(2)}) collective-permute-start(bf16[100,768]{1,0:T(8,128)(2,1)S(1)} %get-tuple-element.26.refs_0_), channel_id=1, source_target_pairs={{0,16},{16,0},{1,17},{17,1},{2,18},{18,2},{3,19},{19,3},{4,20},{20... | collective-permute-start | bytes 460808 | tf_op jit(solution)/shard_map/ppermute | solution.py:379
  31.4 0.0 copy-start.3
  31.4 4.9 %edge_block.3.refs_0_ = bf16[100,256]{1,0:T(8,128)(2,1)S(1)} custom-call(f32[1,1024]{1,0:T(1,128)S(1)} %get-tuple-element.18.alive, bf16[1536,128]{1,0:T(8,128)(2,1)S(1)} %get-tuple-element.19.flags, bf16[100,1024]{1,0:T(8,128)(2,1)S(1)} %bitcast.12, bf16[1024,1024]{1,0:T(8,128)(2,1)S(1)} %bitcast.9, bf16[1024,1024]{1,0:T(8,128)(2,1)S(1)} %copy-done.1, ...), custom_call_target="tpu_custom_call" | custom-call | flops 1342177280 | bytes 10485760 | tf_op jit(solution)/shard_map/edge_block/pallas_call | solution.py:384
  36.3 0.1 collective-permute-start.2
  36.4 0.0 collective-permute-done.3.refs_1_
  36.4 0.0 copy-done.3
  36.4 1.4 %score.2 = (bf16[100,1024]{1,0:T(8,128)(2,1)}, f32[100,1024]{1,0:T(8,128)}, f32[100,1,1024]{2,1,0:T(1,128)}) custom-call(f32[1,1024]{1,0:T(1,128)S(1)} %get-tuple-element.18.alive, bf16[100,768]{1,0:T(8,128)(2,1)S(1)} %get-tuple-element.26.refs_0_, bf16[100,768]{1,0:T(8,128)(2,1)S(1)} %collective-permute-done.3.refs_1_, f32[100,1024]{1,0:T(8,128)S(1)} %copy-done.3), custom_call_target="tpu_custom_call" | custom-call | flops 3072000 | bytes 1536000 | tf_op jit(solution)/shard_map/score/pallas_call | solution.py:304
  37.8 3.1 %collective-permute-done.2.refs_1_ = bf16[100,256]{1,0:T(8,128)(2,1)S(1)} collective-permute-done((bf16[100,256]{1,0:T(8,128)(2,1)S(1)}, bf16[100,256]{1,0:T(8,128)(2,1)S(1)}, u32[]{:S(2)}, u32[]{:S(2)}) %collective-permute-start.2) | collective-permute-done | bytes 51232 | tf_op jit(solution)/shard_map/ppermute | solution.py:379
  40.8 0.9 %score.3 = (bf16[100,1024]{1,0:T(8,128)(2,1)}, f32[100,1024]{1,0:T(8,128)}, f32[100,1,1024]{2,1,0:T(1,128)}) custom-call(f32[1,1024]{1,0:T(1,128)S(1)} %get-tuple-element.18.alive, bf16[100,256]{1,0:T(8,128)(2,1)S(1)} %edge_block.3.refs_0_, ...), custom_call_target="tpu_custom_call", output_to_operand_aliasing={{0}: (4, {}), {1}: (5, {}), {2}: (6, {})} | custom-call | flops 1024000 | bytes 512000 | tf_op jit(solution)/shard_map/score/pallas_call | solution.py:304
Async XLA Ops:
  0.6 2.8 %copy-start = (bf16[1,1024,1024]{2,1,0:T(8,128)(2,1)S(1)}, bf16[1,1024,1024]{2,1,0:T(8,128)(2,1)}, u32[]{:S(2)}) copy-start(bf16[1,1024,1024]{2,1,0:T(8,128)(2,1)} %param.8) | copy-start | bytes 6291460
  0.6 2.8 %copy-start.1 = (bf16[1024,1024]{1,0:T(8,128)(2,1)S(1)}, bf16[1024,1024]{1,0:T(8,128)(2,1)}, u32[]{:S(2)}) copy-start(bf16[1024,1024]{1,0:T(8,128)(2,1)} %w_proj.5) | copy-start | bytes 6291460
  0.7 4.4 %copy-start.2 = (bf16[1024,3072]{1,0:T(8,128)(2,1)S(1)}, bf16[1024,3072]{1,0:T(8,128)(2,1)}, u32[]{:S(2)}) copy-start(bf16[1024,3072]{1,0:T(8,128)(2,1)} %refs_4_.1) | copy-start | bytes 18874372
  0.7 4.3 %copy-start.4 = (bf16[1024,100]{0,1:T(8,128)(2,1)S(1)}, bf16[1024,100]{0,1:T(8,128)(2,1)}, u32[]{:S(2)}) copy-start(bf16[1024,100]{0,1:T(8,128)(2,1)} %param.13) | copy-start | bytes 614404
  0.7 4.3 %copy-start.5 = (bf16[1,1024]{1,0:T(2,128)(2,1)S(1)}, bf16[1,1024]{1,0:T(2,128)(2,1)}, u32[]{:S(2)}) copy-start(bf16[1,1024]{1,0:T(2,128)(2,1)} %refs_0_.1) | copy-start | bytes 6148
  0.7 4.3 %copy-start.6 = (f32[1024]{0:T(1024)S(1)}, f32[1024]{0:T(1024)}, u32[]{:S(2)}) copy-start(f32[1024]{0:T(1024)} %param.10) | copy-start | bytes 12292
  0.7 4.3 %copy-start.7 = (s32[16]{0:T(128)S(1)}, s32[16]{0:T(128)}, u32[]{:S(2)}) copy-start(s32[16]{0:T(128)} %param.15) | copy-start | bytes 196
  2.1 19.0 %collective-permute-start = (bf16[256,1024]{1,0:T(8,128)(2,1)S(1)}, bf16[256,1024]{1,0:T(8,128)(2,1)S(1)}, u32[]{:S(2)}, u32[]{:S(2)}) collective-permute-start(bf16[256,1024]{1,0:T(8,128)(2,1)S(1)} %get-tuple-element.22), channel_id=1, source_target_pairs={{0,1},{2,3},{4,5},{6,7},{8,9},{10,11},{12,13},{14,15},{1,0},{3,2},... | collective-permute-start | bytes 1572872 | tf_op jit(solution)/shard_map/ppermute | solution.py:348
  2.6 18.5 %collective-permute-start.1 = (bf16[256,1024]{1,0:T(8,128)(2,1)S(1)}, bf16[256,1024]{1,0:T(8,128)(2,1)S(1)}, u32[]{:S(2)}, u32[]{:S(2)}) collective-permute-start(bf16[256,1024]{1,0:T(8,128)(2,1)S(1)} %get-tuple-element.23), channel_id=1, source_target_pairs={{1,2},{3,4},{5,6},{7,8},{9,10},{11,12},{13,14},{2,1},{4,3},{6,5},{... | collective-permute-start | bytes 1572872 | tf_op jit(solution)/shard_map/ppermute | solution.py:349
  28.3 8.1 %collective-permute-start.3 = (bf16[100,768]{1,0:T(8,128)(2,1)S(1)}, bf16[100,768]{1,0:T(8,128)(2,1)S(1)}, u32[]{:S(2)}, u32[]{:S(2)}) collective-permute-start(bf16[100,768]{1,0:T(8,128)(2,1)S(1)} %get-tuple-element.26.refs_0_), channel_id=1, source_target_pairs={{0,16},{16,0},{1,17},{17,1},{2,18},{18,2},{3,19},{19,3},{4,20},{20... | collective-permute-start | bytes 460808 | tf_op jit(solution)/shard_map/ppermute | solution.py:379
  31.4 5.0 %copy-start.3 = (f32[100,1024]{1,0:T(8,128)S(1)}, f32[100,1024]{1,0:T(8,128)}, u32[]{:S(2)}) copy-start(f32[100,1024]{1,0:T(8,128)} %refs_2_.3) | copy-start | bytes 1228804
  36.3 4.5 %collective-permute-start.2 = (bf16[100,256]{1,0:T(8,128)(2,1)S(1)}, bf16[100,256]{1,0:T(8,128)(2,1)S(1)}, u32[]{:S(2)}, u32[]{:S(2)}) collective-permute-start(bf16[100,256]{1,0:T(8,128)(2,1)S(1)} %edge_block.3.refs_0_), channel_id=1, source_target_pairs={{0,16},{16,0},{1,17},{17,1},{2,18},{18,2},{3,19},{19,3},{4,20},{20... | collective-permute-start | bytes 153608 | tf_op jit(solution)/shard_map/ppermute | solution.py:379

commit v7 on v6

--- a/solution.py
+++ b/solution.py
@@ -74,7 +74,7 @@
             top = jnp.max(t, axis=1, keepdims=True)
             p = jnp.exp2((t - top) * LOG2E).astype(BF16)
             groups.append(jnp.concatenate([p, outside] if g % 2 == 0 else [outside, p], axis=1))
-        return jnp.concatenate(groups, axis=0)
+        return groups
 
     steps = [(block, c) for block in blocks for c in range(pairs)]
     later = scores(*steps[0])
@@ -84,10 +84,13 @@
             later = scores(*steps[n + 1])
         _, _, values, _, store, finish = block
         v = jnp.concatenate([values(c), ones], axis=1)
-        o = jnp.dot(weights(s), v, preferred_element_type=F32)
-        num = jnp.where(first, o[:half, :LANES], o[half:, :LANES])
-        den = jnp.where(first, o[:half, LANES:], o[half:, LANES:])
-        store(c, (num / den).astype(BF16))
+        w = weights(s)
+        heads = [
+            jnp.dot(jnp.concatenate(w[2 * h : 2 * h + 2], axis=0), v, preferred_element_type=F32) for h in range(2)
+        ]
+        o = jnp.concatenate(heads, axis=0)
+        o = o[:, :LANES] / o[:, LANES:]
+        store(c, jnp.where(first, o[:half], o[half:]).astype(BF16))
         if c == pairs - 1:
             finish()
 

time: 42.1 us -> 41.7 us (level)
  no operation moved by 1% of the time
where the time goes in v7:
time: 41.7 us; the launch traced here: 41.6 us
  Pallas kernels  31.5 us (76%)
  starting transfers between devices  4.52 us (11%)
  waiting for transfers between devices  3.08 us (7%)
  local copies, waits for them, and re-layouts  1.55 us (4%)
  between operations  0.94 us (2%)
    pallas_call x1, Pallas kernels, on_device(): pl.pallas_call(inner_kernel, in_specs=[VMEM] * 7, out_specs=[VMEM] * 5, o...  15.8 us
    pallas_call x2, Pallas kernels, edge(): pl.pallas_call(functools.partial(edge_kernel, side), in_specs=[VMEM] * (7...  12.1 us
    ppermute x2, starting transfers between devices, exchange(): lax.ppermute(part, 'ens', [(i, (i + s) % members) for i in range(members)])  3.15 us
    ppermute x2, waiting for transfers between devices, exchange(): lax.ppermute(part, 'ens', [(i, (i + s) % members) for i in range(members)])  3.07 us
    pallas_call x2, Pallas kernels, score_call(): pl.pallas_call(functools.partial(score_kernel, count, len(carried), place...  2.23 us
    unnamed x16, local copies, waits for them, and re-layouts  1.55 us
    pallas_call x1, Pallas kernels, on_device(): pl.pallas_call(facing_kernel, in_specs=[ANY], out_specs=[VMEM] * 2, out_s...  1.38 us
  transfers between devices with their start and end apart: 4, of which 1 were waited for; matrix products, arithmetic and copies ran while one was open for 0% of the time, Pallas kernels for 53%

profile of v7, /device:TPU:0, one launch (start us, length us, event | category | flops | bytes accessed | tf_op | source)
XLA Modules:
  0.0 41.6 jit_solution(5614664477657537224)
XLA Ops:
  0.6 0.0 copy-start
  0.6 0.0 copy-start.1
  0.7 0.0 copy-start.2
  0.7 0.0 copy-start.4
  0.7 0.0 copy-start.5
  0.7 0.0 copy-start.6
  0.7 0.0 copy-start.7
  0.7 1.4 %facing.1 = (bf16[256,1024]{1,0:T(8,128)(2,1)S(1)}, bf16[256,1024]{1,0:T(8,128)(2,1)S(1)}) custom-call(bf16[1024,1024]{1,0:T(8,128)(2,1)} %bitcast.6), custom_call_target="tpu_custom_call" | custom-call | flops 8000000000 | bytes 1048576 | tf_op jit(solution)/shard_map/facing/pallas_call | solution.py:341
  2.1 0.6 %collective-permute-start = (bf16[256,1024]{1,0:T(8,128)(2,1)S(1)}, bf16[256,1024]{1,0:T(8,128)(2,1)S(1)}, u32[]{:S(2)}, u32[]{:S(2)}) collective-permute-start(bf16[256,1024]{1,0:T(8,128)(2,1)S(1)} %get-tuple-element.22), channel_id=1, source_target_pairs={{0,1},{2,3},{4,5},{6,7},{8,9},{10,11},{12,13},{14,15},{1,0},{3,2},... | collective-permute-start | bytes 1572872 | tf_op jit(solution)/shard_map/ppermute | solution.py:351
  2.6 0.8 %collective-permute-start.1 = (bf16[256,1024]{1,0:T(8,128)(2,1)S(1)}, bf16[256,1024]{1,0:T(8,128)(2,1)S(1)}, u32[]{:S(2)}, u32[]{:S(2)}) collective-permute-start(bf16[256,1024]{1,0:T(8,128)(2,1)S(1)} %get-tuple-element.23), channel_id=1, source_target_pairs={{1,2},{3,4},{5,6},{7,8},{9,10},{11,12},{13,14},{2,1},{4,3},{6,5},{... | collective-permute-start | bytes 1572872 | tf_op jit(solution)/shard_map/ppermute | solution.py:352
  3.5 0.0 copy-done
  3.5 0.0 copy-done.1
  3.5 1.5 %copy-done.2 = bf16[1024,3072]{1,0:T(8,128)(2,1)S(1)} copy-done((bf16[1024,3072]{1,0:T(8,128)(2,1)S(1)}, bf16[1024,3072]{1,0:T(8,128)(2,1)}, u32[]{:S(2)}) %copy-start.2) | copy-done | bytes 6291480
  5.0 0.0 copy-done.4
  5.0 0.0 copy-done.5
  5.0 0.0 copy-done.6
  5.0 0.0 copy-done.7
  5.0 15.8 %inner_blocks.1 = (bf16[100,512]{1,0:T(8,128)(2,1)S(1)}, bf16[512,1024]{1,0:T(8,128)(2,1)S(1)}, bf16[1024,2048]{1,0:T(8,128)(2,1)S(1)}, bf16[1536,128]{1,0:T(8,128)(2,1)S(1)}, f32[1,1024]{1,0:T(1,128)S(1)}) custom-call(s32[1,16]{1,0:T(1,128)S(1)} %bitcast.15, bf16[1024,1024]{1,0:T(8,128)(2,1)S(1)} %bitcast.7, bf16[1,1024]{1,0:T(2,128)(2,1)S(1)} %copy-done.5, ...), custom_call_target="tpu_custom_call" | custom-call | flops 9126805504 | bytes 10485760 | tf_op jit(solution)/shard_map/inner_blocks/pallas_call | solution.py:355
  20.8 0.0 collective-permute-done.refs_2_
  20.9 0.0 collective-permute-done.1.refs_3_
  20.9 7.2 %edge_block.2 = (bf16[100,768]{1,0:T(8,128)(2,1)S(1)}, bf16[256,2048]{1,0:T(8,128)(2,1)S(1)}) custom-call(f32[1,1024]{1,0:T(1,128)S(1)} %get-tuple-element.18.alive, bf16[1536,128]{1,0:T(8,128)(2,1)S(1)} %get-tuple-element.19.flags, bf16[100,1024]{1,0:T(8,128)(2,1)S(1)} %bitcast.11, bf16[1024,1024]{1,0:T(8,128)(2,1)S(1)} %bitcast.8, ...), custom_call_target="tpu_custom_call" | custom-call | flops 3489660928 | bytes 10485760 | tf_op jit(solution)/shard_map/edge_block/pallas_call | solution.py:387
  28.0 3.1 %collective-permute-start.3 = (bf16[100,768]{1,0:T(8,128)(2,1)S(1)}, bf16[100,768]{1,0:T(8,128)(2,1)S(1)}, u32[]{:S(2)}, u32[]{:S(2)}) collective-permute-start(bf16[100,768]{1,0:T(8,128)(2,1)S(1)} %get-tuple-element.26.refs_0_), channel_id=1, source_target_pairs={{0,16},{16,0},{1,17},{17,1},{2,18},{18,2},{3,19},{19,3},{4,20},{20... | collective-permute-start | bytes 460808 | tf_op jit(solution)/shard_map/ppermute | solution.py:382
  31.1 0.0 copy-start.3
  31.1 4.9 %edge_block.3.refs_0_ = bf16[100,256]{1,0:T(8,128)(2,1)S(1)} custom-call(f32[1,1024]{1,0:T(1,128)S(1)} %get-tuple-element.18.alive, bf16[1536,128]{1,0:T(8,128)(2,1)S(1)} %get-tuple-element.19.flags, bf16[100,1024]{1,0:T(8,128)(2,1)S(1)} %bitcast.12, bf16[1024,1024]{1,0:T(8,128)(2,1)S(1)} %bitcast.9, bf16[1024,1024]{1,0:T(8,128)(2,1)S(1)} %copy-done.1, ...), custom_call_target="tpu_custom_call" | custom-call | flops 1342177280 | bytes 10485760 | tf_op jit(solution)/shard_map/edge_block/pallas_call | solution.py:387
  36.0 0.1 collective-permute-start.2
  36.1 0.0 collective-permute-done.3.refs_1_
  36.1 0.0 copy-done.3
  36.1 1.4 %score.2 = (bf16[100,1024]{1,0:T(8,128)(2,1)}, f32[100,1024]{1,0:T(8,128)}, f32[100,1,1024]{2,1,0:T(1,128)}) custom-call(f32[1,1024]{1,0:T(1,128)S(1)} %get-tuple-element.18.alive, bf16[100,768]{1,0:T(8,128)(2,1)S(1)} %get-tuple-element.26.refs_0_, bf16[100,768]{1,0:T(8,128)(2,1)S(1)} %collective-permute-done.3.refs_1_, f32[100,1024]{1,0:T(8,128)S(1)} %copy-done.3), custom_call_target="tpu_custom_call" | custom-call | flops 3072000 | bytes 1536000 | tf_op jit(solution)/shard_map/score/pallas_call | solution.py:307
  37.5 3.1 %collective-permute-done.2.refs_1_ = bf16[100,256]{1,0:T(8,128)(2,1)S(1)} collective-permute-done((bf16[100,256]{1,0:T(8,128)(2,1)S(1)}, bf16[100,256]{1,0:T(8,128)(2,1)S(1)}, u32[]{:S(2)}, u32[]{:S(2)}) %collective-permute-start.2) | collective-permute-done | bytes 51232 | tf_op jit(solution)/shard_map/ppermute | solution.py:382
  40.5 0.9 %score.3 = (bf16[100,1024]{1,0:T(8,128)(2,1)}, f32[100,1024]{1,0:T(8,128)}, f32[100,1,1024]{2,1,0:T(1,128)}) custom-call(f32[1,1024]{1,0:T(1,128)S(1)} %get-tuple-element.18.alive, bf16[100,256]{1,0:T(8,128)(2,1)S(1)} %edge_block.3.refs_0_, ...), custom_call_target="tpu_custom_call", output_to_operand_aliasing={{0}: (4, {}), {1}: (5, {}), {2}: (6, {})} | custom-call | flops 1024000 | bytes 512000 | tf_op jit(solution)/shard_map/score/pallas_call | solution.py:307
Async XLA Ops:
  0.6 2.8 %copy-start = (bf16[1,1024,1024]{2,1,0:T(8,128)(2,1)S(1)}, bf16[1,1024,1024]{2,1,0:T(8,128)(2,1)}, u32[]{:S(2)}) copy-start(bf16[1,1024,1024]{2,1,0:T(8,128)(2,1)} %param.8) | copy-start | bytes 6291460
  0.6 2.8 %copy-start.1 = (bf16[1024,1024]{1,0:T(8,128)(2,1)S(1)}, bf16[1024,1024]{1,0:T(8,128)(2,1)}, u32[]{:S(2)}) copy-start(bf16[1024,1024]{1,0:T(8,128)(2,1)} %w_proj.5) | copy-start | bytes 6291460
  0.7 4.4 %copy-start.2 = (bf16[1024,3072]{1,0:T(8,128)(2,1)S(1)}, bf16[1024,3072]{1,0:T(8,128)(2,1)}, u32[]{:S(2)}) copy-start(bf16[1024,3072]{1,0:T(8,128)(2,1)} %refs_4_.1) | copy-start | bytes 18874372
  0.7 4.3 %copy-start.4 = (bf16[1024,100]{0,1:T(8,128)(2,1)S(1)}, bf16[1024,100]{0,1:T(8,128)(2,1)}, u32[]{:S(2)}) copy-start(bf16[1024,100]{0,1:T(8,128)(2,1)} %param.13) | copy-start | bytes 614404
  0.7 4.3 %copy-start.5 = (bf16[1,1024]{1,0:T(2,128)(2,1)S(1)}, bf16[1,1024]{1,0:T(2,128)(2,1)}, u32[]{:S(2)}) copy-start(bf16[1,1024]{1,0:T(2,128)(2,1)} %refs_0_.1) | copy-start | bytes 6148
  0.7 4.3 %copy-start.6 = (f32[1024]{0:T(1024)S(1)}, f32[1024]{0:T(1024)}, u32[]{:S(2)}) copy-start(f32[1024]{0:T(1024)} %param.10) | copy-start | bytes 12292
  0.7 4.3 %copy-start.7 = (s32[16]{0:T(128)S(1)}, s32[16]{0:T(128)}, u32[]{:S(2)}) copy-start(s32[16]{0:T(128)} %param.15) | copy-start | bytes 196
  2.1 18.8 %collective-permute-start = (bf16[256,1024]{1,0:T(8,128)(2,1)S(1)}, bf16[256,1024]{1,0:T(8,128)(2,1)S(1)}, u32[]{:S(2)}, u32[]{:S(2)}) collective-permute-start(bf16[256,1024]{1,0:T(8,128)(2,1)S(1)} %get-tuple-element.22), channel_id=1, source_target_pairs={{0,1},{2,3},{4,5},{6,7},{8,9},{10,11},{12,13},{14,15},{1,0},{3,2},... | collective-permute-start | bytes 1572872 | tf_op jit(solution)/shard_map/ppermute | solution.py:351
  2.6 18.2 %collective-permute-start.1 = (bf16[256,1024]{1,0:T(8,128)(2,1)S(1)}, bf16[256,1024]{1,0:T(8,128)(2,1)S(1)}, u32[]{:S(2)}, u32[]{:S(2)}) collective-permute-start(bf16[256,1024]{1,0:T(8,128)(2,1)S(1)} %get-tuple-element.23), channel_id=1, source_target_pairs={{1,2},{3,4},{5,6},{7,8},{9,10},{11,12},{13,14},{2,1},{4,3},{6,5},{... | collective-permute-start | bytes 1572872 | tf_op jit(solution)/shard_map/ppermute | solution.py:352
  28.0 8.1 %collective-permute-start.3 = (bf16[100,768]{1,0:T(8,128)(2,1)S(1)}, bf16[100,768]{1,0:T(8,128)(2,1)S(1)}, u32[]{:S(2)}, u32[]{:S(2)}) collective-permute-start(bf16[100,768]{1,0:T(8,128)(2,1)S(1)} %get-tuple-element.26.refs_0_), channel_id=1, source_target_pairs={{0,16},{16,0},{1,17},{17,1},{2,18},{18,2},{3,19},{19,3},{4,20},{20... | collective-permute-start | bytes 460808 | tf_op jit(solution)/shard_map/ppermute | solution.py:382
  31.1 5.0 %copy-start.3 = (f32[100,1024]{1,0:T(8,128)S(1)}, f32[100,1024]{1,0:T(8,128)}, u32[]{:S(2)}) copy-start(f32[100,1024]{1,0:T(8,128)} %refs_2_.3) | copy-start | bytes 1228804
  36.0 4.5 %collective-permute-start.2 = (bf16[100,256]{1,0:T(8,128)(2,1)S(1)}, bf16[100,256]{1,0:T(8,128)(2,1)S(1)}, u32[]{:S(2)}, u32[]{:S(2)}) collective-permute-start(bf16[100,256]{1,0:T(8,128)(2,1)S(1)} %edge_block.3.refs_0_), channel_id=1, source_target_pairs={{0,16},{16,0},{1,17},{17,1},{2,18},{18,2},{3,19},{19,3},{4,20},{20... | collective-permute-start | bytes 153608 | tf_op jit(solution)/shard_map/ppermute | solution.py:382

commit v8 on v7

--- a/solution.py
+++ b/solution.py
@@ -272,33 +272,35 @@
 
 def score_kernel(others, carried, places, alive, *refs):
     mine, rest, truth = refs[0], refs[1 : 1 + others], refs[1 + others]
-    pred, score, deriv = refs[2 + others + carried : 5 + others + carried]
-    score_buf, deriv_buf, sem = refs[5 + others + carried :]
+    refs = refs[2 + others :]
     half = HALF_WINDOW
     moves = []
+    if carried:
+        score, deriv, score_buf, deriv_buf, sem = refs[carried:]
+    else:
+        last, pred, score, deriv, score_buf, deriv_buf, sem = refs
+        split = mine.shape[1]
+        moves.append(pltpu.make_async_copy(mine, pred.at[:, :split], sem.at[2, 0]))
+        moves.append(pltpu.make_async_copy(last, pred.at[:, split:], sem.at[2, 1]))
+        for c in moves:
+            c.start()
     for i, place in enumerate(places):
         here, there = slice(i * half, (i + 1) * half), slice(place * half, (place + 1) * half)
-        moves.append(pltpu.make_async_copy(mine.at[:, here], pred.at[:, there], sem.at[0, i]))
-        moves[-1].start()
-    for i, place in enumerate(places):
-        here, there = slice(i * half, (i + 1) * half), slice(place * half, (place + 1) * half)
-        f = mine[:, here]
         live = alive[:, there] > 0.0
-        score_buf[i], d = score_values(f, [r[:, here] for r in rest], truth[:, there], live)
-        moves.append(pltpu.make_async_copy(score_buf.at[i], score.at[:, there], sem.at[1, i]))
+        score_buf[i], d = score_values(mine[:, here], [r[:, here] for r in rest], truth[:, there], live)
+        moves.append(pltpu.make_async_copy(score_buf.at[i], score.at[:, there], sem.at[0, i]))
         moves[-1].start()
         deriv_buf[i] = d[:, None, :]
-        moves.append(pltpu.make_async_copy(deriv_buf.at[i], deriv.at[:, :, there], sem.at[2, i]))
+        moves.append(pltpu.make_async_copy(deriv_buf.at[i], deriv.at[:, :, there], sem.at[1, i]))
         moves[-1].start()
     for c in moves:
         c.wait()
 
 
-def score_call(alive, mine, others, truth, carried, places):
+def score_call(alive, mine, others, truth, carried, places, *last):
     half = HALF_WINDOW
     fields, nodes = truth.shape
-    shapes = [
-        jax.ShapeDtypeStruct((fields, nodes), BF16),
+    shapes = [jax.ShapeDtypeStruct((fields, nodes), BF16)] * len(last) + [
         jax.ShapeDtypeStruct((fields, nodes), F32),
         jax.ShapeDtypeStruct((fields, 1, nodes), F32),
     ]
@@ -306,13 +308,13 @@
     parts = len(places)
     return pl.pallas_call(
         functools.partial(score_kernel, count, len(carried), places),
-        in_specs=[VMEM] * (3 + count) + [ANY] * len(carried),
-        out_specs=[ANY] * 3,
+        in_specs=[VMEM] * (3 + count + len(last)) + [ANY] * len(carried),
+        out_specs=[ANY] * len(shapes),
         out_shape=shapes,
         scratch_shapes=[
             pltpu.VMEM((parts, fields, half), F32),
             pltpu.VMEM((parts, fields, 1, half), F32),
-            pltpu.SemaphoreType.DMA((3, parts)),
+            pltpu.SemaphoreType.DMA((3, max(parts, 2))),
         ],
         compiler_params=pltpu.CompilerParams(vmem_limit_bytes=8 << 20),
         input_output_aliases={3 + count + i: i for i in range(len(carried))},
@@ -320,7 +322,7 @@
             flops=40 * fields * half * parts, bytes_accessed=20 * fields * half * parts, transcendentals=0
         ),
         name="score",
-    )(alive, mine, *others, truth, *carried)
+    )(alive, mine, *others, truth, *last, *carried)
 
 
 def neighbours(count, start):
@@ -409,8 +411,9 @@
     others_most = exchange(pred_most)
     (pred_last,) = edge(1, [(fields, half)], [(half, width)], 2 * half * width * width, halo_high)
     others_last = exchange(pred_last)
-    partial = score_call(alive, pred_most, others_most, truth, [], list(range(blocks - 1)))
-    pred, score, deriv = score_call(alive, pred_last, others_last, truth, partial, [blocks - 1])
+    places = list(range(blocks - 1))
+    pred, *partial = score_call(alive, pred_most, others_most, truth, [], places, pred_last)
+    score, deriv = score_call(alive, pred_last, others_last, truth, partial, [blocks - 1])
     return pred[None], score, deriv.transpose(1, 0, 2)
 
 

time: 41.7 us -> 41.8 us (level)
  no operation moved by 1% of the time
where the time goes in v8:
time: 41.8 us; the launch traced here: 41.6 us
  Pallas kernels  31.5 us (75%)
  starting transfers between devices  4.52 us (11%)
  waiting for transfers between devices  3.07 us (7%)
  local copies, waits for them, and re-layouts  1.55 us (4%)
  between operations  0.94 us (2%)
    pallas_call x1, Pallas kernels, on_device(): pl.pallas_call(inner_kernel, in_specs=[VMEM] * 7, out_specs=[VMEM] * 5, o...  15.8 us
    pallas_call x2, Pallas kernels, edge(): pl.pallas_call(functools.partial(edge_kernel, side), in_specs=[VMEM] * (7...  12.1 us
    ppermute x2, starting transfers between devices, exchange(): lax.ppermute(part, 'ens', [(i, (i + s) % members) for i in range(members)])  3.15 us
    ppermute x2, waiting for transfers between devices, exchange(): lax.ppermute(part, 'ens', [(i, (i + s) % members) for i in range(members)])  3.07 us
    pallas_call x2, Pallas kernels, score_call(): pl.pallas_call(functools.partial(score_kernel, count, len(carried), place...  2.26 us
    unnamed x16, local copies, waits for them, and re-layouts  1.55 us
    pallas_call x1, Pallas kernels, on_device(): pl.pallas_call(facing_kernel, in_specs=[ANY], out_specs=[VMEM] * 2, out_s...  1.38 us
  transfers between devices with their start and end apart: 4, of which 1 were waited for; matrix products, arithmetic and copies ran while one was open for 0% of the time, Pallas kernels for 53%

profile of v8, /device:TPU:0, one launch (start us, length us, event | category | flops | bytes accessed | tf_op | source)
XLA Modules:
  0.0 41.6 jit_solution(7615158162371965733)
XLA Ops:
  0.6 0.0 copy-start
  0.6 0.0 copy-start.1
  0.7 0.0 copy-start.2
  0.7 0.0 copy-start.4
  0.7 0.0 copy-start.5
  0.7 0.0 copy-start.6
  0.7 0.0 copy-start.7
  0.7 1.4 %facing.1 = (bf16[256,1024]{1,0:T(8,128)(2,1)S(1)}, bf16[256,1024]{1,0:T(8,128)(2,1)S(1)}) custom-call(bf16[1024,1024]{1,0:T(8,128)(2,1)} %bitcast.6), custom_call_target="tpu_custom_call" | custom-call | flops 8000000000 | bytes 1048576 | tf_op jit(solution)/shard_map/facing/pallas_call | solution.py:343
  2.1 0.6 %collective-permute-start = (bf16[256,1024]{1,0:T(8,128)(2,1)S(1)}, bf16[256,1024]{1,0:T(8,128)(2,1)S(1)}, u32[]{:S(2)}, u32[]{:S(2)}) collective-permute-start(bf16[256,1024]{1,0:T(8,128)(2,1)S(1)} %get-tuple-element.21), channel_id=1, source_target_pairs={{0,1},{2,3},{4,5},{6,7},{8,9},{10,11},{12,13},{14,15},{1,0},{3,2},... | collective-permute-start | bytes 1572872 | tf_op jit(solution)/shard_map/ppermute | solution.py:353
  2.6 0.8 %collective-permute-start.1 = (bf16[256,1024]{1,0:T(8,128)(2,1)S(1)}, bf16[256,1024]{1,0:T(8,128)(2,1)S(1)}, u32[]{:S(2)}, u32[]{:S(2)}) collective-permute-start(bf16[256,1024]{1,0:T(8,128)(2,1)S(1)} %get-tuple-element.22), channel_id=1, source_target_pairs={{1,2},{3,4},{5,6},{7,8},{9,10},{11,12},{13,14},{2,1},{4,3},{6,5},{... | collective-permute-start | bytes 1572872 | tf_op jit(solution)/shard_map/ppermute | solution.py:354
  3.5 0.0 copy-done
  3.5 0.0 copy-done.1
  3.5 1.5 %copy-done.2 = bf16[1024,3072]{1,0:T(8,128)(2,1)S(1)} copy-done((bf16[1024,3072]{1,0:T(8,128)(2,1)S(1)}, bf16[1024,3072]{1,0:T(8,128)(2,1)}, u32[]{:S(2)}) %copy-start.2) | copy-done | bytes 6291480
  5.0 0.0 copy-done.4
  5.0 0.0 copy-done.5
  5.0 0.0 copy-done.6
  5.0 0.0 copy-done.7
  5.0 15.8 %inner_blocks.1 = (bf16[100,512]{1,0:T(8,128)(2,1)S(1)}, bf16[512,1024]{1,0:T(8,128)(2,1)S(1)}, bf16[1024,2048]{1,0:T(8,128)(2,1)S(1)}, bf16[1536,128]{1,0:T(8,128)(2,1)S(1)}, f32[1,1024]{1,0:T(1,128)S(1)}) custom-call(s32[1,16]{1,0:T(1,128)S(1)} %bitcast.15, bf16[1024,1024]{1,0:T(8,128)(2,1)S(1)} %bitcast.7, bf16[1,1024]{1,0:T(2,128)(2,1)S(1)} %copy-done.5, ...), custom_call_target="tpu_custom_call" | custom-call | flops 9126805504 | bytes 10485760 | tf_op jit(solution)/shard_map/inner_blocks/pallas_call | solution.py:357
  20.8 0.0 collective-permute-done.refs_2_
  20.9 0.0 collective-permute-done.1.refs_3_
  20.9 7.2 %edge_block.2 = (bf16[100,768]{1,0:T(8,128)(2,1)S(1)}, bf16[256,2048]{1,0:T(8,128)(2,1)S(1)}) custom-call(f32[1,1024]{1,0:T(1,128)S(1)} %get-tuple-element.17.alive, bf16[1536,128]{1,0:T(8,128)(2,1)S(1)} %get-tuple-element.18.flags, bf16[100,1024]{1,0:T(8,128)(2,1)S(1)} %bitcast.11, bf16[1024,1024]{1,0:T(8,128)(2,1)S(1)} %bitcast.8, ...), custom_call_target="tpu_custom_call" | custom-call | flops 3489660928 | bytes 10485760 | tf_op jit(solution)/shard_map/edge_block/pallas_call | solution.py:389
  28.0 3.1 %collective-permute-start.2 = (bf16[100,768]{1,0:T(8,128)(2,1)S(1)}, bf16[100,768]{1,0:T(8,128)(2,1)S(1)}, u32[]{:S(2)}, u32[]{:S(2)}) collective-permute-start(bf16[100,768]{1,0:T(8,128)(2,1)S(1)} %get-tuple-element.24.refs_0_), channel_id=1, source_target_pairs={{0,16},{16,0},{1,17},{17,1},{2,18},{18,2},{3,19},{19,3},{4,20},{20... | collective-permute-start | bytes 460808 | tf_op jit(solution)/shard_map/ppermute | solution.py:384
  31.1 0.0 copy-start.3
  31.1 4.9 %edge_block.3.refs_3_.refs_0_ = bf16[100,256]{1,0:T(8,128)(2,1)S(1)} custom-call(f32[1,1024]{1,0:T(1,128)S(1)} %get-tuple-element.17.alive, bf16[1536,128]{1,0:T(8,128)(2,1)S(1)} %get-tuple-element.18.flags, bf16[100,1024]{1,0:T(8,128)(2,1)S(1)} %bitcast.12, bf16[1024,1024]{1,0:T(8,128)(2,1)S(1)} %bitcast.9, bf16[1024,1024]{1,0:T(8,128)(2,1)S(1)} %copy-done.1, ...), custom_call_target="tpu_custom_call" | custom-call | flops 1342177280 | bytes 10485760 | tf_op jit(solution)/shard_map/edge_block/pallas_call | solution.py:389
  36.0 0.1 collective-permute-start.3
  36.1 0.0 collective-permute-done.2.refs_1_
  36.1 0.0 copy-done.3
  36.1 1.4 %score.2 = (bf16[100,1024]{1,0:T(8,128)(2,1)}, f32[100,1024]{1,0:T(8,128)}, f32[100,1,1024]{2,1,0:T(1,128)}) custom-call(f32[1,1024]{1,0:T(1,128)S(1)} %get-tuple-element.17.alive, bf16[100,768]{1,0:T(8,128)(2,1)S(1)} %get-tuple-element.24.refs_0_, bf16[100,768]{1,0:T(8,128)(2,1)S(1)} %collective-permute-done.2.refs_1_, f32[100,1024]{1,0:T(8,128)S(1)} %copy-done.3, ...), custom_call_target="tpu_custom_call" | custom-call | flops 3072000 | bytes 1536000 | tf_op jit(solution)/shard_map/score/pallas_call | solution.py:309
  37.5 3.1 %collective-permute-done.3.refs_1_ = bf16[100,256]{1,0:T(8,128)(2,1)S(1)} collective-permute-done((bf16[100,256]{1,0:T(8,128)(2,1)S(1)}, bf16[100,256]{1,0:T(8,128)(2,1)S(1)}, u32[]{:S(2)}, u32[]{:S(2)}) %collective-permute-start.3) | collective-permute-done | bytes 51232 | tf_op jit(solution)/shard_map/ppermute | solution.py:384
  40.5 0.9 %score.3 = (f32[100,1024]{1,0:T(8,128)}, f32[100,1,1024]{2,1,0:T(1,128)}) custom-call(f32[1,1024]{1,0:T(1,128)S(1)} %get-tuple-element.17.alive, bf16[100,256]{1,0:T(8,128)(2,1)S(1)} %edge_block.3.refs_3_.refs_0_, bf16[100,256]{1,0:T(8,128)(2,1)S(1)} %collective-permute-done.3.refs_1_, ...), custom_call_target="tpu_custom_call", output_to_operand_aliasing={{0}: (4, {}), {1}: (5, {})} | custom-call | flops 1024000 | bytes 512000 | tf_op jit(solution)/shard_map/score/pallas_call | solution.py:309
Async XLA Ops:
  0.6 2.8 %copy-start = (bf16[1,1024,1024]{2,1,0:T(8,128)(2,1)S(1)}, bf16[1,1024,1024]{2,1,0:T(8,128)(2,1)}, u32[]{:S(2)}) copy-start(bf16[1,1024,1024]{2,1,0:T(8,128)(2,1)} %param.8) | copy-start | bytes 6291460
  0.6 2.8 %copy-start.1 = (bf16[1024,1024]{1,0:T(8,128)(2,1)S(1)}, bf16[1024,1024]{1,0:T(8,128)(2,1)}, u32[]{:S(2)}) copy-start(bf16[1024,1024]{1,0:T(8,128)(2,1)} %w_proj.5) | copy-start | bytes 6291460
  0.7 4.4 %copy-start.2 = (bf16[1024,3072]{1,0:T(8,128)(2,1)S(1)}, bf16[1024,3072]{1,0:T(8,128)(2,1)}, u32[]{:S(2)}) copy-start(bf16[1024,3072]{1,0:T(8,128)(2,1)} %refs_4_.1) | copy-start | bytes 18874372
  0.7 4.3 %copy-start.4 = (bf16[1024,100]{0,1:T(8,128)(2,1)S(1)}, bf16[1024,100]{0,1:T(8,128)(2,1)}, u32[]{:S(2)}) copy-start(bf16[1024,100]{0,1:T(8,128)(2,1)} %param.13) | copy-start | bytes 614404
  0.7 4.3 %copy-start.5 = (bf16[1,1024]{1,0:T(2,128)(2,1)S(1)}, bf16[1,1024]{1,0:T(2,128)(2,1)}, u32[]{:S(2)}) copy-start(bf16[1,1024]{1,0:T(2,128)(2,1)} %refs_0_.1) | copy-start | bytes 6148
  0.7 4.3 %copy-start.6 = (f32[1024]{0:T(1024)S(1)}, f32[1024]{0:T(1024)}, u32[]{:S(2)}) copy-start(f32[1024]{0:T(1024)} %param.10) | copy-start | bytes 12292
  0.7 4.3 %copy-start.7 = (s32[16]{0:T(128)S(1)}, s32[16]{0:T(128)}, u32[]{:S(2)}) copy-start(s32[16]{0:T(128)} %param.15) | copy-start | bytes 196
  2.1 18.8 %collective-permute-start = (bf16[256,1024]{1,0:T(8,128)(2,1)S(1)}, bf16[256,1024]{1,0:T(8,128)(2,1)S(1)}, u32[]{:S(2)}, u32[]{:S(2)}) collective-permute-start(bf16[256,1024]{1,0:T(8,128)(2,1)S(1)} %get-tuple-element.21), channel_id=1, source_target_pairs={{0,1},{2,3},{4,5},{6,7},{8,9},{10,11},{12,13},{14,15},{1,0},{3,2},... | collective-permute-start | bytes 1572872 | tf_op jit(solution)/shard_map/ppermute | solution.py:353
  2.6 18.2 %collective-permute-start.1 = (bf16[256,1024]{1,0:T(8,128)(2,1)S(1)}, bf16[256,1024]{1,0:T(8,128)(2,1)S(1)}, u32[]{:S(2)}, u32[]{:S(2)}) collective-permute-start(bf16[256,1024]{1,0:T(8,128)(2,1)S(1)} %get-tuple-element.22), channel_id=1, source_target_pairs={{1,2},{3,4},{5,6},{7,8},{9,10},{11,12},{13,14},{2,1},{4,3},{6,5},{... | collective-permute-start | bytes 1572872 | tf_op jit(solution)/shard_map/ppermute | solution.py:354
  28.0 8.1 %collective-permute-start.2 = (bf16[100,768]{1,0:T(8,128)(2,1)S(1)}, bf16[100,768]{1,0:T(8,128)(2,1)S(1)}, u32[]{:S(2)}, u32[]{:S(2)}) collective-permute-start(bf16[100,768]{1,0:T(8,128)(2,1)S(1)} %get-tuple-element.24.refs_0_), channel_id=1, source_target_pairs={{0,16},{16,0},{1,17},{17,1},{2,18},{18,2},{3,19},{19,3},{4,20},{20... | collective-permute-start | bytes 460808 | tf_op jit(solution)/shard_map/ppermute | solution.py:384
  31.1 5.0 %copy-start.3 = (f32[100,1024]{1,0:T(8,128)S(1)}, f32[100,1024]{1,0:T(8,128)}, u32[]{:S(2)}) copy-start(f32[100,1024]{1,0:T(8,128)} %refs_2_.3) | copy-start | bytes 1228804
  36.0 4.5 %collective-permute-start.3 = (bf16[100,256]{1,0:T(8,128)(2,1)S(1)}, bf16[100,256]{1,0:T(8,128)(2,1)S(1)}, u32[]{:S(2)}, u32[]{:S(2)}) collective-permute-start(bf16[100,256]{1,0:T(8,128)(2,1)S(1)} %edge_block.3.refs_3_.refs_0_), channel_id=1, source_target_pairs={{0,16},{16,0},{1,17},{17,1},{2,18},{18,2},{3,19},{19,3},{4,20},{20... | collective-permute-start | bytes 153608 | tf_op jit(solution)/shard_map/ppermute | solution.py:384
